TPU v7x, 256 devices: a whole 4x4x8 slice. The times are simulated.
256 devices in a mesh: shot: 32 (over z, y_hi, core), tm: 8 (over x, y_lo).
Axes of the slice: x: 4, y: 4 (y_hi: 2, y_lo: 2; y = y_hi * 2 + y_lo), z: 8, core: 2. Of those that a mesh axis runs over, the one named last changes fastest.
Arguments:
- blended: float32 [128, 32, 8192], P(None, 'shot', 'tm'), may hold values from -12 to 12
- delays: int32 [32, 2], replicated, may hold values from 0 to 127, as said below
- thresholds: float32 [2, 64], replicated, may hold values from 0.2 to 1.6
Outputs:
- deblended: bfloat16 [128, 64, 8192], P(None, 'shot', 'tm')
Inputs may be any that keep to these rules, and one draw needn't show every extreme that they name: delays[e, k] is the delay of source 2 e + k in experiment e; some source has delay 0 and some has delay 128 - 1.
All inputs are finite; a program needn't handle non-finite values.
Results may differ from a plain program's by a relative error of at most 0.0066.
Values may be sent and summed in bfloat16 or wider, within the bound.
A program may use at most 64 MiB of HBM per device.

v0:
```python
import math

import jax
import jax.numpy as jnp
from jax import lax
from jax.experimental import pallas as pl
from jax.experimental.pallas import tpu as pltpu
from jax.sharding import PartitionSpec as P

SRC = 64
SRC_EXP = 2
WIN = 256
BLK = 128
ITERS = 2


RELAX = 0.5


def shifted(array, axis, by):
    count = lax.axis_size(axis)
    pairs = [(i, i + by) for i in range(count) if 0 <= i + by < count]
    return lax.ppermute(array, axis, pairs)


def phase_table(length_first, length_second, period):
    first_index = jnp.arange(length_first, dtype=jnp.int32)[:, None]
    second_index = jnp.arange(length_second, dtype=jnp.int32)[None, :]
    return (first_index * second_index % period).astype(jnp.float32) * (2.0 * math.pi / period)


def make_tables():
    time_angle = phase_table(WIN, WIN, WIN)
    time_scale = 1.0 / math.sqrt(WIN)
    cos_forward = jnp.cos(time_angle).astype(jnp.bfloat16)
    sin_forward = -jnp.sin(time_angle).astype(jnp.bfloat16)
    cos_inverse = jnp.cos(time_angle) * time_scale
    sin_inverse = -jnp.sin(time_angle) * time_scale
    source_angle = phase_table(SRC, SRC, SRC)
    cos_source = jnp.cos(source_angle) / math.sqrt(SRC)
    sin_source = jnp.sin(source_angle) / math.sqrt(SRC)
    return (cos_forward, sin_forward, cos_inverse, sin_inverse, cos_source, sin_source)


def blend(estimate, own_delays):
    receivers, sources, samples = estimate.shape
    blocks = samples // BLK
    experiments = sources // SRC_EXP
    earlier = shifted(estimate[:, :, samples - BLK :], "tm", 1)
    upper = estimate.reshape(receivers, sources, blocks, BLK)
    shifts = own_delays.reshape(-1)
    row_index = jnp.arange(BLK, dtype=jnp.int32)[None, :, None]
    column_index = jnp.arange(BLK, dtype=jnp.int32)[None, None, :]
    select_same = (row_index == column_index - shifts[:, None, None]).astype(jnp.bfloat16)
    select_prior = (row_index == BLK + column_index - shifts[:, None, None]).astype(jnp.bfloat16)
    same = jnp.einsum("rsnb,sbi->rsni", upper, select_same, preferred_element_type=jnp.float32)
    onward = jnp.einsum("rsnb,sbi->rsni", upper, select_prior, preferred_element_type=jnp.float32)
    edge_part = jnp.einsum(
        "rsb,sbi->rsi", earlier, select_prior, preferred_element_type=jnp.float32
    )
    same = jnp.sum(same.reshape(receivers, experiments, SRC_EXP, blocks, BLK), axis=2)
    onward = jnp.sum(onward.reshape(receivers, experiments, SRC_EXP, blocks, BLK), axis=2)
    edge_part = jnp.sum(edge_part.reshape(receivers, experiments, SRC_EXP, BLK), axis=2)
    carried = jnp.concatenate([edge_part[:, :, None], onward[:, :, : blocks - 1]], axis=2)
    return (same + carried).reshape(receivers, experiments, samples)


def spread(residual, own_delays):
    receivers, experiments, samples = residual.shape
    blocks = samples // BLK
    later = shifted(residual[:, :, :BLK], "tm", -1)
    lower = residual.reshape(receivers, experiments, blocks, BLK)
    row_index = jnp.arange(BLK, dtype=jnp.int32)[None, None, :, None]
    column_index = jnp.arange(BLK, dtype=jnp.int32)[None, None, None, :]
    select_same = (row_index == column_index + own_delays[:, :, None, None]).astype(jnp.bfloat16)
    select_next = (row_index + BLK == column_index + own_delays[:, :, None, None]).astype(
        jnp.bfloat16
    )
    same = jnp.einsum("rena,ekai->rekni", lower, select_same, preferred_element_type=jnp.float32)
    backward = jnp.einsum(
        "rena,ekai->rekni", lower, select_next, preferred_element_type=jnp.float32
    )
    edge_part = jnp.einsum("rea,ekai->reki", later, select_next, preferred_element_type=jnp.float32)
    carried = jnp.concatenate([backward[:, :, :, 1:], edge_part[:, :, :, None]], axis=3)
    return (same + carried).reshape(receivers, experiments * SRC_EXP, samples)


def filter_tables():
    time_angle = phase_table(WIN, WIN, WIN)
    time_scale = 1.0 / math.sqrt(WIN)
    forward = jnp.concatenate(
        [jnp.cos(time_angle).astype(jnp.bfloat16), -jnp.sin(time_angle).astype(jnp.bfloat16)],
        axis=1,
    )
    inverse = jnp.concatenate(
        [jnp.cos(time_angle) * time_scale, -jnp.sin(time_angle) * time_scale], axis=0
    )
    source_angle = phase_table(SRC, SRC, SRC)
    cos_source = jnp.cos(source_angle) / math.sqrt(SRC)
    sin_source = jnp.sin(source_angle) / math.sqrt(SRC)
    mix_forward = jnp.block([[cos_source, sin_source], [-sin_source, cos_source]])
    mix_inverse = jnp.block([[cos_source, -sin_source], [sin_source, cos_source]])
    return forward, inverse, mix_forward, mix_inverse


def filter_kernel(u_ref, forward_ref, inverse_ref, mixf_ref, mixi_ref, limit_ref, out_ref):
    sources = u_ref.shape[1]
    windows = u_ref.shape[2] // WIN
    scale = 1.0 / math.sqrt(WIN)
    exact = lax.Precision.HIGHEST
    limit = limit_ref[...]
    for w in range(windows):
        cols = slice(w * WIN, (w + 1) * WIN)
        spectrum = jnp.dot(u_ref[0, :, cols], forward_ref[...], preferred_element_type=jnp.float32)
        spectrum = spectrum * scale
        stacked = jnp.concatenate([spectrum[:, :WIN], spectrum[:, WIN:]], axis=0)
        coeffs = jnp.dot(mixf_ref[...], stacked, precision=exact, preferred_element_type=jnp.float32)
        real_part = coeffs[:sources]
        imag_part = coeffs[sources:]
        magnitude = jnp.sqrt(real_part * real_part + imag_part * imag_part)
        factor = jnp.maximum(magnitude - limit, 0.0) / jnp.maximum(magnitude, limit)
        kept = jnp.concatenate([real_part * factor, imag_part * factor], axis=0)
        back = jnp.dot(mixi_ref[...], kept, precision=exact, preferred_element_type=jnp.float32)
        joined = jnp.concatenate([back[:sources], back[sources:]], axis=1)
        restored = jnp.dot(joined, inverse_ref[...], precision=exact, preferred_element_type=jnp.float32)
        out_ref[0, :, cols] = restored.astype(out_ref.dtype)


def coherence(gathers, limits, tables):
    forward, inverse, mix_forward, mix_inverse = tables
    receivers, sources, samples = gathers.shape
    whole = lambda r: (0, 0)
    return pl.pallas_call(
        filter_kernel,
        grid=(receivers,),
        in_specs=[
            pl.BlockSpec((1, sources, samples), lambda r: (r, 0, 0)),
            pl.BlockSpec(forward.shape, whole),
            pl.BlockSpec(inverse.shape, whole),
            pl.BlockSpec(mix_forward.shape, whole),
            pl.BlockSpec(mix_inverse.shape, whole),
            pl.BlockSpec((sources, 1), whole),
        ],
        out_specs=pl.BlockSpec((1, sources, samples), lambda r: (r, 0, 0)),
        out_shape=jax.ShapeDtypeStruct(gathers.shape, jnp.bfloat16),
    )(gathers, forward, inverse, mix_forward, mix_inverse, limits.reshape(sources, 1))


def local(blended, delays, thresholds):
    tables = filter_tables()
    records = lax.all_to_all(blended, "shot", split_axis=0, concat_axis=1, tiled=True)
    estimate = None
    for sweep in range(ITERS):
        if sweep == 0:
            residual = records.astype(jnp.bfloat16)
            update = (RELAX * spread(residual, delays)).astype(jnp.bfloat16)
        else:
            residual = (records - blend(estimate, delays)).astype(jnp.bfloat16)
            update = (estimate.astype(jnp.float32) + RELAX * spread(residual, delays)).astype(
                jnp.bfloat16
            )
        estimate = coherence(update, thresholds[sweep], tables).astype(jnp.bfloat16)
    return lax.all_to_all(estimate, "shot", split_axis=1, concat_axis=0, tiled=True)


def solution(mesh):
    return jax.shard_map(
        local,
        mesh=mesh,
        in_specs=(P(None, "shot", "tm"), P(), P()),
        out_specs=P(None, "shot", "tm"),
        check_vma=False,
    )
```

profile of v0, /device:TPU:3, one launch (start us, length us, event | category | flops | bytes accessed | tf_op | source)
XLA Modules:
  0.0 118.0 jit_solution(11738969936571550580)
XLA Ops:
  0.0 12.1 %all-to-all-start = ((f32[128,1,1024]{2,1,0:T(1,128)}), f32[128,1,1024]{2,1,0:T(1,128)S(1)}, u32[]{:S(2)}, u32[]{:S(2)}) async-start(f32[128,1,1024]{2,1,0:T(1,128)} %param.3), calls=%async_computation | async-start | bytes 1048576 | tf_op jit(solution)/shard_map/all_to_all | solution.py:151
  12.1 1.0 convert_negate_fusion
  13.1 1.0 fusion.76
  14.0 0.2 sine_multiply_fusion
  14.2 0.1 fusion.93
  14.4 0.1 sub.43
  14.6 0.7 copy.26.limit_ref
  15.3 0.7 copy.32.limit_ref
  16.0 0.8 fusion.80
  16.8 0.7 pad_maximum_fusion.1.forward_ref
  17.5 1.1 negate_multiply_fusion
  18.5 0.8 pad_maximum_fusion.inverse_ref
  19.4 0.1 iota_add_fusion
  19.5 9.5 %all-to-all-done = f32[128,1,1024]{2,1,0:T(1,128)S(1)} async-done(((f32[128,1,1024]{2,1,0:T(1,128)}), f32[128,1,1024]{2,1,0:T(1,128)S(1)}, u32[]{:S(2)}, u32[]{:S(2)}) %all-to-all-start) | async-done | bytes 524320 | tf_op jit(solution)/shard_map/all_to_all | solution.py:151
  29.1 1.2 %reduce = f32[128,1024]{1,0:T(8,128)S(1)} reduce(f32[128,1,1024]{2,1,0:T(1,128)S(1)} %all-to-all-done, f32[]{:T(128)} %constant.47), dimensions={1}, to_apply=%all_to_all.28.reduce_sub_computation | reduce | bytes 1048580 | tf_op jit(solution)/shard_map/all_to_all | solution.py:151
  30.3 0.1 all_to_all.29
  30.5 0.2 all_to_all.31
  30.7 2.3 %collective-permute-start = (bf16[4,32,128]{2,0,1:T(4,128)(2,1)S(1)}, bf16[4,32,128]{2,0,1:T(4,128)(2,1)S(1)}, u32[]{:S(2)}, u32[]{:S(2)}) collective-permute-start(bf16[4,32,128]{2,0,1:T(4,128)(2,1)S(1)} %slice.46), channel_id=1, source_target_pairs={{1,0},{2,1},{3,2},{4,3},{5,4},{6,5},{7,6},{9,8},{10,9},{11,10},{12... | collective-permute-start | bytes 98312 | tf_op jit(solution)/shard_map/ppermute | solution.py:23
  33.0 0.9 fusion.31
  33.9 0.1 slice.32
  34.1 1.3 %collective-permute-done = bf16[4,32,128]{2,0,1:T(4,128)(2,1)S(1)} collective-permute-done((bf16[4,32,128]{2,0,1:T(4,128)(2,1)S(1)}, bf16[4,32,128]{2,0,1:T(4,128)(2,1)S(1)}, u32[]{:S(2)}, u32[]{:S(2)}) %collective-permute-start) | collective-permute-done | bytes 32800 | tf_op jit(solution)/shard_map/ppermute | solution.py:23
  35.4 0.8 fusion.2
  36.2 1.1 fusion.51
  37.2 0.1 reshape.110
  37.4 1.0 copy.43.u_ref
  38.3 16.5 %shard_map.37 = bf16[4,64,1024]{2,1,0:T(8,128)(2,1)} custom-call(bf16[4,64,1024]{2,1,0:T(8,128)(2,1)} %copy.43.u_ref, bf16[256,512]{1,0:T(8,128)(2,1)} %pad_maximum_fusion.1.forward_ref, f32[512,256]{1,0:T(8,128)} %pad_maximum_fusion.inverse_ref, f32[128,128]{1,0:T(8,128)} %get-tuple-element.8.mixf_ref, f32[128,128]{1,0:T(8,128)} %get-tuple-element.7.mixi_ref, ...), custom_call_target="tpu_custom_call" | custom-call | tf_op jit(solution)/shard_map/pallas_call | solution.py:133
  54.8 0.8 slice.34
  55.6 1.1 copy.46
  56.8 3.4 %collective-permute-start.1 = (bf16[4,64,128]{2,1,0:T(8,128)(2,1)S(1)}, bf16[4,64,128]{2,1,0:T(8,128)(2,1)S(1)}, u32[]{:S(2)}, u32[]{:S(2)}) collective-permute-start(bf16[4,64,128]{2,1,0:T(8,128)(2,1)S(1)} %slice.34), channel_id=1, source_target_pairs={{0,1},{1,2},{2,3},{3,4},{4,5},{5,6},{6,7},{8,9},{9,10},{10,11},{11... | collective-permute-start | bytes 196616 | tf_op jit(solution)/shard_map/ppermute | solution.py:23
  60.2 0.8 bitcast_reduce_fusion.1
  60.9 0.8 bitcast_reduce_fusion
  61.7 1.0 collective-permute-done.1
  62.7 0.8 bitcast_reduce_fusion.2
  63.5 0.2 fusion.68
  63.7 0.2 add.114
  63.9 2.3 %collective-permute-start.2 = (bf16[4,32,128]{2,0,1:T(4,128)(2,1)S(1)}, bf16[4,32,128]{2,0,1:T(4,128)(2,1)S(1)}, u32[]{:S(2)}, u32[]{:S(2)}) collective-permute-start(bf16[4,32,128]{2,0,1:T(4,128)(2,1)S(1)} %fusion.81), channel_id=1, source_target_pairs={{1,0},{2,1},{3,2},{4,3},{5,4},{6,5},{7,6},{9,8},{10,9},{11,10},{12... | collective-permute-start | bytes 98312 | tf_op jit(solution)/shard_map/ppermute | solution.py:23
  66.2 0.8 fusion.32
  67.0 0.1 slice.36
  67.2 1.4 %collective-permute-done.2 = bf16[4,32,128]{2,0,1:T(4,128)(2,1)S(1)} collective-permute-done((bf16[4,32,128]{2,0,1:T(4,128)(2,1)S(1)}, bf16[4,32,128]{2,0,1:T(4,128)(2,1)S(1)}, u32[]{:S(2)}, u32[]{:S(2)}) %collective-permute-start.2) | collective-permute-done | bytes 32800 | tf_op jit(solution)/shard_map/ppermute | solution.py:23
  68.6 0.8 fusion
  69.4 0.9 fusion.42
  70.3 0.4 reshape.111
  70.7 0.7 copy-done
  71.4 1.4 %fusion.54.u_ref = bf16[4,64,1024]{2,1,0:T(8,128)(2,1)} fusion(f32[4,64,1024]{2,0,1:T(4,128)S(1)} %reshape.111, bf16[4,64,1024]{2,1,0:T(8,128)(2,1)S(1)} %copy-done), kind=kLoop, calls=%fused_computation.43 | loop fusion | flops 786432 | bytes 2097152 | tf_op jit(solution)/shard_map/convert_element_type | solution.py:159
  72.8 16.5 %shard_map.38 = bf16[4,64,1024]{2,1,0:T(8,128)(2,1)} custom-call(bf16[4,64,1024]{2,1,0:T(8,128)(2,1)} %fusion.54.u_ref, bf16[256,512]{1,0:T(8,128)(2,1)} %pad_maximum_fusion.1.forward_ref, f32[512,256]{1,0:T(8,128)} %pad_maximum_fusion.inverse_ref, f32[128,128]{1,0:T(8,128)} %get-tuple-element.8.mixf_ref, f32[128,128]{1,0:T(8,128)} %get-tuple-element.7.mixi_ref, ...), custom_call_target="tpu_custom_call" | custom-call | tf_op jit(solution)/shard_map/pallas_call | solution.py:133
  89.3 1.4 %copy.33 = bf16[4,64,1024]{2,0,1:T(4,128)(2,1)S(1)} copy(bf16[4,64,1024]{2,1,0:T(8,128)(2,1)} %shard_map.38) | data formatting | bytes 1048576 | tf_op jit(solution)/shard_map/pallas_call | solution.py:133
  90.7 25.9 %all_to_all.39 = bf16[4,64,1024]{2,0,1:T(4,128)(2,1)S(1)} all-to-all(bf16[4,64,1024]{2,0,1:T(4,128)(2,1)S(1)} %copy.33), channel_id=1, replica_groups=mesh['shot'=32,'tm'=8] {'shot'}, dimensions={1} | all-to-all | bytes 1048576 | tf_op jit(solution)/shard_map/all_to_all | solution.py:163
  116.6 1.3 %copy.34 = bf16[32,4,2,1024]{3,2,1,0:T(2,128)(2,1)} copy(bf16[32,4,2,1024]{3,1,2,0:T(4,128)(2,1)S(1)} %bitcast.150) | data formatting | bytes 1048576 | tf_op jit(solution)/shard_map/all_to_all | solution.py:163
  (11 shorter events, 0.2 us)
Async XLA Ops:
  0.0 14.3 %copy-start.1 = (s32[32,2]{0,1:T(2,128)S(1)}, s32[32,2]{0,1:T(2,128)}, u32[]{:S(2)}) copy-start(s32[32,2]{0,1:T(2,128)} %param.4) | copy-start | bytes 772
  0.0 14.6 %copy-start.2 = (f32[2,64]{1,0:T(2,128)S(1)}, f32[2,64]{1,0:T(2,128)}, u32[]{:S(2)}) copy-start(f32[2,64]{1,0:T(2,128)} %param.5) | copy-start | bytes 1540
  0.0 29.1 %all-to-all-start = ((f32[128,1,1024]{2,1,0:T(1,128)}), f32[128,1,1024]{2,1,0:T(1,128)S(1)}, u32[]{:S(2)}, u32[]{:S(2)}) async-start(f32[128,1,1024]{2,1,0:T(1,128)} %param.3), calls=%async_computation | async-start | bytes 1048576 | tf_op jit(solution)/shard_map/all_to_all | solution.py:151
  30.7 4.7 %collective-permute-start = (bf16[4,32,128]{2,0,1:T(4,128)(2,1)S(1)}, bf16[4,32,128]{2,0,1:T(4,128)(2,1)S(1)}, u32[]{:S(2)}, u32[]{:S(2)}) collective-permute-start(bf16[4,32,128]{2,0,1:T(4,128)(2,1)S(1)} %slice.46), channel_id=1, source_target_pairs={{1,0},{2,1},{3,2},{4,3},{5,4},{6,5},{7,6},{9,8},{10,9},{11,10},{12... | collective-permute-start | bytes 98312 | tf_op jit(solution)/shard_map/ppermute | solution.py:23
  56.8 5.9 %collective-permute-start.1 = (bf16[4,64,128]{2,1,0:T(8,128)(2,1)S(1)}, bf16[4,64,128]{2,1,0:T(8,128)(2,1)S(1)}, u32[]{:S(2)}, u32[]{:S(2)}) collective-permute-start(bf16[4,64,128]{2,1,0:T(8,128)(2,1)S(1)} %slice.34), channel_id=1, source_target_pairs={{0,1},{1,2},{2,3},{3,4},{4,5},{5,6},{6,7},{8,9},{9,10},{10,11},{11... | collective-permute-start | bytes 196616 | tf_op jit(solution)/shard_map/ppermute | solution.py:23
  63.9 4.7 %collective-permute-start.2 = (bf16[4,32,128]{2,0,1:T(4,128)(2,1)S(1)}, bf16[4,32,128]{2,0,1:T(4,128)(2,1)S(1)}, u32[]{:S(2)}, u32[]{:S(2)}) collective-permute-start(bf16[4,32,128]{2,0,1:T(4,128)(2,1)S(1)} %fusion.81), channel_id=1, source_target_pairs={{1,0},{2,1},{3,2},{4,3},{5,4},{6,5},{7,6},{9,8},{10,9},{11,10},{12... | collective-permute-start | bytes 98312 | tf_op jit(solution)/shard_map/ppermute | solution.py:23
  70.3 1.0 copy-start
where the time goes:
time: 120 us; the launch traced here: 118 us
  Pallas kernels  32.9 us (27%)
  blocking collectives  25.9 us (22%)
  starting transfers between devices  20 us (17%)
  waiting for transfers between devices  13.2 us (11%)
  local copies, waits for them, and re-layouts  9.29 us (8%)
  other arithmetic  8.71 us (7%)
  matrix products  7.65 us (6%)
    pallas_call x2, Pallas kernels, coherence(): pl.pallas_call(filter_kernel, grid=(receivers,), in_specs=[pl.BlockSpec((...  32.9 us
    all_to_all x1, blocking collectives, local(): lax.all_to_all(estimate, 'shot', split_axis=1, concat_axis=0, tiled=True)  25.9 us
    all_to_all x1, starting transfers between devices, local(): lax.all_to_all(blended, 'shot', split_axis=0, concat_axis=1, tiled=True)  12.1 us
    all_to_all x1, waiting for transfers between devices, local(): lax.all_to_all(blended, 'shot', split_axis=0, concat_axis=1, tiled=True)  9.53 us
    ppermute x3, starting transfers between devices, shifted(): return lax.ppermute(array, axis, pairs)  7.94 us
    ppermute x3, waiting for transfers between devices, shifted(): return lax.ppermute(array, axis, pairs)  3.7 us
  transfers between devices with their start and end apart: 4, of which 4 were waited for; matrix products, arithmetic and copies ran while one was open for 9% of the time, Pallas kernels for 0%

commit v1 on v0

--- a/solution.py
+++ b/solution.py
@@ -85,6 +85,11 @@
     return (same + carried).reshape(receivers, experiments * SRC_EXP, samples)
 
 
+def split(value):
+    high = value.astype(jnp.bfloat16)
+    return high, (value - high.astype(jnp.float32)).astype(jnp.bfloat16)
+
+
 def filter_tables():
     time_angle = phase_table(WIN, WIN, WIN)
     time_scale = 1.0 / math.sqrt(WIN)
@@ -92,58 +97,82 @@
         [jnp.cos(time_angle).astype(jnp.bfloat16), -jnp.sin(time_angle).astype(jnp.bfloat16)],
         axis=1,
     )
-    inverse = jnp.concatenate(
-        [jnp.cos(time_angle) * time_scale, -jnp.sin(time_angle) * time_scale], axis=0
-    )
+    inverse_high, inverse_low = split(
+        jnp.concatenate([jnp.cos(time_angle) * time_scale, -jnp.sin(time_angle) * time_scale], 0)
+    )
+    inverse = jnp.concatenate([inverse_high, inverse_high, inverse_low], axis=0)
     source_angle = phase_table(SRC, SRC, SRC)
     cos_source = jnp.cos(source_angle) / math.sqrt(SRC)
     sin_source = jnp.sin(source_angle) / math.sqrt(SRC)
-    mix_forward = jnp.block([[cos_source, sin_source], [-sin_source, cos_source]])
-    mix_inverse = jnp.block([[cos_source, -sin_source], [sin_source, cos_source]])
+    mix_forward = split(jnp.block([[cos_source, sin_source], [-sin_source, cos_source]]))
+    mix_inverse = split(jnp.block([[cos_source, -sin_source], [sin_source, cos_source]]))
     return forward, inverse, mix_forward, mix_inverse
 
 
-def filter_kernel(u_ref, forward_ref, inverse_ref, mixf_ref, mixi_ref, limit_ref, out_ref):
-    sources = u_ref.shape[1]
-    windows = u_ref.shape[2] // WIN
+def mix(table, value):
+    table_high, table_low = table
+    value_high, value_low = split(value)
+    stacked = jnp.concatenate([value_high, value_low, value_high], axis=0)
+    joined = jnp.concatenate([table_high, table_high, table_low], axis=1)
+    return jnp.dot(joined, stacked, preferred_element_type=jnp.float32)
+
+
+def filter_kernel(
+    u_ref, forward_ref, inverse_ref, mfh_ref, mfl_ref, mih_ref, mil_ref, limit_ref, out_ref
+):
+    receivers, sources, samples = u_ref.shape
+    windows = samples // WIN
+    groups = [(r, w) for r in range(receivers) for w in range(windows)]
     scale = 1.0 / math.sqrt(WIN)
-    exact = lax.Precision.HIGHEST
+    rows = jnp.concatenate(
+        [u_ref[r, :, w * WIN : (w + 1) * WIN] for r, w in groups], axis=0
+    )
+    spectrum = jnp.dot(rows, forward_ref[...], preferred_element_type=jnp.float32) * scale
+    block = lambda g: slice(g * sources, (g + 1) * sources)
+    field = jnp.concatenate(
+        [
+            jnp.concatenate([spectrum[block(g), :WIN], spectrum[block(g), WIN:]], axis=0)
+            for g in range(len(groups))
+        ],
+        axis=1,
+    )
+    coeffs = mix((mfh_ref[...], mfl_ref[...]), field)
+    real_part = coeffs[:sources]
+    imag_part = coeffs[sources:]
     limit = limit_ref[...]
-    for w in range(windows):
-        cols = slice(w * WIN, (w + 1) * WIN)
-        spectrum = jnp.dot(u_ref[0, :, cols], forward_ref[...], preferred_element_type=jnp.float32)
-        spectrum = spectrum * scale
-        stacked = jnp.concatenate([spectrum[:, :WIN], spectrum[:, WIN:]], axis=0)
-        coeffs = jnp.dot(mixf_ref[...], stacked, precision=exact, preferred_element_type=jnp.float32)
-        real_part = coeffs[:sources]
-        imag_part = coeffs[sources:]
-        magnitude = jnp.sqrt(real_part * real_part + imag_part * imag_part)
-        factor = jnp.maximum(magnitude - limit, 0.0) / jnp.maximum(magnitude, limit)
-        kept = jnp.concatenate([real_part * factor, imag_part * factor], axis=0)
-        back = jnp.dot(mixi_ref[...], kept, precision=exact, preferred_element_type=jnp.float32)
-        joined = jnp.concatenate([back[:sources], back[sources:]], axis=1)
-        restored = jnp.dot(joined, inverse_ref[...], precision=exact, preferred_element_type=jnp.float32)
-        out_ref[0, :, cols] = restored.astype(out_ref.dtype)
+    magnitude = jnp.sqrt(real_part * real_part + imag_part * imag_part)
+    factor = jnp.maximum(magnitude - limit, 0.0) / jnp.maximum(magnitude, limit)
+    kept = jnp.concatenate([real_part * factor, imag_part * factor], axis=0)
+    back = mix((mih_ref[...], mil_ref[...]), kept)
+    lanes = lambda g: slice(g * WIN, (g + 1) * WIN)
+    joined = jnp.concatenate(
+        [
+            jnp.concatenate([back[:sources, lanes(g)], back[sources:, lanes(g)]], axis=1)
+            for g in range(len(groups))
+        ],
+        axis=0,
+    )
+    joined_high, joined_low = split(joined)
+    restored = jnp.dot(
+        jnp.concatenate([joined_high, joined_low, joined_high], axis=1),
+        inverse_ref[...],
+        preferred_element_type=jnp.float32,
+    )
+    for g, (r, w) in enumerate(groups):
+        out_ref[r, :, w * WIN : (w + 1) * WIN] = restored[block(g)].astype(out_ref.dtype)
 
 
 def coherence(gathers, limits, tables):
     forward, inverse, mix_forward, mix_inverse = tables
     receivers, sources, samples = gathers.shape
-    whole = lambda r: (0, 0)
+    vmem = pl.BlockSpec(memory_space=pltpu.VMEM)
     return pl.pallas_call(
         filter_kernel,
-        grid=(receivers,),
-        in_specs=[
-            pl.BlockSpec((1, sources, samples), lambda r: (r, 0, 0)),
-            pl.BlockSpec(forward.shape, whole),
-            pl.BlockSpec(inverse.shape, whole),
-            pl.BlockSpec(mix_forward.shape, whole),
-            pl.BlockSpec(mix_inverse.shape, whole),
-            pl.BlockSpec((sources, 1), whole),
-        ],
-        out_specs=pl.BlockSpec((1, sources, samples), lambda r: (r, 0, 0)),
+        in_specs=[vmem] * 8,
+        out_specs=vmem,
         out_shape=jax.ShapeDtypeStruct(gathers.shape, jnp.bfloat16),
-    )(gathers, forward, inverse, mix_forward, mix_inverse, limits.reshape(sources, 1))
+        compiler_params=pltpu.CompilerParams(vmem_limit_bytes=48 * 1024 * 1024),
+    )(gathers, forward, inverse, *mix_forward, *mix_inverse, limits.reshape(sources, 1))
 
 
 def local(blended, delays, thresholds):

time: 120 us -> 90.3 us (0.75)
  Pallas kernels: 32.9 us -> 5.92 us
  local copies, waits for them, and re-layouts: 9.29 us -> 4.97 us
  waiting for transfers between devices: 13.2 us -> 15.4 us
  other arithmetic: 8.71 us -> 6.68 us
  matrix products: 7.65 us -> 9.56 us
    pallas_call x2, Pallas kernels: 32.9 us -> 5.92 us  [coherence(): pl.pallas_call(filter_kernel, in_specs=[vmem] * 8, out_specs=vmem, out_sh...]
    all_to_all x1, waiting for transfers between devices: 9.53 us -> 12.7 us  [local(): lax.all_to_all(blended, 'shot', split_axis=0, concat_axis=1, tiled=True)]
    unnamed x8, local copies, waits for them, and re-layouts: 1.89 us -> 0.2 us
    concatenate x2 -> x1, other arithmetic: 1.59 us -> 0.05 us  [filter_tables(): inverse = jnp.concatenate([inverse_high, inverse_high, inverse_low], axis=0)]
    another operation x3, local copies, waits for them, and re-layouts: 1.42 us -> 0.2 us  [coherence(): limits.reshape(sources, 1)]
    mul x1, local copies, waits for them, and re-layouts: 0.36 us -> 1.56 us  [local(): RELAX * spread(residual, delays)]
  transfers between devices with their start and end apart: 4 -> 4, of which waited for: 4 -> 4; matrix products, arithmetic and copies ran while one was open for 9% -> 10% of each run, Pallas kernels for 0% -> 0%
where the time goes in v1:
time: 90.3 us; the launch traced here: 88.7 us
  blocking collectives  25.9 us (29%)
  starting transfers between devices  20 us (22%)
  waiting for transfers between devices  15.4 us (17%)
  matrix products  9.56 us (11%)
  other arithmetic  6.68 us (7%)
  Pallas kernels  5.92 us (7%)
  local copies, waits for them, and re-layouts  4.97 us (6%)
    all_to_all x1, blocking collectives, local(): lax.all_to_all(estimate, 'shot', split_axis=1, concat_axis=0, tiled=True)  25.9 us
    all_to_all x1, waiting for transfers between devices, local(): lax.all_to_all(blended, 'shot', split_axis=0, concat_axis=1, tiled=True)  12.7 us
    all_to_all x1, starting transfers between devices, local(): lax.all_to_all(blended, 'shot', split_axis=0, concat_axis=1, tiled=True)  12.1 us
    ppermute x3, starting transfers between devices, shifted(): return lax.ppermute(array, axis, pairs)  7.94 us
    pallas_call x2, Pallas kernels, coherence(): pl.pallas_call(filter_kernel, in_specs=[vmem] * 8, out_specs=vmem, out_sh...  5.92 us
    dot_general x2, matrix products, spread(): jnp.einsum('rena,ekai->rekni', lower, select_same, preferred_element_type...  2.95 us
    dot_general x2, matrix products, spread(): jnp.einsum('rena,ekai->rekni', lower, select_next, preferred_element_type...  2.69 us
    ppermute x3, waiting for transfers between devices, shifted(): return lax.ppermute(array, axis, pairs)  2.68 us
  transfers between devices with their start and end apart: 4, of which 4 were waited for; matrix products, arithmetic and copies ran while one was open for 10% of the time, Pallas kernels for 0%

profile of v1, /device:TPU:3, one launch (start us, length us, event | category | flops | bytes accessed | tf_op | source)
XLA Modules:
  0.0 88.7 jit_solution(7830087906307961471)
XLA Ops:
  0.0 12.1 %all-to-all-start = ((f32[128,1,1024]{2,1,0:T(1,128)}), f32[128,1,1024]{2,1,0:T(1,128)S(1)}, u32[]{:S(2)}, u32[]{:S(2)}) async-start(f32[128,1,1024]{2,1,0:T(1,128)} %param.3), calls=%async_computation | async-start | bytes 1048576 | tf_op jit(solution)/shard_map/all_to_all | solution.py:180
  12.1 1.0 %convert_negate_fusion = bf16[256,256]{1,0:T(8,128)(2,1)S(1)} fusion(), kind=kLoop, calls=%fused_computation.68 | loop fusion | flops 1179648 | bytes 131072 | tf_op jit(solution)/shard_map/neg | solution.py:97
  13.1 1.0 %fusion.77 = bf16[256,256]{1,0:T(8,128)(2,1)S(1)} fusion(), kind=kLoop, calls=%fused_computation.71 | loop fusion | flops 983040 | bytes 131072 | tf_op jit(solution)/shard_map/convert_element_type | solution.py:97
  14.0 1.1 %negate_multiply_fusion = (f32[256,256]{1,0:T(8,128)S(1)}, f32[256,256]{1,0:T(8,128)S(1)}) fusion(), kind=kLoop, calls=%fused_computation.62 | loop fusion | flops 1114112 | bytes 524288 | tf_op jit(solution)/shard_map/mul | solution.py:101
  15.1 0.2 sine_multiply_fusion
  15.3 0.1 fusion.96
  15.4 0.1 fusion.94
  15.5 0.1 subtract_convert_fusion.2
  15.6 0.1 copy.24
  15.7 0.1 sub.55
  15.8 0.1 copy.26.limit_ref
  15.9 0.1 copy.32.limit_ref
  16.2 0.1 iota_add_fusion
  16.3 0.1 broadcast_subtract_fusion
  16.3 0.1 pad_maximum_fusion.inverse_ref
  16.4 12.7 %all-to-all-done = f32[128,1,1024]{2,1,0:T(1,128)S(1)} async-done(((f32[128,1,1024]{2,1,0:T(1,128)}), f32[128,1,1024]{2,1,0:T(1,128)S(1)}, u32[]{:S(2)}, u32[]{:S(2)}) %all-to-all-start) | async-done | bytes 524320 | tf_op jit(solution)/shard_map/all_to_all | solution.py:180
  29.1 1.2 %reduce = f32[128,1024]{1,0:T(8,128)S(1)} reduce(f32[128,1,1024]{2,1,0:T(1,128)S(1)} %all-to-all-done, f32[]{:T(128)} %constant.47), dimensions={1}, to_apply=%all_to_all.28.reduce_sub_computation | reduce | bytes 1048580 | tf_op jit(solution)/shard_map/all_to_all | solution.py:180
  30.3 0.1 all_to_all.29
  30.5 0.2 all_to_all.31
  30.7 2.3 %collective-permute-start = (bf16[4,32,128]{2,0,1:T(4,128)(2,1)S(1)}, bf16[4,32,128]{2,0,1:T(4,128)(2,1)S(1)}, u32[]{:S(2)}, u32[]{:S(2)}) collective-permute-start(bf16[4,32,128]{2,0,1:T(4,128)(2,1)S(1)} %slice.46), channel_id=1, source_target_pairs={{1,0},{2,1},{3,2},{4,3},{5,4},{6,5},{7,6},{9,8},{10,9},{11,10},{12... | collective-permute-start | bytes 98312 | tf_op jit(solution)/shard_map/ppermute | solution.py:23
  33.0 0.9 %fusion.31 = f32[4,32,2,8,128]{4,3,0,2,1:T(8,128)S(1)} fusion(s32[32,2,128]{2,1,0:T(2,128)S(1)} %iota_add_fusion, s32[128]{0:T(128)S(1)} %iota_add_fusion.1, f32[4,32,8,128]{3,2,0,1:T(8,128)S(1)} %all_to_all.31), kind=kOutput, calls=%fused_computation.31 | convolution fusion | flops 68288512 | bytes 1606144 | tf_op jit(solution)/shard_map/rena,ekai->rekni/dot_general | solution.py:80
  33.9 0.1 slice.32
  34.1 1.3 %collective-permute-done = bf16[4,32,128]{2,0,1:T(4,128)(2,1)S(1)} collective-permute-done((bf16[4,32,128]{2,0,1:T(4,128)(2,1)S(1)}, bf16[4,32,128]{2,0,1:T(4,128)(2,1)S(1)}, u32[]{:S(2)}, u32[]{:S(2)}) %collective-permute-start) | collective-permute-done | bytes 32800 | tf_op jit(solution)/shard_map/ppermute | solution.py:23
  35.4 0.8 fusion.2
  36.2 1.1 %fusion.51 = bf16[4,32,2,8,128]{4,3,0,2,1:T(8,128)(2,1)S(1)} fusion(s32[32,2,128]{2,1,0:T(2,128)S(1)} %iota_add_fusion, f32[4,32,2,1,128]{4,3,0,2,1:T(1,128)S(1)} %bitcast.156, f32[4,32,2,7,128]{4,3,0,2,1:T(8,128)S(1)} %slice.32, f32[4,32,8,128]{3,2,0,1:T(8,128)S(1)} %all_to_all.31), kind=kOutput, calls=%fused_computation.39 | convolution fusion | flops 69337088 | bytes 2129920 | tf_op jit(solution)/shard_map/rena,ekai->rekni/dot_general | solution.py:79
  37.2 0.1 reshape.110
  37.4 0.2 copy.43.u_ref
  37.5 3.0 %shard_map.37 = bf16[4,64,1024]{2,1,0:T(8,128)(2,1)S(1)} custom-call(bf16[4,64,1024]{2,1,0:T(8,128)(2,1)S(1)} %copy.43.u_ref, bf16[256,512]{1,0:T(8,128)(2,1)S(1)} %pad_maximum_fusion.2.forward_ref, bf16[1536,256]{1,0:T(8,128)(2,1)S(1)} %pad_maximum_fusion.inverse_ref, bf16[128,128]{1,0:T(8,128)(2,1)S(1)} %get-tuple-element.10.mfh_ref, ...), custom_call_target="tpu_custom_call" | custom-call | tf_op jit(solution)/shard_map/pallas_call | solution.py:169
  40.5 0.1 copy.46
  40.6 3.4 %collective-permute-start.1 = (bf16[4,64,128]{2,1,0:T(8,128)(2,1)S(1)}, bf16[4,64,128]{2,1,0:T(8,128)(2,1)S(1)}, u32[]{:S(2)}, u32[]{:S(2)}) collective-permute-start(bf16[4,64,128]{2,1,0:T(8,128)(2,1)S(1)} %slice.34), channel_id=1, source_target_pairs={{0,1},{1,2},{2,3},{3,4},{4,5},{5,6},{6,7},{8,9},{9,10},{10,11},{11... | collective-permute-start | bytes 196616 | tf_op jit(solution)/shard_map/ppermute | solution.py:23
  44.0 0.8 bitcast_reduce_fusion.1
  44.8 0.8 bitcast_reduce_fusion
  45.6 1.0 %collective-permute-done.1 = bf16[4,64,128]{2,1,0:T(8,128)(2,1)S(1)} collective-permute-done((bf16[4,64,128]{2,1,0:T(8,128)(2,1)S(1)}, bf16[4,64,128]{2,1,0:T(8,128)(2,1)S(1)}, u32[]{:S(2)}, u32[]{:S(2)}) %collective-permute-start.1) | collective-permute-done | bytes 65568 | tf_op jit(solution)/shard_map/ppermute | solution.py:23
  46.5 0.8 bitcast_reduce_fusion.2
  47.3 0.9 %fusion.69 = (bf16[4,32,8,128,1]{3,2,0,4,1:T(8,128)(2,1)}, f32[4,32,8,128]{3,2,0,1:T(8,128)S(1)}) fusion(f32[4,32,8,128]{3,2,0,1:T(8,128)S(1)} %all_to_all.31, f32[4,32,8,128]{3,2,0,1:T(8,128)S(1)} %bitcast_reduce_fusion.1, f32[4,32,7,128]{3,2,0,1:T(8,128)S(1)} %bitcast.151, f32[4,32,1,128]{3,2,0,1:T(1,128)S(1)} %bitcast.154), kind=kLoop, calls=%fused_computation.58 | loop fusion | flops 524288 | bytes 2359296 | tf_op jit(solution)/shard_map/convert_element_type | solution.py:187
  48.3 0.2 add.114
  48.5 2.3 %collective-permute-start.2 = (bf16[4,32,128]{2,0,1:T(4,128)(2,1)S(1)}, bf16[4,32,128]{2,0,1:T(4,128)(2,1)S(1)}, u32[]{:S(2)}, u32[]{:S(2)}) collective-permute-start(bf16[4,32,128]{2,0,1:T(4,128)(2,1)S(1)} %fusion.82), channel_id=1, source_target_pairs={{1,0},{2,1},{3,2},{4,3},{5,4},{6,5},{7,6},{9,8},{10,9},{11,10},{12... | collective-permute-start | bytes 98312 | tf_op jit(solution)/shard_map/ppermute | solution.py:23
  50.8 1.8 %fusion.32 = f32[4,32,2,8,128]{4,3,0,2,1:T(8,128)S(1)} fusion(bf16[4,32,8,128,1]{3,2,0,4,1:T(8,128)(2,1)} %get-tuple-element.5, s32[32,2,128]{2,1,0:T(2,128)S(1)} %iota_add_fusion, s32[128]{0:T(128)S(1)} %iota_add_fusion.1), kind=kOutput, calls=%fused_computation.32 | convolution fusion | flops 68157440 | bytes 1344000 | tf_op jit(solution)/shard_map/rena,ekai->rekni/dot_general | solution.py:80
  52.5 0.2 slice.36
  52.7 0.4 collective-permute-done.2
  53.1 0.8 fusion
  53.9 1.9 %fusion.42 = f32[4,32,2,8,128]{4,3,0,2,1:T(8,128)} fusion(bf16[4,32,8,128,1]{3,2,0,4,1:T(8,128)(2,1)S(1)} %copy-done, s32[32,2,128]{2,1,0:T(2,128)S(1)} %iota_add_fusion, f32[4,32,2,1,128]{4,3,0,2,1:T(1,128)S(1)} %bitcast.155, f32[4,32,2,7,128]{4,3,0,2,1:T(8,128)S(1)} %slice.36), kind=kOutput, calls=%fused_computation.36 | convolution fusion | flops 68943872 | bytes 2392064 | tf_op jit(solution)/shard_map/rena,ekai->rekni/dot_general | solution.py:79
  55.8 1.6 %reshape.111 = f32[4,64,1024]{2,0,1:T(4,128)S(1)} reshape(f32[4,32,2,8,128]{4,3,0,2,1:T(8,128)} %fusion.42) | data formatting | bytes 2097152 | tf_op jit(solution)/shard_map/mul | solution.py:188
  57.4 0.7 fusion.54.u_ref
  58.1 3.0 %shard_map.38 = bf16[4,64,1024]{2,1,0:T(8,128)(2,1)S(1)} custom-call(bf16[4,64,1024]{2,1,0:T(8,128)(2,1)S(1)} %fusion.54.u_ref, bf16[256,512]{1,0:T(8,128)(2,1)S(1)} %pad_maximum_fusion.2.forward_ref, bf16[1536,256]{1,0:T(8,128)(2,1)S(1)} %pad_maximum_fusion.inverse_ref, bf16[128,128]{1,0:T(8,128)(2,1)S(1)} %get-tuple-element.10.mfh_ref, ...), custom_call_target="tpu_custom_call" | custom-call | tf_op jit(solution)/shard_map/pallas_call | solution.py:169
  61.0 0.4 copy.33
  61.4 25.9 %all_to_all.39 = bf16[4,64,1024]{2,0,1:T(4,128)(2,1)S(1)} all-to-all(bf16[4,64,1024]{2,0,1:T(4,128)(2,1)S(1)} %copy.33), channel_id=1, replica_groups=mesh['shot'=32,'tm'=8] {'shot'}, dimensions={1} | all-to-all | bytes 1048576 | tf_op jit(solution)/shard_map/all_to_all | solution.py:192
  87.4 1.3 %copy.34 = bf16[32,4,2,1024]{3,2,1,0:T(2,128)(2,1)} copy(bf16[32,4,2,1024]{3,1,2,0:T(4,128)(2,1)S(1)} %bitcast.150) | data formatting | bytes 1048576 | tf_op jit(solution)/shard_map/all_to_all | solution.py:192
  (14 shorter events, 0.2 us)
Async XLA Ops:
  0.0 15.6 %copy-start.1 = (s32[32,2]{0,1:T(2,128)S(1)}, s32[32,2]{0,1:T(2,128)}, u32[]{:S(2)}) copy-start(s32[32,2]{0,1:T(2,128)} %param.4) | copy-start | bytes 772
  0.0 15.8 %copy-start.2 = (f32[2,64]{1,0:T(2,128)S(1)}, f32[2,64]{1,0:T(2,128)}, u32[]{:S(2)}) copy-start(f32[2,64]{1,0:T(2,128)} %param.5) | copy-start | bytes 1540
  0.0 29.1 %all-to-all-start = ((f32[128,1,1024]{2,1,0:T(1,128)}), f32[128,1,1024]{2,1,0:T(1,128)S(1)}, u32[]{:S(2)}, u32[]{:S(2)}) async-start(f32[128,1,1024]{2,1,0:T(1,128)} %param.3), calls=%async_computation | async-start | bytes 1048576 | tf_op jit(solution)/shard_map/all_to_all | solution.py:180
  30.7 4.7 %collective-permute-start = (bf16[4,32,128]{2,0,1:T(4,128)(2,1)S(1)}, bf16[4,32,128]{2,0,1:T(4,128)(2,1)S(1)}, u32[]{:S(2)}, u32[]{:S(2)}) collective-permute-start(bf16[4,32,128]{2,0,1:T(4,128)(2,1)S(1)} %slice.46), channel_id=1, source_target_pairs={{1,0},{2,1},{3,2},{4,3},{5,4},{6,5},{7,6},{9,8},{10,9},{11,10},{12... | collective-permute-start | bytes 98312 | tf_op jit(solution)/shard_map/ppermute | solution.py:23
  40.6 5.9 %collective-permute-start.1 = (bf16[4,64,128]{2,1,0:T(8,128)(2,1)S(1)}, bf16[4,64,128]{2,1,0:T(8,128)(2,1)S(1)}, u32[]{:S(2)}, u32[]{:S(2)}) collective-permute-start(bf16[4,64,128]{2,1,0:T(8,128)(2,1)S(1)} %slice.34), channel_id=1, source_target_pairs={{0,1},{1,2},{2,3},{3,4},{4,5},{5,6},{6,7},{8,9},{9,10},{10,11},{11... | collective-permute-start | bytes 196616 | tf_op jit(solution)/shard_map/ppermute | solution.py:23
  48.5 4.7 %collective-permute-start.2 = (bf16[4,32,128]{2,0,1:T(4,128)(2,1)S(1)}, bf16[4,32,128]{2,0,1:T(4,128)(2,1)S(1)}, u32[]{:S(2)}, u32[]{:S(2)}) collective-permute-start(bf16[4,32,128]{2,0,1:T(4,128)(2,1)S(1)} %fusion.82), channel_id=1, source_target_pairs={{1,0},{2,1},{3,2},{4,3},{5,4},{6,5},{7,6},{9,8},{10,9},{11,10},{12... | collective-permute-start | bytes 98312 | tf_op jit(solution)/shard_map/ppermute | solution.py:23
  52.7 1.2 %copy-start = (bf16[4,32,8,128,1]{3,2,0,4,1:T(8,128)(2,1)S(1)}, bf16[4,32,8,128,1]{3,2,0,4,1:T(8,128)(2,1)}, u32[]{:S(2)}) copy-start(bf16[4,32,8,128,1]{3,2,0,4,1:T(8,128)(2,1)} %get-tuple-element.5) | copy-start | bytes 786436

commit v2 on v1

--- a/solution.py
+++ b/solution.py
@@ -1,6 +1,8 @@
 import math
 
 import jax
+import ml_dtypes
+import numpy as np
 import jax.numpy as jnp
 from jax import lax
 from jax.experimental import pallas as pl
@@ -90,22 +92,29 @@
     return high, (value - high.astype(jnp.float32)).astype(jnp.bfloat16)
 
 
+def exact_split(value):
+    high = value.astype(ml_dtypes.bfloat16)
+    low = (value - high.astype(np.float64)).astype(ml_dtypes.bfloat16)
+    return jnp.asarray(high), jnp.asarray(low)
+
+
 def filter_tables():
     time_angle = phase_table(WIN, WIN, WIN)
-    time_scale = 1.0 / math.sqrt(WIN)
     forward = jnp.concatenate(
         [jnp.cos(time_angle).astype(jnp.bfloat16), -jnp.sin(time_angle).astype(jnp.bfloat16)],
         axis=1,
     )
-    inverse_high, inverse_low = split(
-        jnp.concatenate([jnp.cos(time_angle) * time_scale, -jnp.sin(time_angle) * time_scale], 0)
+    turn = lambda n: (np.arange(n)[:, None] * np.arange(n)[None, :] % n) * (2.0 * np.pi / n)
+    time_turn = turn(WIN)
+    inverse_high, inverse_low = exact_split(
+        np.concatenate([np.cos(time_turn), -np.sin(time_turn)], axis=0) / math.sqrt(WIN)
     )
     inverse = jnp.concatenate([inverse_high, inverse_high, inverse_low], axis=0)
-    source_angle = phase_table(SRC, SRC, SRC)
-    cos_source = jnp.cos(source_angle) / math.sqrt(SRC)
-    sin_source = jnp.sin(source_angle) / math.sqrt(SRC)
-    mix_forward = split(jnp.block([[cos_source, sin_source], [-sin_source, cos_source]]))
-    mix_inverse = split(jnp.block([[cos_source, -sin_source], [sin_source, cos_source]]))
+    source_turn = turn(SRC)
+    cos_source = np.cos(source_turn) / math.sqrt(SRC)
+    sin_source = np.sin(source_turn) / math.sqrt(SRC)
+    mix_forward = exact_split(np.block([[cos_source, sin_source], [-sin_source, cos_source]]))
+    mix_inverse = exact_split(np.block([[cos_source, -sin_source], [sin_source, cos_source]]))
     return forward, inverse, mix_forward, mix_inverse
 
 

time: 90.3 us -> 91.2 us (level)
  waiting for transfers between devices: 15.4 us -> 17.1 us
  other arithmetic: 6.68 us -> 5.01 us
    all_to_all x1, waiting for transfers between devices: 12.7 us -> 14.4 us  [local(): lax.all_to_all(blended, 'shot', split_axis=0, concat_axis=1, tiled=True)]
    mul x1 -> x0, other arithmetic: 1.06 us -> none  [filter_tables(): -jnp.sin(time_angle) * time_scale]
  transfers between devices with their start and end apart: 4 -> 4, of which waited for: 4 -> 4; matrix products, arithmetic and copies ran while one was open for 10% -> 8% of each run, Pallas kernels for 0% -> 0%
where the time goes in v2:
time: 91.2 us; the launch traced here: 89.5 us
  blocking collectives  25.9 us (28%)
  starting transfers between devices  20 us (22%)
  waiting for transfers between devices  17.1 us (19%)
  matrix products  9.55 us (10%)
  Pallas kernels  5.92 us (6%)
  local copies, waits for them, and re-layouts  5.77 us (6%)
  other arithmetic  5.01 us (5%)
    all_to_all x1, blocking collectives, local(): lax.all_to_all(estimate, 'shot', split_axis=1, concat_axis=0, tiled=True)  25.9 us
    all_to_all x1, waiting for transfers between devices, local(): lax.all_to_all(blended, 'shot', split_axis=0, concat_axis=1, tiled=True)  14.4 us
    all_to_all x1, starting transfers between devices, local(): lax.all_to_all(blended, 'shot', split_axis=0, concat_axis=1, tiled=True)  12.1 us
    ppermute x3, starting transfers between devices, shifted(): return lax.ppermute(array, axis, pairs)  7.94 us
    pallas_call x2, Pallas kernels, coherence(): pl.pallas_call(filter_kernel, in_specs=[vmem] * 8, out_specs=vmem, out_sh...  5.92 us
    dot_general x2, matrix products, spread(): jnp.einsum('rena,ekai->rekni', lower, select_same, preferred_element_type...  2.94 us
    dot_general x2, matrix products, spread(): jnp.einsum('rena,ekai->rekni', lower, select_next, preferred_element_type...  2.69 us
    ppermute x3, waiting for transfers between devices, shifted(): return lax.ppermute(array, axis, pairs)  2.68 us
  transfers between devices with their start and end apart: 4, of which 4 were waited for; matrix products, arithmetic and copies ran while one was open for 8% of the time, Pallas kernels for 0%

profile of v2, /device:TPU:3, one launch (start us, length us, event | category | flops | bytes accessed | tf_op | source)
XLA Modules:
  0.0 89.5 jit_solution(2549452080453395224)
XLA Ops:
  0.0 12.1 %all-to-all-start = ((f32[128,1,1024]{2,1,0:T(1,128)}), f32[128,1,1024]{2,1,0:T(1,128)S(1)}, u32[]{:S(2)}, u32[]{:S(2)}) async-start(f32[128,1,1024]{2,1,0:T(1,128)} %param.9), calls=%async_computation | async-start | bytes 1048576 | tf_op jit(solution)/shard_map/all_to_all | solution.py:189
  12.1 0.1 copy.30
  12.2 0.1 sub.43
  12.3 0.1 copy.32.limit_ref
  12.4 0.1 copy.38.limit_ref
  12.5 1.0 %fusion.74 = bf16[256,256]{1,0:T(8,128)(2,1)S(1)} fusion(), kind=kLoop, calls=%fused_computation.63 | loop fusion | flops 1179648 | bytes 131072 | tf_op jit(solution)/shard_map/neg | solution.py:104
  13.5 1.0 %cosine_convert_fusion = bf16[256,256]{1,0:T(8,128)(2,1)S(1)} fusion(), kind=kLoop, calls=%fused_computation.59 | loop fusion | flops 983040 | bytes 131072 | tf_op jit(solution)/shard_map/convert_element_type | solution.py:104
  14.5 0.1 iota_add_fusion
  14.6 0.1 broadcast_subtract_fusion
  14.7 14.4 %all-to-all-done = f32[128,1,1024]{2,1,0:T(1,128)S(1)} async-done(((f32[128,1,1024]{2,1,0:T(1,128)}), f32[128,1,1024]{2,1,0:T(1,128)S(1)}, u32[]{:S(2)}, u32[]{:S(2)}) %all-to-all-start) | async-done | bytes 524320 | tf_op jit(solution)/shard_map/all_to_all | solution.py:189
  29.1 1.2 %reduce = f32[128,1024]{1,0:T(8,128)S(1)} reduce(f32[128,1,1024]{2,1,0:T(1,128)S(1)} %all-to-all-done, f32[]{:T(128)} %constant.44), dimensions={1}, to_apply=%all_to_all.28.reduce_sub_computation | reduce | bytes 1048580 | tf_op jit(solution)/shard_map/all_to_all | solution.py:189
  30.3 0.1 all_to_all.29
  30.5 0.2 all_to_all.31
  30.7 2.3 %collective-permute-start = (bf16[4,32,128]{2,0,1:T(4,128)(2,1)S(1)}, bf16[4,32,128]{2,0,1:T(4,128)(2,1)S(1)}, u32[]{:S(2)}, u32[]{:S(2)}) collective-permute-start(bf16[4,32,128]{2,0,1:T(4,128)(2,1)S(1)} %slice.46), channel_id=1, source_target_pairs={{1,0},{2,1},{3,2},{4,3},{5,4},{6,5},{7,6},{9,8},{10,9},{11,10},{12... | collective-permute-start | bytes 98312 | tf_op jit(solution)/shard_map/ppermute | solution.py:25
  33.0 0.9 %fusion.31 = f32[4,32,2,8,128]{4,3,0,2,1:T(8,128)S(1)} fusion(s32[32,2,128]{2,1,0:T(2,128)S(1)} %iota_add_fusion, s32[128]{0:T(128)S(1)} %iota_add_fusion.1, f32[4,32,8,128]{3,2,0,1:T(8,128)S(1)} %all_to_all.31), kind=kOutput, calls=%fused_computation.31 | convolution fusion | flops 68288512 | bytes 1606144 | tf_op jit(solution)/shard_map/rena,ekai->rekni/dot_general | solution.py:82
  33.9 0.1 slice.32
  34.1 1.3 %collective-permute-done = bf16[4,32,128]{2,0,1:T(4,128)(2,1)S(1)} collective-permute-done((bf16[4,32,128]{2,0,1:T(4,128)(2,1)S(1)}, bf16[4,32,128]{2,0,1:T(4,128)(2,1)S(1)}, u32[]{:S(2)}, u32[]{:S(2)}) %collective-permute-start) | collective-permute-done | bytes 32800 | tf_op jit(solution)/shard_map/ppermute | solution.py:25
  35.4 0.8 fusion.2
  36.2 1.0 %fusion.51 = bf16[4,32,2,8,128]{4,3,0,2,1:T(8,128)(2,1)S(1)} fusion(s32[32,2,128]{2,1,0:T(2,128)S(1)} %iota_add_fusion, f32[4,32,2,1,128]{4,3,0,2,1:T(1,128)S(1)} %bitcast.156, f32[4,32,2,7,128]{4,3,0,2,1:T(8,128)S(1)} %slice.32, f32[4,32,8,128]{3,2,0,1:T(8,128)S(1)} %all_to_all.31), kind=kOutput, calls=%fused_computation.39 | convolution fusion | flops 69337088 | bytes 2129920 | tf_op jit(solution)/shard_map/rena,ekai->rekni/dot_general | solution.py:81
  37.2 0.0 copy-start
  37.2 0.0 copy-start.1
  37.3 0.0 copy-start.2
  37.3 0.0 copy-start.3
  37.3 0.0 copy-start.4
  37.3 0.1 reshape.110
  37.4 0.2 copy.49.u_ref
  37.6 0.8 copy-done
  38.4 3.0 %shard_map.91 = bf16[4,64,1024]{2,1,0:T(8,128)(2,1)S(1)} custom-call(bf16[4,64,1024]{2,1,0:T(8,128)(2,1)S(1)} %copy.49.u_ref, bf16[256,512]{1,0:T(8,128)(2,1)S(1)} %pad_maximum_fusion.forward_ref, bf16[1536,256]{1,0:T(8,128)(2,1)S(1)} %copy-done, bf16[128,128]{1,0:T(8,128)(2,1)S(1)} %copy-done.1, bf16[128,128]{1,0:T(8,128)(2,1)S(1)} %copy-done.2, ...), custom_call_target="tpu_custom_call" | custom-call | tf_op jit(solution)/shard_map/pallas_call | solution.py:178
  41.4 0.1 copy.52
  41.5 3.4 %collective-permute-start.1 = (bf16[4,64,128]{2,1,0:T(8,128)(2,1)S(1)}, bf16[4,64,128]{2,1,0:T(8,128)(2,1)S(1)}, u32[]{:S(2)}, u32[]{:S(2)}) collective-permute-start(bf16[4,64,128]{2,1,0:T(8,128)(2,1)S(1)} %slice.34), channel_id=1, source_target_pairs={{0,1},{1,2},{2,3},{3,4},{4,5},{5,6},{6,7},{8,9},{9,10},{10,11},{11... | collective-permute-start | bytes 196616 | tf_op jit(solution)/shard_map/ppermute | solution.py:25
  44.9 0.8 bitcast_reduce_fusion.1
  45.6 0.8 bitcast_reduce_fusion
  46.4 1.0 %collective-permute-done.1 = bf16[4,64,128]{2,1,0:T(8,128)(2,1)S(1)} collective-permute-done((bf16[4,64,128]{2,1,0:T(8,128)(2,1)S(1)}, bf16[4,64,128]{2,1,0:T(8,128)(2,1)S(1)}, u32[]{:S(2)}, u32[]{:S(2)}) %collective-permute-start.1) | collective-permute-done | bytes 65568 | tf_op jit(solution)/shard_map/ppermute | solution.py:25
  47.4 0.8 bitcast_reduce_fusion.2
  48.2 0.9 %fusion.68 = (bf16[4,32,8,128,1]{3,2,0,4,1:T(8,128)(2,1)}, f32[4,32,8,128]{3,2,0,1:T(8,128)S(1)}) fusion(f32[4,32,8,128]{3,2,0,1:T(8,128)S(1)} %all_to_all.31, f32[4,32,8,128]{3,2,0,1:T(8,128)S(1)} %bitcast_reduce_fusion.1, f32[4,32,7,128]{3,2,0,1:T(8,128)S(1)} %bitcast.151, f32[4,32,1,128]{3,2,0,1:T(1,128)S(1)} %bitcast.154), kind=kLoop, calls=%fused_computation.54 | loop fusion | flops 524288 | bytes 2359296 | tf_op jit(solution)/shard_map/convert_element_type | solution.py:196
  49.1 0.2 add.89
  49.3 2.3 %collective-permute-start.2 = (bf16[4,32,128]{2,0,1:T(4,128)(2,1)S(1)}, bf16[4,32,128]{2,0,1:T(4,128)(2,1)S(1)}, u32[]{:S(2)}, u32[]{:S(2)}) collective-permute-start(bf16[4,32,128]{2,0,1:T(4,128)(2,1)S(1)} %fusion.77), channel_id=1, source_target_pairs={{1,0},{2,1},{3,2},{4,3},{5,4},{6,5},{7,6},{9,8},{10,9},{11,10},{12... | collective-permute-start | bytes 98312 | tf_op jit(solution)/shard_map/ppermute | solution.py:25
  51.6 1.8 %fusion.32 = f32[4,32,2,8,128]{4,3,0,2,1:T(8,128)S(1)} fusion(bf16[4,32,8,128,1]{3,2,0,4,1:T(8,128)(2,1)} %get-tuple-element.5, s32[32,2,128]{2,1,0:T(2,128)S(1)} %iota_add_fusion, s32[128]{0:T(128)S(1)} %iota_add_fusion.1), kind=kOutput, calls=%fused_computation.32 | convolution fusion | flops 68157440 | bytes 1344000 | tf_op jit(solution)/shard_map/rena,ekai->rekni/dot_general | solution.py:82
  53.4 0.2 slice.36
  53.6 0.4 collective-permute-done.2
  54.0 0.8 fusion
  54.8 1.9 %fusion.42 = f32[4,32,2,8,128]{4,3,0,2,1:T(8,128)} fusion(bf16[4,32,8,128,1]{3,2,0,4,1:T(8,128)(2,1)S(1)} %copy-done.5, s32[32,2,128]{2,1,0:T(2,128)S(1)} %iota_add_fusion, f32[4,32,2,1,128]{4,3,0,2,1:T(1,128)S(1)} %bitcast.155, f32[4,32,2,7,128]{4,3,0,2,1:T(8,128)S(1)} %slice.36), kind=kOutput, calls=%fused_computation.36 | convolution fusion | flops 68943872 | bytes 2392064 | tf_op jit(solution)/shard_map/rena,ekai->rekni/dot_general | solution.py:81
  56.7 1.6 %reshape.111 = f32[4,64,1024]{2,0,1:T(4,128)S(1)} reshape(f32[4,32,2,8,128]{4,3,0,2,1:T(8,128)} %fusion.42) | data formatting | bytes 2097152 | tf_op jit(solution)/shard_map/mul | solution.py:197
  58.2 0.7 fusion.54.u_ref
  58.9 3.0 %shard_map.92 = bf16[4,64,1024]{2,1,0:T(8,128)(2,1)S(1)} custom-call(bf16[4,64,1024]{2,1,0:T(8,128)(2,1)S(1)} %fusion.54.u_ref, bf16[256,512]{1,0:T(8,128)(2,1)S(1)} %pad_maximum_fusion.forward_ref, bf16[1536,256]{1,0:T(8,128)(2,1)S(1)} %copy-done, bf16[128,128]{1,0:T(8,128)(2,1)S(1)} %copy-done.1, bf16[128,128]{1,0:T(8,128)(2,1)S(1)} %copy-done.2, ...), custom_call_target="tpu_custom_call" | custom-call | tf_op jit(solution)/shard_map/pallas_call | solution.py:178
  61.9 0.4 copy.39
  62.3 25.9 %all_to_all.39 = bf16[4,64,1024]{2,0,1:T(4,128)(2,1)S(1)} all-to-all(bf16[4,64,1024]{2,0,1:T(4,128)(2,1)S(1)} %copy.39), channel_id=1, replica_groups=mesh['shot'=32,'tm'=8] {'shot'}, dimensions={1} | all-to-all | bytes 1048576 | tf_op jit(solution)/shard_map/all_to_all | solution.py:201
  88.2 1.3 %copy.40 = bf16[32,4,2,1024]{3,2,1,0:T(2,128)(2,1)} copy(bf16[32,4,2,1024]{3,1,2,0:T(4,128)(2,1)S(1)} %bitcast.150) | data formatting | bytes 1048576 | tf_op jit(solution)/shard_map/all_to_all | solution.py:201
  (16 shorter events, 0.1 us)
Async XLA Ops:
  0.0 12.1 %copy-start.7 = (f32[2,64]{1,0:T(2,128)S(1)}, f32[2,64]{1,0:T(2,128)}, u32[]{:S(2)}) copy-start(f32[2,64]{1,0:T(2,128)} %param.11) | copy-start | bytes 1540
  0.0 12.1 %copy-start.6 = (s32[32,2]{0,1:T(2,128)S(1)}, s32[32,2]{0,1:T(2,128)}, u32[]{:S(2)}) copy-start(s32[32,2]{0,1:T(2,128)} %param.10) | copy-start | bytes 772
  0.0 29.1 %all-to-all-start = ((f32[128,1,1024]{2,1,0:T(1,128)}), f32[128,1,1024]{2,1,0:T(1,128)S(1)}, u32[]{:S(2)}, u32[]{:S(2)}) async-start(f32[128,1,1024]{2,1,0:T(1,128)} %param.9), calls=%async_computation | async-start | bytes 1048576 | tf_op jit(solution)/shard_map/all_to_all | solution.py:189
  30.7 4.7 %collective-permute-start = (bf16[4,32,128]{2,0,1:T(4,128)(2,1)S(1)}, bf16[4,32,128]{2,0,1:T(4,128)(2,1)S(1)}, u32[]{:S(2)}, u32[]{:S(2)}) collective-permute-start(bf16[4,32,128]{2,0,1:T(4,128)(2,1)S(1)} %slice.46), channel_id=1, source_target_pairs={{1,0},{2,1},{3,2},{4,3},{5,4},{6,5},{7,6},{9,8},{10,9},{11,10},{12... | collective-permute-start | bytes 98312 | tf_op jit(solution)/shard_map/ppermute | solution.py:25
  37.2 1.1 %copy-start = (bf16[1536,256]{1,0:T(8,128)(2,1)S(1)}, bf16[1536,256]{1,0:T(8,128)(2,1)}, u32[]{:S(2)}) copy-start(bf16[1536,256]{1,0:T(8,128)(2,1)} %constant.43.inverse_ref) | copy-start | bytes 2359300
  37.2 1.1 %copy-start.1 = (bf16[128,128]{1,0:T(8,128)(2,1)S(1)}, bf16[128,128]{1,0:T(8,128)(2,1)}, u32[]{:S(2)}) copy-start(bf16[128,128]{1,0:T(8,128)(2,1)} %constant.38.clone.mfh_ref) | copy-start | bytes 98308
  37.3 1.1 %copy-start.2 = (bf16[128,128]{1,0:T(8,128)(2,1)S(1)}, bf16[128,128]{1,0:T(8,128)(2,1)}, u32[]{:S(2)}) copy-start(bf16[128,128]{1,0:T(8,128)(2,1)} %constant.39.clone.mfl_ref) | copy-start | bytes 98308
  37.3 1.1 %copy-start.3 = (bf16[128,128]{1,0:T(8,128)(2,1)S(1)}, bf16[128,128]{1,0:T(8,128)(2,1)}, u32[]{:S(2)}) copy-start(bf16[128,128]{1,0:T(8,128)(2,1)} %constant.40.clone.mih_ref) | copy-start | bytes 98308
  37.3 1.1 %copy-start.4 = (bf16[128,128]{1,0:T(8,128)(2,1)S(1)}, bf16[128,128]{1,0:T(8,128)(2,1)}, u32[]{:S(2)}) copy-start(bf16[128,128]{1,0:T(8,128)(2,1)} %constant.41.clone.mil_ref) | copy-start | bytes 98308
  41.5 5.9 %collective-permute-start.1 = (bf16[4,64,128]{2,1,0:T(8,128)(2,1)S(1)}, bf16[4,64,128]{2,1,0:T(8,128)(2,1)S(1)}, u32[]{:S(2)}, u32[]{:S(2)}) collective-permute-start(bf16[4,64,128]{2,1,0:T(8,128)(2,1)S(1)} %slice.34), channel_id=1, source_target_pairs={{0,1},{1,2},{2,3},{3,4},{4,5},{5,6},{6,7},{8,9},{9,10},{10,11},{11... | collective-permute-start | bytes 196616 | tf_op jit(solution)/shard_map/ppermute | solution.py:25
  49.3 4.7 %collective-permute-start.2 = (bf16[4,32,128]{2,0,1:T(4,128)(2,1)S(1)}, bf16[4,32,128]{2,0,1:T(4,128)(2,1)S(1)}, u32[]{:S(2)}, u32[]{:S(2)}) collective-permute-start(bf16[4,32,128]{2,0,1:T(4,128)(2,1)S(1)} %fusion.77), channel_id=1, source_target_pairs={{1,0},{2,1},{3,2},{4,3},{5,4},{6,5},{7,6},{9,8},{10,9},{11,10},{12... | collective-permute-start | bytes 98312 | tf_op jit(solution)/shard_map/ppermute | solution.py:25
  53.6 1.2 %copy-start.5 = (bf16[4,32,8,128,1]{3,2,0,4,1:T(8,128)(2,1)S(1)}, bf16[4,32,8,128,1]{3,2,0,4,1:T(8,128)(2,1)}, u32[]{:S(2)}) copy-start(bf16[4,32,8,128,1]{3,2,0,4,1:T(8,128)(2,1)} %get-tuple-element.5) | copy-start | bytes 786436

commit v3 on v2

--- a/solution.py
+++ b/solution.py
@@ -1,3 +1,4 @@
+import functools
 import math
 
 import jax
@@ -184,6 +185,76 @@
     )(gathers, forward, inverse, *mix_forward, *mix_inverse, limits.reshape(sources, 1))
 
 
+def exchange_kernel(count, outgoing, incoming, src_ref, out_ref, send_sem, recv_sem, own_sem):
+    me = lax.axis_index("shot")
+    row = lax.axis_index("tm")
+    barrier = pltpu.get_barrier_semaphore()
+
+    def greet(step, carry):
+        peer = lax.rem(me + step, count)
+        pl.semaphore_signal(barrier, 1, device_id=(peer, row), device_id_type=pl.DeviceIdType.MESH)
+        return carry
+
+    lax.fori_loop(1, count, greet, 0)
+    pl.semaphore_wait(barrier, count - 1)
+    own = pltpu.make_async_copy(src_ref.at[outgoing(me)], out_ref.at[incoming(me)], own_sem)
+    own.start()
+
+    def remote(peer, sender):
+        return pltpu.make_async_remote_copy(
+            src_ref=src_ref.at[outgoing(peer)],
+            dst_ref=out_ref.at[incoming(sender)],
+            send_sem=send_sem.at[peer],
+            recv_sem=recv_sem.at[sender],
+            device_id=(peer, row),
+            device_id_type=pl.DeviceIdType.MESH,
+        )
+
+    def send(step, carry):
+        remote(lax.rem(me + step, count), me).start()
+        return carry
+
+    lax.fori_loop(1, count, send, 0)
+
+    def finish(step, carry):
+        peer = lax.rem(me + step, count)
+        remote(peer, me).wait_send()
+        remote(me, peer).wait_recv()
+        return carry
+
+    lax.fori_loop(1, count, finish, 0)
+    own.wait()
+
+
+def exchange(value, out_shape, outgoing, incoming):
+    count = lax.axis_size("shot")
+    anywhere = pl.BlockSpec(memory_space=pl.ANY)
+    return pl.pallas_call(
+        functools.partial(exchange_kernel, count, outgoing, incoming),
+        in_specs=[anywhere],
+        out_specs=anywhere,
+        out_shape=jax.ShapeDtypeStruct(out_shape, value.dtype),
+        scratch_shapes=[
+            pltpu.SemaphoreType.DMA((count,)),
+            pltpu.SemaphoreType.DMA((count,)),
+            pltpu.SemaphoreType.DMA,
+        ],
+        compiler_params=pltpu.CompilerParams(collective_id=0, has_side_effects=True),
+    )(value)
+
+
+def to_sources(estimate):
+    receivers, sources, samples = estimate.shape
+    count = lax.axis_size("shot")
+    own = sources // count
+    return exchange(
+        estimate,
+        (receivers * count, own, samples),
+        lambda peer: (slice(None), pl.ds(peer * own, own), slice(None)),
+        lambda sender: (pl.ds(sender * receivers, receivers), slice(None), slice(None)),
+    )
+
+
 def local(blended, delays, thresholds):
     tables = filter_tables()
     records = lax.all_to_all(blended, "shot", split_axis=0, concat_axis=1, tiled=True)
@@ -197,8 +268,8 @@
             update = (estimate.astype(jnp.float32) + RELAX * spread(residual, delays)).astype(
                 jnp.bfloat16
             )
-        estimate = coherence(update, thresholds[sweep], tables).astype(jnp.bfloat16)
-    return lax.all_to_all(estimate, "shot", split_axis=1, concat_axis=0, tiled=True)
+        estimate = coherence(update, thresholds[sweep], tables)
+    return to_sources(estimate)
 
 
 def solution(mesh):

time: 91.2 us -> 89.9 us (0.986)
  blocking collectives: 25.9 us -> 0 us
  Pallas kernels: 5.92 us -> 29.5 us
  local copies, waits for them, and re-layouts: 5.77 us -> 7.04 us
    all_to_all x1 -> x0, blocking collectives: 25.9 us -> none  [local(): lax.all_to_all(estimate, 'shot', split_axis=1, concat_axis=0, tiled=True)]
    pallas_call x0 -> x1, Pallas kernels: none -> 23.6 us  [exchange(): pl.pallas_call(functools.partial(exchange_kernel, count, outgoing, incomi...]
    unnamed x18 -> x21, local copies, waits for them, and re-layouts: 1.01 us -> 3.99 us
    all_to_all x1 -> x0, local copies, waits for them, and re-layouts: 1.31 us -> none  [local(): lax.all_to_all(estimate, 'shot', split_axis=1, concat_axis=0, tiled=True)]
where the time goes in v3:
time: 89.9 us; the launch traced here: 88.5 us
  Pallas kernels  29.5 us (33%)
  starting transfers between devices  20 us (22%)
  waiting for transfers between devices  17.1 us (19%)
  matrix products  9.56 us (11%)
  local copies, waits for them, and re-layouts  7.04 us (8%)
  other arithmetic  5.01 us (6%)
    pallas_call x1, Pallas kernels, exchange(): pl.pallas_call(functools.partial(exchange_kernel, count, outgoing, incomi...  23.6 us
    all_to_all x1, waiting for transfers between devices, local(): lax.all_to_all(blended, 'shot', split_axis=0, concat_axis=1, tiled=True)  14.4 us
    all_to_all x1, starting transfers between devices, local(): lax.all_to_all(blended, 'shot', split_axis=0, concat_axis=1, tiled=True)  12.1 us
    ppermute x3, starting transfers between devices, shifted(): return lax.ppermute(array, axis, pairs)  7.94 us
    pallas_call x2, Pallas kernels, coherence(): pl.pallas_call(filter_kernel, in_specs=[vmem] * 8, out_specs=vmem, out_sh...  5.92 us
    unnamed x21, local copies, waits for them, and re-layouts  3.99 us
    dot_general x2, matrix products, spread(): jnp.einsum('rena,ekai->rekni', lower, select_same, preferred_element_type...  2.95 us
    dot_general x2, matrix products, spread(): jnp.einsum('rena,ekai->rekni', lower, select_next, preferred_element_type...  2.69 us
  transfers between devices with their start and end apart: 4, of which 4 were waited for; matrix products, arithmetic and copies ran while one was open for 8% of the time, Pallas kernels for 0%

profile of v3, /device:TPU:3, one launch (start us, length us, event | category | flops | bytes accessed | tf_op | source)
XLA Modules:
  0.0 88.5 jit_solution(4108516216177867603)
XLA Ops:
  0.0 12.1 %all-to-all-start = ((f32[128,1,1024]{2,1,0:T(1,128)}), f32[128,1,1024]{2,1,0:T(1,128)S(1)}, u32[]{:S(2)}, u32[]{:S(2)}) async-start(f32[128,1,1024]{2,1,0:T(1,128)} %param.9), calls=%async_computation | async-start | bytes 1048576 | tf_op jit(solution)/shard_map/all_to_all | solution.py:260
  12.1 0.1 copy.19
  12.2 0.1 sub.43
  12.3 0.1 copy.21.limit_ref
  12.4 0.1 copy.27.limit_ref
  12.5 1.0 %fusion.74 = bf16[256,256]{1,0:T(8,128)(2,1)S(1)} fusion(), kind=kLoop, calls=%fused_computation.63 | loop fusion | flops 1179648 | bytes 131072 | tf_op jit(solution)/shard_map/neg | solution.py:105
  13.5 1.0 %cosine_convert_fusion = bf16[256,256]{1,0:T(8,128)(2,1)S(1)} fusion(), kind=kLoop, calls=%fused_computation.59 | loop fusion | flops 983040 | bytes 131072 | tf_op jit(solution)/shard_map/convert_element_type | solution.py:105
  14.5 0.1 iota_add_fusion
  14.6 0.1 broadcast_subtract_fusion
  14.7 14.4 %all-to-all-done = f32[128,1,1024]{2,1,0:T(1,128)S(1)} async-done(((f32[128,1,1024]{2,1,0:T(1,128)}), f32[128,1,1024]{2,1,0:T(1,128)S(1)}, u32[]{:S(2)}, u32[]{:S(2)}) %all-to-all-start) | async-done | bytes 524320 | tf_op jit(solution)/shard_map/all_to_all | solution.py:260
  29.1 1.2 %reduce = f32[128,1024]{1,0:T(8,128)S(1)} reduce(f32[128,1,1024]{2,1,0:T(1,128)S(1)} %all-to-all-done, f32[]{:T(128)} %constant.44), dimensions={1}, to_apply=%all_to_all.15.reduce_sub_computation | reduce | bytes 1048580 | tf_op jit(solution)/shard_map/all_to_all | solution.py:260
  30.3 0.1 all_to_all.16
  30.5 0.2 all_to_all.18
  30.7 2.3 %collective-permute-start = (bf16[4,32,128]{2,0,1:T(4,128)(2,1)S(1)}, bf16[4,32,128]{2,0,1:T(4,128)(2,1)S(1)}, u32[]{:S(2)}, u32[]{:S(2)}) collective-permute-start(bf16[4,32,128]{2,0,1:T(4,128)(2,1)S(1)} %slice.46), channel_id=1, source_target_pairs={{1,0},{2,1},{3,2},{4,3},{5,4},{6,5},{7,6},{9,8},{10,9},{11,10},{12... | collective-permute-start | bytes 98312 | tf_op jit(solution)/shard_map/ppermute | solution.py:26
  33.0 0.9 %fusion.31 = f32[4,32,2,8,128]{4,3,0,2,1:T(8,128)S(1)} fusion(s32[32,2,128]{2,1,0:T(2,128)S(1)} %iota_add_fusion, s32[128]{0:T(128)S(1)} %iota_add_fusion.1, f32[4,32,8,128]{3,2,0,1:T(8,128)S(1)} %all_to_all.18), kind=kOutput, calls=%fused_computation.31 | convolution fusion | flops 68288512 | bytes 1606144 | tf_op jit(solution)/shard_map/rena,ekai->rekni/dot_general | solution.py:83
  33.9 0.1 slice.32
  34.1 1.3 %collective-permute-done = bf16[4,32,128]{2,0,1:T(4,128)(2,1)S(1)} collective-permute-done((bf16[4,32,128]{2,0,1:T(4,128)(2,1)S(1)}, bf16[4,32,128]{2,0,1:T(4,128)(2,1)S(1)}, u32[]{:S(2)}, u32[]{:S(2)}) %collective-permute-start) | collective-permute-done | bytes 32800 | tf_op jit(solution)/shard_map/ppermute | solution.py:26
  35.4 0.8 fusion.2
  36.2 1.0 %fusion.51 = bf16[4,32,2,8,128]{4,3,0,2,1:T(8,128)(2,1)S(1)} fusion(s32[32,2,128]{2,1,0:T(2,128)S(1)} %iota_add_fusion, f32[4,32,2,1,128]{4,3,0,2,1:T(1,128)S(1)} %bitcast.151, f32[4,32,2,7,128]{4,3,0,2,1:T(8,128)S(1)} %slice.32, f32[4,32,8,128]{3,2,0,1:T(8,128)S(1)} %all_to_all.18), kind=kOutput, calls=%fused_computation.39 | convolution fusion | flops 69337088 | bytes 2129920 | tf_op jit(solution)/shard_map/rena,ekai->rekni/dot_general | solution.py:82
  37.2 0.0 copy-start
  37.2 0.0 copy-start.2
  37.3 0.0 copy-start.3
  37.3 0.0 copy-start.4
  37.3 0.0 copy-start.5
  37.3 0.1 reshape.110
  37.4 0.2 copy.36.u_ref
  37.6 0.8 copy-done
  38.4 3.0 %shard_map.91 = bf16[4,64,1024]{2,1,0:T(8,128)(2,1)S(1)} custom-call(bf16[4,64,1024]{2,1,0:T(8,128)(2,1)S(1)} %copy.36.u_ref, bf16[256,512]{1,0:T(8,128)(2,1)S(1)} %pad_maximum_fusion.forward_ref, bf16[1536,256]{1,0:T(8,128)(2,1)S(1)} %copy-done, bf16[128,128]{1,0:T(8,128)(2,1)S(1)} %copy-done.2, bf16[128,128]{1,0:T(8,128)(2,1)S(1)} %copy-done.3, ...), custom_call_target="tpu_custom_call" | custom-call | tf_op jit(solution)/shard_map/pallas_call | solution.py:179
  41.4 0.1 copy.39
  41.5 3.4 %collective-permute-start.1 = (bf16[4,64,128]{2,1,0:T(8,128)(2,1)S(1)}, bf16[4,64,128]{2,1,0:T(8,128)(2,1)S(1)}, u32[]{:S(2)}, u32[]{:S(2)}) collective-permute-start(bf16[4,64,128]{2,1,0:T(8,128)(2,1)S(1)} %slice.34), channel_id=1, source_target_pairs={{0,1},{1,2},{2,3},{3,4},{4,5},{5,6},{6,7},{8,9},{9,10},{10,11},{11... | collective-permute-start | bytes 196616 | tf_op jit(solution)/shard_map/ppermute | solution.py:26
  44.9 0.8 bitcast_reduce_fusion.1
  45.6 0.8 bitcast_reduce_fusion
  46.4 1.0 %collective-permute-done.1 = bf16[4,64,128]{2,1,0:T(8,128)(2,1)S(1)} collective-permute-done((bf16[4,64,128]{2,1,0:T(8,128)(2,1)S(1)}, bf16[4,64,128]{2,1,0:T(8,128)(2,1)S(1)}, u32[]{:S(2)}, u32[]{:S(2)}) %collective-permute-start.1) | collective-permute-done | bytes 65568 | tf_op jit(solution)/shard_map/ppermute | solution.py:26
  47.4 0.8 bitcast_reduce_fusion.2
  48.2 0.9 %fusion.68 = (bf16[4,32,8,128,1]{3,2,0,4,1:T(8,128)(2,1)}, f32[4,32,8,128]{3,2,0,1:T(8,128)S(1)}) fusion(f32[4,32,8,128]{3,2,0,1:T(8,128)S(1)} %all_to_all.18, f32[4,32,8,128]{3,2,0,1:T(8,128)S(1)} %bitcast_reduce_fusion.1, f32[4,32,7,128]{3,2,0,1:T(8,128)S(1)} %bitcast.146, f32[4,32,1,128]{3,2,0,1:T(1,128)S(1)} %bitcast.149), kind=kLoop, calls=%fused_computation.54 | loop fusion | flops 524288 | bytes 2359296 | tf_op jit(solution)/shard_map/convert_element_type | solution.py:267
  49.1 0.2 add.89
  49.3 2.3 %collective-permute-start.2 = (bf16[4,32,128]{2,0,1:T(4,128)(2,1)S(1)}, bf16[4,32,128]{2,0,1:T(4,128)(2,1)S(1)}, u32[]{:S(2)}, u32[]{:S(2)}) collective-permute-start(bf16[4,32,128]{2,0,1:T(4,128)(2,1)S(1)} %fusion.77), channel_id=1, source_target_pairs={{1,0},{2,1},{3,2},{4,3},{5,4},{6,5},{7,6},{9,8},{10,9},{11,10},{12... | collective-permute-start | bytes 98312 | tf_op jit(solution)/shard_map/ppermute | solution.py:26
  51.6 1.8 %fusion.32 = f32[4,32,2,8,128]{4,3,0,2,1:T(8,128)S(1)} fusion(bf16[4,32,8,128,1]{3,2,0,4,1:T(8,128)(2,1)} %get-tuple-element.5, s32[32,2,128]{2,1,0:T(2,128)S(1)} %iota_add_fusion, s32[128]{0:T(128)S(1)} %iota_add_fusion.1), kind=kOutput, calls=%fused_computation.32 | convolution fusion | flops 68157440 | bytes 1344000 | tf_op jit(solution)/shard_map/rena,ekai->rekni/dot_general | solution.py:83
  53.4 0.2 slice.36
  53.6 0.4 collective-permute-done.2
  54.0 0.8 fusion
  54.8 1.9 %fusion.42 = f32[4,32,2,8,128]{4,3,0,2,1:T(8,128)} fusion(bf16[4,32,8,128,1]{3,2,0,4,1:T(8,128)(2,1)S(1)} %copy-done.6, s32[32,2,128]{2,1,0:T(2,128)S(1)} %iota_add_fusion, f32[4,32,2,1,128]{4,3,0,2,1:T(1,128)S(1)} %bitcast.150, f32[4,32,2,7,128]{4,3,0,2,1:T(8,128)S(1)} %slice.36), kind=kOutput, calls=%fused_computation.36 | convolution fusion | flops 68943872 | bytes 2392064 | tf_op jit(solution)/shard_map/rena,ekai->rekni/dot_general | solution.py:82
  56.7 1.6 %reshape.111 = f32[4,64,1024]{2,0,1:T(4,128)S(1)} reshape(f32[4,32,2,8,128]{4,3,0,2,1:T(8,128)} %fusion.42) | data formatting | bytes 2097152 | tf_op jit(solution)/shard_map/mul | solution.py:268
  58.2 0.7 fusion.54.u_ref
  58.9 3.0 %shard_map.92.src_ref = bf16[4,64,1024]{2,1,0:T(8,128)(2,1)S(1)} custom-call(bf16[4,64,1024]{2,1,0:T(8,128)(2,1)S(1)} %fusion.54.u_ref, bf16[256,512]{1,0:T(8,128)(2,1)S(1)} %pad_maximum_fusion.forward_ref, bf16[1536,256]{1,0:T(8,128)(2,1)S(1)} %copy-done, bf16[128,128]{1,0:T(8,128)(2,1)S(1)} %copy-done.2, bf16[128,128]{1,0:T(8,128)(2,1)S(1)} %copy-done.3, ...), custom_call_target="tpu_custom_call" | custom-call | tf_op jit(solution)/shard_map/pallas_call | solution.py:179
  61.9 0.8 copy-done.1
  62.7 23.6 %shard_map.93 = bf16[128,2,1024]{2,1,0:T(2,128)(2,1)} custom-call(bf16[4,64,1024]{2,1,0:T(8,128)(2,1)} %copy-done.1), custom_call_target="tpu_custom_call" | custom-call | tf_op jit(solution)/shard_map/pallas_call | solution.py:232
  86.3 2.2 %copy.56 = bf16[128,2,1024]{2,1,0:T(2,128)(2,1)} copy(bf16[128,2,1024]{2,1,0:T(2,128)(2,1)} %shard_map.93) | data formatting | bytes 1048576
  (17 shorter events, 0.1 us)
Async XLA Ops:
  0.0 12.1 %copy-start.8 = (f32[2,64]{1,0:T(2,128)S(1)}, f32[2,64]{1,0:T(2,128)}, u32[]{:S(2)}) copy-start(f32[2,64]{1,0:T(2,128)} %param.11) | copy-start | bytes 1540
  0.0 12.1 %copy-start.7 = (s32[32,2]{0,1:T(2,128)S(1)}, s32[32,2]{0,1:T(2,128)}, u32[]{:S(2)}) copy-start(s32[32,2]{0,1:T(2,128)} %param.10) | copy-start | bytes 772
  0.0 29.1 %all-to-all-start = ((f32[128,1,1024]{2,1,0:T(1,128)}), f32[128,1,1024]{2,1,0:T(1,128)S(1)}, u32[]{:S(2)}, u32[]{:S(2)}) async-start(f32[128,1,1024]{2,1,0:T(1,128)} %param.9), calls=%async_computation | async-start | bytes 1048576 | tf_op jit(solution)/shard_map/all_to_all | solution.py:260
  30.7 4.7 %collective-permute-start = (bf16[4,32,128]{2,0,1:T(4,128)(2,1)S(1)}, bf16[4,32,128]{2,0,1:T(4,128)(2,1)S(1)}, u32[]{:S(2)}, u32[]{:S(2)}) collective-permute-start(bf16[4,32,128]{2,0,1:T(4,128)(2,1)S(1)} %slice.46), channel_id=1, source_target_pairs={{1,0},{2,1},{3,2},{4,3},{5,4},{6,5},{7,6},{9,8},{10,9},{11,10},{12... | collective-permute-start | bytes 98312 | tf_op jit(solution)/shard_map/ppermute | solution.py:26
  37.2 1.1 %copy-start = (bf16[1536,256]{1,0:T(8,128)(2,1)S(1)}, bf16[1536,256]{1,0:T(8,128)(2,1)}, u32[]{:S(2)}) copy-start(bf16[1536,256]{1,0:T(8,128)(2,1)} %constant.43.inverse_ref) | copy-start | bytes 2359300
  37.2 1.1 %copy-start.2 = (bf16[128,128]{1,0:T(8,128)(2,1)S(1)}, bf16[128,128]{1,0:T(8,128)(2,1)}, u32[]{:S(2)}) copy-start(bf16[128,128]{1,0:T(8,128)(2,1)} %constant.38.clone.mfh_ref) | copy-start | bytes 98308
  37.3 1.1 %copy-start.3 = (bf16[128,128]{1,0:T(8,128)(2,1)S(1)}, bf16[128,128]{1,0:T(8,128)(2,1)}, u32[]{:S(2)}) copy-start(bf16[128,128]{1,0:T(8,128)(2,1)} %constant.39.clone.mfl_ref) | copy-start | bytes 98308
  37.3 1.1 %copy-start.4 = (bf16[128,128]{1,0:T(8,128)(2,1)S(1)}, bf16[128,128]{1,0:T(8,128)(2,1)}, u32[]{:S(2)}) copy-start(bf16[128,128]{1,0:T(8,128)(2,1)} %constant.40.clone.mih_ref) | copy-start | bytes 98308
  37.3 1.1 %copy-start.5 = (bf16[128,128]{1,0:T(8,128)(2,1)S(1)}, bf16[128,128]{1,0:T(8,128)(2,1)}, u32[]{:S(2)}) copy-start(bf16[128,128]{1,0:T(8,128)(2,1)} %constant.41.clone.mil_ref) | copy-start | bytes 98308
  41.5 5.9 %collective-permute-start.1 = (bf16[4,64,128]{2,1,0:T(8,128)(2,1)S(1)}, bf16[4,64,128]{2,1,0:T(8,128)(2,1)S(1)}, u32[]{:S(2)}, u32[]{:S(2)}) collective-permute-start(bf16[4,64,128]{2,1,0:T(8,128)(2,1)S(1)} %slice.34), channel_id=1, source_target_pairs={{0,1},{1,2},{2,3},{3,4},{4,5},{5,6},{6,7},{8,9},{9,10},{10,11},{11... | collective-permute-start | bytes 196616 | tf_op jit(solution)/shard_map/ppermute | solution.py:26
  49.3 4.7 %collective-permute-start.2 = (bf16[4,32,128]{2,0,1:T(4,128)(2,1)S(1)}, bf16[4,32,128]{2,0,1:T(4,128)(2,1)S(1)}, u32[]{:S(2)}, u32[]{:S(2)}) collective-permute-start(bf16[4,32,128]{2,0,1:T(4,128)(2,1)S(1)} %fusion.77), channel_id=1, source_target_pairs={{1,0},{2,1},{3,2},{4,3},{5,4},{6,5},{7,6},{9,8},{10,9},{11,10},{12... | collective-permute-start | bytes 98312 | tf_op jit(solution)/shard_map/ppermute | solution.py:26
  53.6 1.2 %copy-start.6 = (bf16[4,32,8,128,1]{3,2,0,4,1:T(8,128)(2,1)S(1)}, bf16[4,32,8,128,1]{3,2,0,4,1:T(8,128)(2,1)}, u32[]{:S(2)}) copy-start(bf16[4,32,8,128,1]{3,2,0,4,1:T(8,128)(2,1)} %get-tuple-element.5) | copy-start | bytes 786436
  61.9 0.8 copy-start.1

commit v4 on v3

--- a/solution.py
+++ b/solution.py
@@ -226,7 +226,7 @@
     own.wait()
 
 
-def exchange(value, out_shape, outgoing, incoming):
+def exchange(value, out_shape, outgoing, incoming, tag):
     count = lax.axis_size("shot")
     anywhere = pl.BlockSpec(memory_space=pl.ANY)
     return pl.pallas_call(
@@ -239,7 +239,7 @@
             pltpu.SemaphoreType.DMA((count,)),
             pltpu.SemaphoreType.DMA,
         ],
-        compiler_params=pltpu.CompilerParams(collective_id=0, has_side_effects=True),
+        compiler_params=pltpu.CompilerParams(collective_id=tag, has_side_effects=True),
     )(value)
 
 
@@ -252,12 +252,26 @@
         (receivers * count, own, samples),
         lambda peer: (slice(None), pl.ds(peer * own, own), slice(None)),
         lambda sender: (pl.ds(sender * receivers, receivers), slice(None), slice(None)),
+        0,
+    )
+
+
+def to_receivers(records):
+    receivers, own, samples = records.shape
+    count = lax.axis_size("shot")
+    part = receivers // count
+    return exchange(
+        records,
+        (part, own * count, samples),
+        lambda peer: (pl.ds(peer * part, part), slice(None), slice(None)),
+        lambda sender: (slice(None), pl.ds(sender * own, own), slice(None)),
+        1,
     )
 
 
 def local(blended, delays, thresholds):
     tables = filter_tables()
-    records = lax.all_to_all(blended, "shot", split_axis=0, concat_axis=1, tiled=True)
+    records = to_receivers(blended)
     estimate = None
     for sweep in range(ITERS):
         if sweep == 0:

time: 89.9 us -> 85.8 us (0.954)
  Pallas kernels: 29.5 us -> 53.4 us
  waiting for transfers between devices: 17.1 us -> 3.54 us
  starting transfers between devices: 20 us -> 7.38 us
  matrix products: 9.56 us -> 8.37 us
    pallas_call x1 -> x2, Pallas kernels: 23.6 us -> 47.5 us  [exchange(): pl.pallas_call(functools.partial(exchange_kernel, count, outgoing, incomi...]
    all_to_all x1 -> x0, waiting for transfers between devices: 14.4 us -> none  [local(): lax.all_to_all(blended, 'shot', split_axis=0, concat_axis=1, tiled=True)]
    all_to_all x1 -> x0, starting transfers between devices: 12.1 us -> none  [local(): lax.all_to_all(blended, 'shot', split_axis=0, concat_axis=1, tiled=True)]
    all_to_all x1 -> x0, other arithmetic: 1.24 us -> none  [local(): lax.all_to_all(blended, 'shot', split_axis=0, concat_axis=1, tiled=True)]
    convert_element_type x0 -> x1, other arithmetic: none -> 1.08 us  [local(): residual = records.astype(jnp.bfloat16)]
    dot_general x2, matrix products: 2.69 us -> 1.63 us  [spread(): jnp.einsum('rena,ekai->rekni', lower, select_next, preferred_element_type...]
    unnamed x21 -> x23, local copies, waits for them, and re-layouts: 3.99 us -> 4.78 us
  transfers between devices with their start and end apart: 4 -> 3, of which waited for: 4 -> 2; matrix products, arithmetic and copies ran while one was open for 8% -> 7% of each run, Pallas kernels for 0% -> 0%
where the time goes in v4:
time: 85.8 us; the launch traced here: 84.8 us
  Pallas kernels  53.4 us (62%)
  matrix products  8.37 us (10%)
  local copies, waits for them, and re-layouts  7.46 us (9%)
  starting transfers between devices  7.38 us (9%)
  other arithmetic  4.37 us (5%)
  waiting for transfers between devices  3.54 us (4%)
    pallas_call x2, Pallas kernels, exchange(): pl.pallas_call(functools.partial(exchange_kernel, count, outgoing, incomi...  47.5 us
    ppermute x3, starting transfers between devices, shifted(): return lax.ppermute(array, axis, pairs)  7.38 us
    pallas_call x2, Pallas kernels, coherence(): pl.pallas_call(filter_kernel, in_specs=[vmem] * 8, out_specs=vmem, out_sh...  5.92 us
    unnamed x23, local copies, waits for them, and re-layouts  4.78 us
    ppermute x3, waiting for transfers between devices, shifted(): return lax.ppermute(array, axis, pairs)  3.54 us
    dot_general x2, matrix products, spread(): jnp.einsum('rena,ekai->rekni', lower, select_same, preferred_element_type...  2.81 us
  transfers between devices with their start and end apart: 3, of which 2 were waited for; matrix products, arithmetic and copies ran while one was open for 7% of the time, Pallas kernels for 0%

profile of v4, /device:TPU:3, one launch (start us, length us, event | category | flops | bytes accessed | tf_op | source)
XLA Modules:
  0.0 84.8 jit_solution(17632117282356919385)
XLA Ops:
  0.0 24.1 %shard_map.91 = f32[4,32,1024]{2,1,0:T(8,128)} custom-call(f32[128,1,1024]{2,1,0:T(1,128)} %src_ref.1), custom_call_target="tpu_custom_call" | custom-call | tf_op jit(solution)/shard_map/pallas_call | solution.py:232
  24.1 0.0 copy-start.8
  24.1 1.1 %convert_element_type.34 = bf16[4,32,1024]{2,1,0:T(8,128)(2,1)S(1)} convert(f32[4,32,1024]{2,1,0:T(8,128)} %shard_map.91) | non-fusion elementwise | flops 131072 | bytes 786432 | tf_op jit(solution)/shard_map/convert_element_type | solution.py:278
  25.2 3.0 %collective-permute-start = (bf16[4,32,128]{2,1,0:T(8,128)(2,1)S(1)}, bf16[4,32,128]{2,1,0:T(8,128)(2,1)S(1)}, u32[]{:S(2)}, u32[]{:S(2)}) collective-permute-start(bf16[4,32,128]{2,1,0:T(8,128)(2,1)S(1)} %slice.33), channel_id=1, source_target_pairs={{1,0},{2,1},{3,2},{4,3},{5,4},{6,5},{7,6},{9,8},{10,9},{11,10},{12... | collective-permute-start | bytes 98312 | tf_op jit(solution)/shard_map/ppermute | solution.py:26
  28.2 0.1 copy.40
  28.3 0.1 iota_add_fusion
  28.4 0.1 sub.40
  28.5 1.0 %fusion.76 = bf16[256,256]{1,0:T(8,128)(2,1)S(1)} fusion(), kind=kLoop, calls=%fused_computation.67 | loop fusion | flops 1179648 | bytes 131072 | tf_op jit(solution)/shard_map/neg | solution.py:105
  29.5 1.0 %cosine_convert_fusion = bf16[256,256]{1,0:T(8,128)(2,1)S(1)} fusion(), kind=kLoop, calls=%fused_computation.59 | loop fusion | flops 983040 | bytes 131072 | tf_op jit(solution)/shard_map/convert_element_type | solution.py:105
  30.6 0.1 broadcast_subtract_fusion
  30.7 0.8 fusion.31
  31.5 0.1 slice.32
  31.7 0.1 copy.45.limit_ref
  31.8 0.1 copy.55.limit_ref
  31.9 0.8 fusion.2
  32.6 0.9 %fusion.51 = bf16[4,32,2,8,128]{4,3,0,2,1:T(8,128)(2,1)S(1)} fusion(s32[32,2,128]{2,1,0:T(2,128)S(1)} %iota_add_fusion, f32[4,32,2,1,128]{4,3,0,2,1:T(1,128)S(1)} %bitcast.174, f32[4,32,2,7,128]{4,3,0,2,1:T(8,128)S(1)} %slice.32, bf16[4,32,8,128]{3,2,1,0:T(8,128)(2,1)S(1)} %bitcast.167), kind=kOutput, calls=%fused_computation.39 | convolution fusion | flops 69206016 | bytes 1867776 | tf_op jit(solution)/shard_map/rena,ekai->rekni/dot_general | solution.py:82
  33.6 0.0 copy-start
  33.6 0.0 copy-start.2
  33.6 0.0 copy-start.3
  33.6 0.0 copy-start.4
  33.6 0.0 copy-start.5
  33.6 0.1 reshape.116
  33.8 0.2 copy.72.u_ref
  33.9 0.8 copy-done
  34.7 3.0 %shard_map.92 = bf16[4,64,1024]{2,1,0:T(8,128)(2,1)S(1)} custom-call(bf16[4,64,1024]{2,1,0:T(8,128)(2,1)S(1)} %copy.72.u_ref, bf16[256,512]{1,0:T(8,128)(2,1)S(1)} %pad_maximum_fusion.forward_ref, bf16[1536,256]{1,0:T(8,128)(2,1)S(1)} %copy-done, bf16[128,128]{1,0:T(8,128)(2,1)S(1)} %copy-done.2, bf16[128,128]{1,0:T(8,128)(2,1)S(1)} %copy-done.3, ...), custom_call_target="tpu_custom_call" | custom-call | tf_op jit(solution)/shard_map/pallas_call | solution.py:179
  37.7 0.1 copy.82
  37.8 2.3 %collective-permute-start.1 = (bf16[4,64,128]{2,1,0:T(8,128)(2,1)S(1)}, bf16[4,64,128]{2,1,0:T(8,128)(2,1)S(1)}, u32[]{:S(2)}, u32[]{:S(2)}) collective-permute-start(bf16[4,64,128]{2,1,0:T(8,128)(2,1)S(1)} %slice.34), channel_id=1, source_target_pairs={{0,1},{1,2},{2,3},{3,4},{4,5},{5,6},{6,7},{8,9},{9,10},{10,11},{11... | collective-permute-start | bytes 196616 | tf_op jit(solution)/shard_map/ppermute | solution.py:26
  40.1 0.8 bitcast_reduce_fusion.1
  40.9 0.8 bitcast_reduce_fusion
  41.7 2.0 %collective-permute-done.1 = bf16[4,64,128]{2,1,0:T(8,128)(2,1)S(1)} collective-permute-done((bf16[4,64,128]{2,1,0:T(8,128)(2,1)S(1)}, bf16[4,64,128]{2,1,0:T(8,128)(2,1)S(1)}, u32[]{:S(2)}, u32[]{:S(2)}) %collective-permute-start.1) | collective-permute-done | bytes 65568 | tf_op jit(solution)/shard_map/ppermute | solution.py:26
  43.7 0.8 bitcast_reduce_fusion.2
  44.5 0.1 maximum_add_fusion
  44.7 0.2 reshape.117
  44.9 0.7 copy-done.6
  45.6 0.3 fusion.55
  45.9 2.1 %collective-permute-start.2 = (bf16[4,32,128]{2,1,0:T(8,128)(2,1)S(1)}, bf16[4,32,128]{2,1,0:T(8,128)(2,1)S(1)}, u32[]{:S(2)}, u32[]{:S(2)}) collective-permute-start(bf16[4,32,128]{2,1,0:T(8,128)(2,1)S(1)} %slice.37), channel_id=1, source_target_pairs={{1,0},{2,1},{3,2},{4,3},{5,4},{6,5},{7,6},{9,8},{10,9},{11,10},{12... | collective-permute-start | bytes 98312 | tf_op jit(solution)/shard_map/ppermute | solution.py:26
  48.1 0.8 fusion.32
  48.9 0.2 slice.36
  49.1 1.5 %collective-permute-done.2 = bf16[4,32,128]{2,1,0:T(8,128)(2,1)S(1)} collective-permute-done((bf16[4,32,128]{2,1,0:T(8,128)(2,1)S(1)}, bf16[4,32,128]{2,1,0:T(8,128)(2,1)S(1)}, u32[]{:S(2)}, u32[]{:S(2)}) %collective-permute-start.2) | collective-permute-done | bytes 32800 | tf_op jit(solution)/shard_map/ppermute | solution.py:26
  50.6 0.8 fusion
  51.4 1.9 %fusion.42 = f32[4,32,2,8,128]{4,3,0,2,1:T(8,128)} fusion(s32[32,2,128]{2,1,0:T(2,128)S(1)} %iota_add_fusion, f32[4,32,2,1,128]{4,3,0,2,1:T(1,128)S(1)} %bitcast.173, f32[4,32,2,7,128]{4,3,0,2,1:T(8,128)S(1)} %slice.36, bf16[4,32,8,128]{3,2,1,0:T(8,128)(2,1)S(1)} %bitcast.169), kind=kOutput, calls=%fused_computation.36 | convolution fusion | flops 68943872 | bytes 2392064 | tf_op jit(solution)/shard_map/rena,ekai->rekni/dot_general | solution.py:82
  53.3 1.6 %reshape.118 = f32[4,64,1024]{2,0,1:T(4,128)S(1)} reshape(f32[4,32,2,8,128]{4,3,0,2,1:T(8,128)} %fusion.42) | data formatting | bytes 2097152 | tf_op jit(solution)/shard_map/mul | solution.py:282
  54.8 0.7 fusion.54.u_ref
  55.5 3.0 %shard_map.93.src_ref = bf16[4,64,1024]{2,1,0:T(8,128)(2,1)S(1)} custom-call(bf16[4,64,1024]{2,1,0:T(8,128)(2,1)S(1)} %fusion.54.u_ref, bf16[256,512]{1,0:T(8,128)(2,1)S(1)} %pad_maximum_fusion.forward_ref, bf16[1536,256]{1,0:T(8,128)(2,1)S(1)} %copy-done, bf16[128,128]{1,0:T(8,128)(2,1)S(1)} %copy-done.2, bf16[128,128]{1,0:T(8,128)(2,1)S(1)} %copy-done.3, ...), custom_call_target="tpu_custom_call" | custom-call | tf_op jit(solution)/shard_map/pallas_call | solution.py:179
  58.5 0.0 copy-start.1
  58.5 0.8 copy-done.1
  59.3 23.3 %shard_map.94 = bf16[128,2,1024]{2,1,0:T(2,128)(2,1)} custom-call(bf16[4,64,1024]{2,1,0:T(8,128)(2,1)} %copy-done.1), custom_call_target="tpu_custom_call" | custom-call | tf_op jit(solution)/shard_map/pallas_call | solution.py:232
  82.6 2.2 %copy.115 = bf16[128,2,1024]{2,1,0:T(2,128)(2,1)} copy(bf16[128,2,1024]{2,1,0:T(2,128)(2,1)} %shard_map.94) | data formatting | bytes 1048576
  (17 shorter events, 0.2 us)
Async XLA Ops:
  0.0 28.2 %copy-start.7 = (s32[32,2]{0,1:T(2,128)S(1)}, s32[32,2]{0,1:T(2,128)}, u32[]{:S(2)}) copy-start(s32[32,2]{0,1:T(2,128)} %param.10) | copy-start | bytes 772
  24.1 6.4 %copy-start.8 = (f32[2,64]{1,0:T(2,128)S(1)}, f32[2,64]{1,0:T(2,128)}, u32[]{:S(2)}) copy-start(f32[2,64]{1,0:T(2,128)} %param.11) | copy-start | bytes 1540
  25.2 6.6 %collective-permute-start = (bf16[4,32,128]{2,1,0:T(8,128)(2,1)S(1)}, bf16[4,32,128]{2,1,0:T(8,128)(2,1)S(1)}, u32[]{:S(2)}, u32[]{:S(2)}) collective-permute-start(bf16[4,32,128]{2,1,0:T(8,128)(2,1)S(1)} %slice.33), channel_id=1, source_target_pairs={{1,0},{2,1},{3,2},{4,3},{5,4},{6,5},{7,6},{9,8},{10,9},{11,10},{12... | collective-permute-start | bytes 98312 | tf_op jit(solution)/shard_map/ppermute | solution.py:26
  33.6 1.1 %copy-start = (bf16[1536,256]{1,0:T(8,128)(2,1)S(1)}, bf16[1536,256]{1,0:T(8,128)(2,1)}, u32[]{:S(2)}) copy-start(bf16[1536,256]{1,0:T(8,128)(2,1)} %constant.43.inverse_ref) | copy-start | bytes 2359300
  33.6 1.1 %copy-start.2 = (bf16[128,128]{1,0:T(8,128)(2,1)S(1)}, bf16[128,128]{1,0:T(8,128)(2,1)}, u32[]{:S(2)}) copy-start(bf16[128,128]{1,0:T(8,128)(2,1)} %constant.38.clone.mfh_ref) | copy-start | bytes 98308
  33.6 1.1 %copy-start.3 = (bf16[128,128]{1,0:T(8,128)(2,1)S(1)}, bf16[128,128]{1,0:T(8,128)(2,1)}, u32[]{:S(2)}) copy-start(bf16[128,128]{1,0:T(8,128)(2,1)} %constant.39.clone.mfl_ref) | copy-start | bytes 98308
  33.6 1.1 %copy-start.4 = (bf16[128,128]{1,0:T(8,128)(2,1)S(1)}, bf16[128,128]{1,0:T(8,128)(2,1)}, u32[]{:S(2)}) copy-start(bf16[128,128]{1,0:T(8,128)(2,1)} %constant.40.clone.mih_ref) | copy-start | bytes 98308
  33.6 1.1 %copy-start.5 = (bf16[128,128]{1,0:T(8,128)(2,1)S(1)}, bf16[128,128]{1,0:T(8,128)(2,1)}, u32[]{:S(2)}) copy-start(bf16[128,128]{1,0:T(8,128)(2,1)} %constant.41.clone.mil_ref) | copy-start | bytes 98308
  37.8 5.9 %collective-permute-start.1 = (bf16[4,64,128]{2,1,0:T(8,128)(2,1)S(1)}, bf16[4,64,128]{2,1,0:T(8,128)(2,1)S(1)}, u32[]{:S(2)}, u32[]{:S(2)}) collective-permute-start(bf16[4,64,128]{2,1,0:T(8,128)(2,1)S(1)} %slice.34), channel_id=1, source_target_pairs={{0,1},{1,2},{2,3},{3,4},{4,5},{5,6},{6,7},{8,9},{9,10},{10,11},{11... | collective-permute-start | bytes 196616 | tf_op jit(solution)/shard_map/ppermute | solution.py:26
  44.5 1.0 %copy-start.6 = (f32[4,32,1024]{2,1,0:T(8,128)S(1)}, f32[4,32,1024]{2,1,0:T(8,128)}, u32[]{:S(2)}) copy-start(f32[4,32,1024]{2,1,0:T(8,128)} %shard_map.91) | copy-start | bytes 1572868
  45.9 4.7 %collective-permute-start.2 = (bf16[4,32,128]{2,1,0:T(8,128)(2,1)S(1)}, bf16[4,32,128]{2,1,0:T(8,128)(2,1)S(1)}, u32[]{:S(2)}, u32[]{:S(2)}) collective-permute-start(bf16[4,32,128]{2,1,0:T(8,128)(2,1)S(1)} %slice.37), channel_id=1, source_target_pairs={{1,0},{2,1},{3,2},{4,3},{5,4},{6,5},{7,6},{9,8},{10,9},{11,10},{12... | collective-permute-start | bytes 98312 | tf_op jit(solution)/shard_map/ppermute | solution.py:26
  58.5 0.8 copy-start.1

commit v5 on v4

--- a/solution.py
+++ b/solution.py
@@ -45,11 +45,10 @@
     return (cos_forward, sin_forward, cos_inverse, sin_inverse, cos_source, sin_source)
 
 
-def blend(estimate, own_delays):
+def blend(estimate, earlier, own_delays):
     receivers, sources, samples = estimate.shape
     blocks = samples // BLK
     experiments = sources // SRC_EXP
-    earlier = shifted(estimate[:, :, samples - BLK :], "tm", 1)
     upper = estimate.reshape(receivers, sources, blocks, BLK)
     shifts = own_delays.reshape(-1)
     row_index = jnp.arange(BLK, dtype=jnp.int32)[None, :, None]
@@ -68,10 +67,9 @@
     return (same + carried).reshape(receivers, experiments, samples)
 
 
-def spread(residual, own_delays):
+def spread(residual, later, own_delays):
     receivers, experiments, samples = residual.shape
     blocks = samples // BLK
-    later = shifted(residual[:, :, :BLK], "tm", -1)
     lower = residual.reshape(receivers, experiments, blocks, BLK)
     row_index = jnp.arange(BLK, dtype=jnp.int32)[None, None, :, None]
     column_index = jnp.arange(BLK, dtype=jnp.int32)[None, None, None, :]
@@ -100,13 +98,11 @@
 
 
 def filter_tables():
-    time_angle = phase_table(WIN, WIN, WIN)
-    forward = jnp.concatenate(
-        [jnp.cos(time_angle).astype(jnp.bfloat16), -jnp.sin(time_angle).astype(jnp.bfloat16)],
-        axis=1,
-    )
     turn = lambda n: (np.arange(n)[:, None] * np.arange(n)[None, :] % n) * (2.0 * np.pi / n)
     time_turn = turn(WIN)
+    forward = jnp.asarray(
+        np.concatenate([np.cos(time_turn), -np.sin(time_turn)], axis=1).astype(ml_dtypes.bfloat16)
+    )
     inverse_high, inverse_low = exact_split(
         np.concatenate([np.cos(time_turn), -np.sin(time_turn)], axis=0) / math.sqrt(WIN)
     )
@@ -272,17 +268,21 @@
 def local(blended, delays, thresholds):
     tables = filter_tables()
     records = to_receivers(blended)
-    estimate = None
-    for sweep in range(ITERS):
-        if sweep == 0:
-            residual = records.astype(jnp.bfloat16)
-            update = (RELAX * spread(residual, delays)).astype(jnp.bfloat16)
-        else:
-            residual = (records - blend(estimate, delays)).astype(jnp.bfloat16)
-            update = (estimate.astype(jnp.float32) + RELAX * spread(residual, delays)).astype(
-                jnp.bfloat16
-            )
-        estimate = coherence(update, thresholds[sweep], tables)
+    samples = records.shape[2]
+    following = shifted(records[:, :, :BLK], "tm", -1)
+    residual = records.astype(jnp.bfloat16)
+    update = (RELAX * spread(residual, following.astype(jnp.bfloat16), delays)).astype(jnp.bfloat16)
+    estimate = coherence(update, thresholds[0], tables)
+    before = shifted(estimate[:, :, samples - BLK :], "tm", 1)
+    after = shifted(estimate[:, :, :BLK], "tm", -1)
+    blended_part = blend(jnp.concatenate([estimate, after], axis=2), before, delays)
+    residual = (jnp.concatenate([records, following], axis=2) - blended_part).astype(jnp.bfloat16)
+    last = lax.axis_index("tm") == lax.axis_size("tm") - 1
+    tail = jnp.where(last, jnp.zeros_like(residual[:, :, samples:]), residual[:, :, samples:])
+    update = (
+        estimate.astype(jnp.float32) + RELAX * spread(residual[:, :, :samples], tail, delays)
+    ).astype(jnp.bfloat16)
+    estimate = coherence(update, thresholds[1], tables)
     return to_sources(estimate)
 
 

time: 85.8 us -> 87.4 us (1.019)
  waiting for transfers between devices: 3.54 us -> 0.72 us
  matrix products: 8.37 us -> 10.3 us
  local copies, waits for them, and re-layouts: 7.46 us -> 8.84 us
  starting transfers between devices: 7.38 us -> 8.4 us
    ppermute x3, waiting for transfers between devices: 3.54 us -> 0.72 us  [shifted(): return lax.ppermute(array, axis, pairs)]
    ppermute x3, starting transfers between devices: 7.38 us -> 8.4 us  [shifted(): return lax.ppermute(array, axis, pairs)]
    dot_general x1, matrix products: 0.77 us -> 1.76 us  [blend(): jnp.einsum('rsnb,sbi->rsni', upper, select_prior, preferred_element_type=...]
    neg x1 -> x0, other arithmetic: 0.99 us -> none  [filter_tables(): -jnp.sin(time_angle).astype(jnp.bfloat16)]
    unnamed x23 -> x30, local copies, waits for them, and re-layouts: 4.78 us -> 4.12 us
  transfers between devices with their start and end apart: 3 -> 3, of which waited for: 2 -> 1; matrix products, arithmetic and copies ran while one was open for 7% -> 7% of each run, Pallas kernels for 0% -> 0%
where the time goes in v5:
time: 87.4 us; the launch traced here: 86 us
  Pallas kernels  53.3 us (61%)
  matrix products  10.3 us (12%)
  local copies, waits for them, and re-layouts  8.84 us (10%)
  starting transfers between devices  8.4 us (10%)
  other arithmetic  3.96 us (5%)
    pallas_call x2, Pallas kernels, exchange(): pl.pallas_call(functools.partial(exchange_kernel, count, outgoing, incomi...  47.4 us
    ppermute x3, starting transfers between devices, shifted(): return lax.ppermute(array, axis, pairs)  8.4 us
    pallas_call x2, Pallas kernels, coherence(): pl.pallas_call(filter_kernel, in_specs=[vmem] * 8, out_specs=vmem, out_sh...  5.92 us
    unnamed x30, local copies, waits for them, and re-layouts  4.12 us
    dot_general x2, matrix products, spread(): jnp.einsum('rena,ekai->rekni', lower, select_same, preferred_element_type...  2.83 us
    dot_general x1, matrix products, blend(): jnp.einsum('rsnb,sbi->rsni', upper, select_prior, preferred_element_type=...  1.76 us
  transfers between devices with their start and end apart: 3, of which 1 were waited for; matrix products, arithmetic and copies ran while one was open for 7% of the time, Pallas kernels for 0%

profile of v5, /device:TPU:3, one launch (start us, length us, event | category | flops | bytes accessed | tf_op | source)
XLA Modules:
  0.0 86.0 jit_solution(16991835692577647687)
XLA Ops:
  0.0 24.1 %shard_map.100 = f32[4,32,1024]{2,1,0:T(8,128)} custom-call(f32[128,1,1024]{2,1,0:T(1,128)} %src_ref.1), custom_call_target="tpu_custom_call" | custom-call | tf_op jit(solution)/shard_map/pallas_call | solution.py:228
  24.1 0.8 slice.31
  25.0 2.9 %collective-permute-start = (f32[4,32,128]{2,1,0:T(8,128)S(1)}, f32[4,32,128]{2,1,0:T(8,128)S(1)}, u32[]{:S(2)}, u32[]{:S(2)}) collective-permute-start(f32[4,32,128]{2,1,0:T(8,128)S(1)} %slice.31), channel_id=1, source_target_pairs={{1,0},{2,1},{3,2},{4,3},{5,4},{6,5},{7,6},{9,8},{10,9},{11,10},{12... | collective-permute-start | bytes 196616 | tf_op jit(solution)/shard_map/ppermute | solution.py:26
  27.9 1.1 %convert_element_type.26 = bf16[4,32,1024]{2,1,0:T(8,128)(2,1)S(1)} convert(f32[4,32,1024]{2,1,0:T(8,128)} %shard_map.100) | non-fusion elementwise | flops 131072 | bytes 786432 | tf_op jit(solution)/shard_map/convert_element_type | solution.py:273
  29.0 0.1 copy.41
  29.1 0.1 iota_add_fusion
  29.3 0.8 fusion.31
  30.1 0.1 sub.40
  30.2 0.1 copy.46.limit_ref
  30.3 0.1 slice.40
  30.5 0.8 fusion.2
  31.3 0.9 %fusion.51 = bf16[4,32,2,8,128]{4,3,0,2,1:T(8,128)(2,1)S(1)} fusion(s32[32,2,128]{2,1,0:T(2,128)S(1)} %iota_add_fusion, f32[4,32,2,1,128]{4,3,0,2,1:T(1,128)S(1)} %bitcast.151, f32[4,32,2,7,128]{4,3,0,2,1:T(8,128)S(1)} %slice.40, bf16[4,32,8,128]{3,2,1,0:T(8,128)(2,1)S(1)} %bitcast.146), kind=kOutput, calls=%fused_computation.41 | convolution fusion | flops 69206016 | bytes 1867776 | tf_op jit(solution)/shard_map/rena,ekai->rekni/dot_general | solution.py:80
  32.2 0.0 copy-start
  32.3 0.0 copy-start.2
  32.3 0.0 copy-start.3
  32.3 0.0 copy-start.4
  32.3 0.0 copy-start.5
  32.3 0.0 copy-start.6
  32.3 0.1 reshape.116
  32.4 0.2 copy.73.u_ref
  32.6 0.8 copy-done
  33.4 0.1 copy-done.2
  33.4 3.0 %shard_map.101 = bf16[4,64,1024]{2,1,0:T(8,128)(2,1)S(1)} custom-call(bf16[4,64,1024]{2,1,0:T(8,128)(2,1)S(1)} %copy.73.u_ref, bf16[256,512]{1,0:T(8,128)(2,1)S(1)} %copy-done.2, bf16[1536,256]{1,0:T(8,128)(2,1)S(1)} %copy-done, bf16[128,128]{1,0:T(8,128)(2,1)S(1)} %copy-done.6, bf16[128,128]{1,0:T(8,128)(2,1)S(1)} %copy-done.5, ...), custom_call_target="tpu_custom_call" | custom-call | tf_op jit(solution)/shard_map/pallas_call | solution.py:175
  36.4 3.3 %collective-permute-start.1 = (bf16[4,64,128]{2,1,0:T(8,128)(2,1)S(1)}, bf16[4,64,128]{2,1,0:T(8,128)(2,1)S(1)}, u32[]{:S(2)}, u32[]{:S(2)}) collective-permute-start(bf16[4,64,128]{2,1,0:T(8,128)(2,1)S(1)} %get-tuple-element.6), channel_id=1, source_target_pairs={{1,0},{2,1},{3,2},{4,3},{5,4},{6,5},{7,6},{9,8},{10,9},{11,10},{12... | collective-permute-start | bytes 196616 | tf_op jit(solution)/shard_map/ppermute | solution.py:26
  39.8 0.7 broadcast_subtract_fusion
  40.5 0.1 copy.56.limit_ref
  40.6 2.1 %collective-permute-start.2 = (bf16[4,64,128]{2,1,0:T(8,128)(2,1)S(1)}, bf16[4,64,128]{2,1,0:T(8,128)(2,1)}, u32[]{:S(2)}, u32[]{:S(2)}) collective-permute-start(bf16[4,64,128]{2,1,0:T(8,128)(2,1)S(1)} %get-tuple-element.5), channel_id=1, source_target_pairs={{0,1},{1,2},{2,3},{3,4},{4,5},{5,6},{6,7},{8,9},{9,10},{10,11},{11... | collective-permute-start | bytes 196616 | tf_op jit(solution)/shard_map/ppermute | solution.py:26
  42.7 0.1 pad_maximum_fusion
  42.8 0.3 reshape.101
  43.1 1.8 %bitcast_reduce_fusion = f32[4,32,9,128]{3,2,0,1:T(8,128)S(1)} fusion(s32[64,128]{1,0:T(8,128)} %get-tuple-element.9, bf16[4,64,9,128]{3,2,1,0:T(8,128)(2,1)S(1)} %reshape.101), kind=kOutput, calls=%fused_computation.18 | convolution fusion | flops 76693504 | bytes 1212416 | tf_op jit(solution)/shard_map/rsnb,sbi->rsni/dot_general | solution.py:59
  44.9 0.9 %bitcast_reduce_fusion.1 = f32[4,32,9,128]{3,2,0,1:T(8,128)S(1)} fusion(s32[64,128]{1,0:T(8,128)S(1)} %copy-done.10, bf16[4,64,9,128]{3,2,1,0:T(8,128)(2,1)S(1)} %reshape.101), kind=kOutput, calls=%fused_computation.19 | convolution fusion | flops 76693504 | bytes 1212416 | tf_op jit(solution)/shard_map/rsnb,sbi->rsni/dot_general | solution.py:58
  45.8 0.0 copy-done.8
  45.9 0.7 collective-permute-done.2
  46.6 0.0 copy-done.9
  46.6 1.6 %bitcast_reduce_fusion.2 = f32[4,32,128]{2,0,1:T(4,128)S(1)} fusion(bf16[4,64,128]{2,1,0:T(8,128)(2,1)} %collective-permute-done.2, s32[64,128]{1,0:T(8,128)S(1)} %copy-done.9), kind=kOutput, calls=%fused_computation.56 | convolution fusion | flops 9453568 | bytes 163840 | tf_op jit(solution)/shard_map/rsb,sbi->rsi/dot_general | solution.py:60
  48.3 0.2 maximum_add_fusion
  48.5 1.0 %reshape.117 = f32[4,32,1152]{2,0,1:T(4,128)} reshape(f32[4,32,9,128]{3,2,0,1:T(8,128)S(1)} %maximum_add_fusion) | data formatting | bytes 1179648 | tf_op jit(solution)/shard_map/add | solution.py:67
  49.5 1.1 %fusion.61 = bf16[4,32,1152]{2,1,0:T(8,128)(2,1)S(1)} fusion(f32[4,32,128]{2,1,0:T(8,128)S(1)} %collective-permute-done, f32[4,32,1024]{2,1,0:T(8,128)S(1)} %copy-done.7, f32[4,32,1152]{2,0,1:T(4,128)} %reshape.117), kind=kLoop, calls=%fused_computation.48 | loop fusion | flops 442368 | bytes 1474560 | tf_op jit(solution)/shard_map/convert_element_type | solution.py:279
  50.8 0.8 fusion
  51.6 0.8 fusion.32
  52.4 0.2 slice.45
  52.6 1.9 %fusion.42 = f32[4,32,2,8,128]{4,3,0,2,1:T(8,128)} fusion(s32[32,2,128]{2,1,0:T(2,128)S(1)} %iota_add_fusion, f32[4,32,2,1,128]{4,3,0,2,1:T(1,128)S(1)} %bitcast.150, f32[4,32,2,7,128]{4,3,0,2,1:T(8,128)S(1)} %slice.45, bf16[4,32,8,128]{3,2,1,0:T(8,128)(2,1)S(1)} %bitcast.148), kind=kOutput, calls=%fused_computation.38 | convolution fusion | flops 68943872 | bytes 2392064 | tf_op jit(solution)/shard_map/rena,ekai->rekni/dot_general | solution.py:80
  54.5 1.6 %reshape.118 = f32[4,64,1024]{2,0,1:T(4,128)S(1)} reshape(f32[4,32,2,8,128]{4,3,0,2,1:T(8,128)} %fusion.42) | data formatting | bytes 2097152 | tf_op jit(solution)/shard_map/mul | solution.py:283
  56.0 0.7 fusion.54.u_ref
  56.7 3.0 %shard_map.102.src_ref = bf16[4,64,1024]{2,1,0:T(8,128)(2,1)S(1)} custom-call(bf16[4,64,1024]{2,1,0:T(8,128)(2,1)S(1)} %fusion.54.u_ref, bf16[256,512]{1,0:T(8,128)(2,1)S(1)} %copy-done.2, bf16[1536,256]{1,0:T(8,128)(2,1)S(1)} %copy-done, bf16[128,128]{1,0:T(8,128)(2,1)S(1)} %copy-done.6, bf16[128,128]{1,0:T(8,128)(2,1)S(1)} %copy-done.5, ...), custom_call_target="tpu_custom_call" | custom-call | tf_op jit(solution)/shard_map/pallas_call | solution.py:175
  59.7 0.8 copy-done.1
  60.5 23.3 %shard_map.103 = bf16[128,2,1024]{2,1,0:T(2,128)(2,1)} custom-call(bf16[4,64,1024]{2,1,0:T(8,128)(2,1)} %copy-done.1), custom_call_target="tpu_custom_call" | custom-call | tf_op jit(solution)/shard_map/pallas_call | solution.py:228
  83.8 2.2 %copy.109 = bf16[128,2,1024]{2,1,0:T(2,128)(2,1)} copy(bf16[128,2,1024]{2,1,0:T(2,128)(2,1)} %shard_map.103) | data formatting | bytes 1048576
  (27 shorter events, 0.2 us)
Async XLA Ops:
  0.0 29.0 %copy-start.11 = (s32[32,2]{0,1:T(2,128)S(1)}, s32[32,2]{0,1:T(2,128)}, u32[]{:S(2)}) copy-start(s32[32,2]{0,1:T(2,128)} %param.11) | copy-start | bytes 772
  25.0 5.5 %collective-permute-start = (f32[4,32,128]{2,1,0:T(8,128)S(1)}, f32[4,32,128]{2,1,0:T(8,128)S(1)}, u32[]{:S(2)}, u32[]{:S(2)}) collective-permute-start(f32[4,32,128]{2,1,0:T(8,128)S(1)} %slice.31), channel_id=1, source_target_pairs={{1,0},{2,1},{3,2},{4,3},{5,4},{6,5},{7,6},{9,8},{10,9},{11,10},{12... | collective-permute-start | bytes 196616 | tf_op jit(solution)/shard_map/ppermute | solution.py:26
  29.3 0.8 copy-start.12
  32.2 1.1 %copy-start = (bf16[1536,256]{1,0:T(8,128)(2,1)S(1)}, bf16[1536,256]{1,0:T(8,128)(2,1)}, u32[]{:S(2)}) copy-start(bf16[1536,256]{1,0:T(8,128)(2,1)} %constant.37.inverse_ref) | copy-start | bytes 2359300
  32.3 1.2 %copy-start.2 = (bf16[256,512]{1,0:T(8,128)(2,1)S(1)}, bf16[256,512]{1,0:T(8,128)(2,1)}, u32[]{:S(2)}) copy-start(bf16[256,512]{1,0:T(8,128)(2,1)} %constant.12.clone.forward_ref) | copy-start | bytes 786436
  32.3 1.2 %copy-start.3 = (bf16[128,128]{1,0:T(8,128)(2,1)S(1)}, bf16[128,128]{1,0:T(8,128)(2,1)}, u32[]{:S(2)}) copy-start(bf16[128,128]{1,0:T(8,128)(2,1)} %constant.35.clone.mil_ref) | copy-start | bytes 98308
  32.3 1.2 %copy-start.4 = (bf16[128,128]{1,0:T(8,128)(2,1)S(1)}, bf16[128,128]{1,0:T(8,128)(2,1)}, u32[]{:S(2)}) copy-start(bf16[128,128]{1,0:T(8,128)(2,1)} %constant.34.clone.mih_ref) | copy-start | bytes 98308
  32.3 1.1 %copy-start.5 = (bf16[128,128]{1,0:T(8,128)(2,1)S(1)}, bf16[128,128]{1,0:T(8,128)(2,1)}, u32[]{:S(2)}) copy-start(bf16[128,128]{1,0:T(8,128)(2,1)} %constant.33.clone.mfl_ref) | copy-start | bytes 98308
  32.3 1.1 %copy-start.6 = (bf16[128,128]{1,0:T(8,128)(2,1)S(1)}, bf16[128,128]{1,0:T(8,128)(2,1)}, u32[]{:S(2)}) copy-start(bf16[128,128]{1,0:T(8,128)(2,1)} %constant.32.clone.mfh_ref) | copy-start | bytes 98308
  36.4 6.3 %collective-permute-start.1 = (bf16[4,64,128]{2,1,0:T(8,128)(2,1)S(1)}, bf16[4,64,128]{2,1,0:T(8,128)(2,1)S(1)}, u32[]{:S(2)}, u32[]{:S(2)}) collective-permute-start(bf16[4,64,128]{2,1,0:T(8,128)(2,1)S(1)} %get-tuple-element.6), channel_id=1, source_target_pairs={{1,0},{2,1},{3,2},{4,3},{5,4},{6,5},{7,6},{9,8},{10,9},{11,10},{12... | collective-permute-start | bytes 196616 | tf_op jit(solution)/shard_map/ppermute | solution.py:26
  40.6 6.0 %collective-permute-start.2 = (bf16[4,64,128]{2,1,0:T(8,128)(2,1)S(1)}, bf16[4,64,128]{2,1,0:T(8,128)(2,1)}, u32[]{:S(2)}, u32[]{:S(2)}) collective-permute-start(bf16[4,64,128]{2,1,0:T(8,128)(2,1)S(1)} %get-tuple-element.5), channel_id=1, source_target_pairs={{0,1},{1,2},{2,3},{3,4},{4,5},{5,6},{6,7},{8,9},{9,10},{10,11},{11... | collective-permute-start | bytes 196616 | tf_op jit(solution)/shard_map/ppermute | solution.py:26
  43.1 1.8 %copy-start.10 = (s32[64,128]{1,0:T(8,128)S(1)}, s32[64,128]{1,0:T(8,128)}, u32[]{:S(2)}) copy-start(s32[64,128]{1,0:T(8,128)} %get-tuple-element.10) | copy-start | bytes 98308
  44.9 1.0 %copy-start.8 = (f32[4,32,9,128]{3,2,0,1:T(8,128)}, f32[4,32,9,128]{3,2,0,1:T(8,128)S(1)}, u32[]{:S(2)}) copy-start(f32[4,32,9,128]{3,2,0,1:T(8,128)S(1)} %bitcast_reduce_fusion) | copy-start | bytes 1769476
  45.9 0.8 copy-start.9
  45.9 2.4 %slice-start = ((f32[4,32,9,128]{3,2,0,1:T(8,128)}), f32[4,32,8,128]{3,2,0,1:T(8,128)S(1)}, s32[]{:S(2)}) async-start(f32[4,32,9,128]{3,2,0,1:T(8,128)} %copy-done.8), calls=%async_computation | async-start | bytes 1048576 | tf_op jit(solution)/shard_map/slice | solution.py:66
  48.5 1.1 %copy-start.7 = (f32[4,32,1024]{2,1,0:T(8,128)S(1)}, f32[4,32,1024]{2,1,0:T(8,128)}, u32[]{:S(2)}) copy-start(f32[4,32,1024]{2,1,0:T(8,128)} %shard_map.100) | copy-start | bytes 1572868
  59.7 0.8 copy-start.1

commit v6 on v4

--- a/solution.py
+++ b/solution.py
@@ -127,12 +127,11 @@
     return jnp.dot(joined, stacked, preferred_element_type=jnp.float32)
 
 
-def filter_kernel(
-    u_ref, forward_ref, inverse_ref, mfh_ref, mfl_ref, mih_ref, mil_ref, limit_ref, out_ref
-):
-    receivers, sources, samples = u_ref.shape
+def filter_block(u_ref, first, count, tables, out_ref):
+    forward_ref, inverse_ref, mfh_ref, mfl_ref, mih_ref, mil_ref, limit_ref = tables
+    sources, samples = u_ref.shape[1:]
     windows = samples // WIN
-    groups = [(r, w) for r in range(receivers) for w in range(windows)]
+    groups = [(r, w) for r in range(first, first + count) for w in range(windows)]
     scale = 1.0 / math.sqrt(WIN)
     rows = jnp.concatenate(
         [u_ref[r, :, w * WIN : (w + 1) * WIN] for r, w in groups], axis=0
@@ -172,6 +171,93 @@
         out_ref[r, :, w * WIN : (w + 1) * WIN] = restored[block(g)].astype(out_ref.dtype)
 
 
+def filter_kernel(u_ref, *refs):
+    filter_block(u_ref, 0, u_ref.shape[0], refs[:7], refs[7])
+
+
+def filter_send_kernel(count, halves, u_ref, *refs):
+    tables = refs[:7]
+    out_ref, done_ref, send_sem, recv_sem, own_sem = refs[7:]
+    receivers, sources, samples = u_ref.shape
+    own = sources // count
+    per = receivers // halves
+    me = lax.axis_index("shot")
+    row = lax.axis_index("tm")
+    barrier = pltpu.get_barrier_semaphore()
+
+    def greet(step, carry):
+        peer = lax.rem(me + step, count)
+        pl.semaphore_signal(barrier, 1, device_id=(peer, row), device_id_type=pl.DeviceIdType.MESH)
+        return carry
+
+    lax.fori_loop(1, count, greet, 0)
+
+    def remote(half, peer, sender):
+        return pltpu.make_async_remote_copy(
+            src_ref=done_ref.at[pl.ds(half * per, per), pl.ds(peer * own, own), :],
+            dst_ref=out_ref.at[pl.ds(sender * receivers + half * per, per), :, :],
+            send_sem=send_sem.at[half, peer],
+            recv_sem=recv_sem.at[half, sender],
+            device_id=(peer, row),
+            device_id_type=pl.DeviceIdType.MESH,
+        )
+
+    locals_ = []
+    for half in range(halves):
+        filter_block(u_ref, half * per, per, tables, done_ref)
+        if half == 0:
+            pl.semaphore_wait(barrier, count - 1)
+        mine = pltpu.make_async_copy(
+            done_ref.at[pl.ds(half * per, per), pl.ds(me * own, own), :],
+            out_ref.at[pl.ds(me * receivers + half * per, per), :, :],
+            own_sem.at[half],
+        )
+        mine.start()
+        locals_.append(mine)
+
+        def send(step, carry, half=half):
+            remote(half, lax.rem(me + step, count), me).start()
+            return carry
+
+        lax.fori_loop(1, count, send, 0)
+
+    for half in range(halves):
+
+        def finish(step, carry, half=half):
+            peer = lax.rem(me + step, count)
+            remote(half, peer, me).wait_send()
+            remote(half, me, peer).wait_recv()
+            return carry
+
+        lax.fori_loop(1, count, finish, 0)
+        locals_[half].wait()
+
+
+def filter_and_send(gathers, limits, tables):
+    forward, inverse, mix_forward, mix_inverse = tables
+    receivers, sources, samples = gathers.shape
+    count = lax.axis_size("shot")
+    halves = 2
+    vmem = pl.BlockSpec(memory_space=pltpu.VMEM)
+    return pl.pallas_call(
+        functools.partial(filter_send_kernel, count, halves),
+        in_specs=[vmem] * 8,
+        out_specs=pl.BlockSpec(memory_space=pl.ANY),
+        out_shape=jax.ShapeDtypeStruct(
+            (receivers * count, sources // count, samples), jnp.bfloat16
+        ),
+        scratch_shapes=[
+            pltpu.VMEM(gathers.shape, jnp.bfloat16),
+            pltpu.SemaphoreType.DMA((halves, count)),
+            pltpu.SemaphoreType.DMA((halves, count)),
+            pltpu.SemaphoreType.DMA((halves,)),
+        ],
+        compiler_params=pltpu.CompilerParams(
+            collective_id=2, has_side_effects=True, vmem_limit_bytes=48 * 1024 * 1024
+        ),
+    )(gathers, forward, inverse, *mix_forward, *mix_inverse, limits.reshape(sources, 1))
+
+
 def coherence(gathers, limits, tables):
     forward, inverse, mix_forward, mix_inverse = tables
     receivers, sources, samples = gathers.shape
@@ -282,8 +368,9 @@
             update = (estimate.astype(jnp.float32) + RELAX * spread(residual, delays)).astype(
                 jnp.bfloat16
             )
+        if sweep == ITERS - 1:
+            return filter_and_send(update, thresholds[sweep], tables)
         estimate = coherence(update, thresholds[sweep], tables)
-    return to_sources(estimate)
 
 
 def solution(mesh):

time: 85.8 us -> 81.4 us (0.949)
  local copies, waits for them, and re-layouts: 7.46 us -> 5.27 us
  Pallas kernels: 53.4 us -> 51.3 us
    pallas_call x0 -> x1, Pallas kernels: none -> 24.2 us  [filter_and_send(): pl.pallas_call(functools.partial(filter_send_kernel, count, halves), in_s...]
    pallas_call x2 -> x1, Pallas kernels: 47.5 us -> 24.1 us  [exchange(): pl.pallas_call(functools.partial(exchange_kernel, count, outgoing, incomi...]
    pallas_call x2 -> x1, Pallas kernels: 5.92 us -> 2.96 us  [coherence(): pl.pallas_call(filter_kernel, in_specs=[vmem] * 8, out_specs=vmem, out_sh...]
    unnamed x23 -> x21, local copies, waits for them, and re-layouts: 4.78 us -> 2.59 us
  transfers between devices with their start and end apart: 3 -> 3, of which waited for: 2 -> 2; matrix products, arithmetic and copies ran while one was open for 7% -> 8% of each run, Pallas kernels for 0% -> 0%
where the time goes in v6:
time: 81.4 us; the launch traced here: 80.5 us
  Pallas kernels  51.3 us (63%)
  matrix products  8.36 us (10%)
  starting transfers between devices  7.38 us (9%)
  local copies, waits for them, and re-layouts  5.27 us (6%)
  other arithmetic  4.37 us (5%)
  waiting for transfers between devices  3.54 us (4%)
    pallas_call x1, Pallas kernels, filter_and_send(): pl.pallas_call(functools.partial(filter_send_kernel, count, halves), in_s...  24.2 us
    pallas_call x1, Pallas kernels, exchange(): pl.pallas_call(functools.partial(exchange_kernel, count, outgoing, incomi...  24.1 us
    ppermute x3, starting transfers between devices, shifted(): return lax.ppermute(array, axis, pairs)  7.38 us
    ppermute x3, waiting for transfers between devices, shifted(): return lax.ppermute(array, axis, pairs)  3.54 us
    pallas_call x1, Pallas kernels, coherence(): pl.pallas_call(filter_kernel, in_specs=[vmem] * 8, out_specs=vmem, out_sh...  2.96 us
    dot_general x2, matrix products, spread(): jnp.einsum('rena,ekai->rekni', lower, select_same, preferred_element_type...  2.8 us
    unnamed x21, local copies, waits for them, and re-layouts  2.59 us
    dot_general x2, matrix products, spread(): jnp.einsum('rena,ekai->rekni', lower, select_next, preferred_element_type...  1.63 us
  transfers between devices with their start and end apart: 3, of which 2 were waited for; matrix products, arithmetic and copies ran while one was open for 8% of the time, Pallas kernels for 0%

profile of v6, /device:TPU:3, one launch (start us, length us, event | category | flops | bytes accessed | tf_op | source)
XLA Modules:
  0.0 80.5 jit_solution(4149550630376513047)
XLA Ops:
  0.0 24.1 %shard_map.91 = f32[4,32,1024]{2,1,0:T(8,128)} custom-call(f32[128,1,1024]{2,1,0:T(1,128)} %src_ref.1), custom_call_target="tpu_custom_call" | custom-call | tf_op jit(solution)/shard_map/pallas_call | solution.py:318
  24.1 0.0 copy-start.7
  24.1 1.1 %convert_element_type.34 = bf16[4,32,1024]{2,1,0:T(8,128)(2,1)S(1)} convert(f32[4,32,1024]{2,1,0:T(8,128)} %shard_map.91) | non-fusion elementwise | flops 131072 | bytes 786432 | tf_op jit(solution)/shard_map/convert_element_type | solution.py:364
  25.2 3.0 %collective-permute-start = (bf16[4,32,128]{2,1,0:T(8,128)(2,1)S(1)}, bf16[4,32,128]{2,1,0:T(8,128)(2,1)S(1)}, u32[]{:S(2)}, u32[]{:S(2)}) collective-permute-start(bf16[4,32,128]{2,1,0:T(8,128)(2,1)S(1)} %slice.33), channel_id=1, source_target_pairs={{1,0},{2,1},{3,2},{4,3},{5,4},{6,5},{7,6},{9,8},{10,9},{11,10},{12... | collective-permute-start | bytes 98312 | tf_op jit(solution)/shard_map/ppermute | solution.py:26
  28.2 0.0 copy-done.6
  28.2 0.1 copy.40
  28.3 0.1 iota_add_fusion
  28.4 0.1 sub.40
  28.5 1.0 %fusion.76 = bf16[256,256]{1,0:T(8,128)(2,1)S(1)} fusion(), kind=kLoop, calls=%fused_computation.67 | loop fusion | flops 1179648 | bytes 131072 | tf_op jit(solution)/shard_map/neg | solution.py:105
  29.5 1.0 %cosine_convert_fusion = bf16[256,256]{1,0:T(8,128)(2,1)S(1)} fusion(), kind=kLoop, calls=%fused_computation.59 | loop fusion | flops 983040 | bytes 131072 | tf_op jit(solution)/shard_map/convert_element_type | solution.py:105
  30.6 0.1 broadcast_subtract_fusion
  30.7 0.8 %fusion.31 = f32[4,32,2,8,128]{4,3,0,2,1:T(8,128)S(1)} fusion(s32[32,2,128]{2,1,0:T(2,128)S(1)} %iota_add_fusion, s32[128]{0:T(128)S(1)} %iota_add_fusion.1, bf16[4,32,8,128]{3,2,1,0:T(8,128)(2,1)S(1)} %bitcast.166), kind=kOutput, calls=%fused_computation.31 | convolution fusion | flops 68157440 | bytes 1344000 | tf_op jit(solution)/shard_map/rena,ekai->rekni/dot_general | solution.py:83
  31.5 0.1 slice.32
  31.7 0.1 copy.45.refs_6_
  31.8 0.1 copy.55.refs_6_
  31.8 0.0 collective-permute-done
  31.9 0.8 fusion.2
  32.6 0.9 %fusion.51 = bf16[4,32,2,8,128]{4,3,0,2,1:T(8,128)(2,1)S(1)} fusion(s32[32,2,128]{2,1,0:T(2,128)S(1)} %iota_add_fusion, f32[4,32,2,1,128]{4,3,0,2,1:T(1,128)S(1)} %bitcast.174, f32[4,32,2,7,128]{4,3,0,2,1:T(8,128)S(1)} %slice.32, bf16[4,32,8,128]{3,2,1,0:T(8,128)(2,1)S(1)} %bitcast.167), kind=kOutput, calls=%fused_computation.39 | convolution fusion | flops 69206016 | bytes 1867776 | tf_op jit(solution)/shard_map/rena,ekai->rekni/dot_general | solution.py:82
  33.6 0.0 copy-start
  33.6 0.0 copy-start.1
  33.6 0.0 copy-start.2
  33.6 0.0 copy-start.3
  33.6 0.0 copy-start.4
  33.6 0.1 reshape.116
  33.8 0.2 copy.72.u_ref
  33.9 0.8 copy-done
  34.7 0.0 copy-done.2
  34.7 3.0 %shard_map.92 = bf16[4,64,1024]{2,1,0:T(8,128)(2,1)S(1)} custom-call(bf16[4,64,1024]{2,1,0:T(8,128)(2,1)S(1)} %copy.72.u_ref, bf16[256,512]{1,0:T(8,128)(2,1)S(1)} %pad_maximum_fusion.refs_0_, bf16[1536,256]{1,0:T(8,128)(2,1)S(1)} %copy-done, bf16[128,128]{1,0:T(8,128)(2,1)S(1)} %copy-done.1, bf16[128,128]{1,0:T(8,128)(2,1)S(1)} %copy-done.2, ...), custom_call_target="tpu_custom_call" | custom-call | tf_op jit(solution)/shard_map/pallas_call | solution.py:265
  37.7 0.1 copy.82
  37.8 2.3 %collective-permute-start.1 = (bf16[4,64,128]{2,1,0:T(8,128)(2,1)S(1)}, bf16[4,64,128]{2,1,0:T(8,128)(2,1)S(1)}, u32[]{:S(2)}, u32[]{:S(2)}) collective-permute-start(bf16[4,64,128]{2,1,0:T(8,128)(2,1)S(1)} %slice.34), channel_id=1, source_target_pairs={{0,1},{1,2},{2,3},{3,4},{4,5},{5,6},{6,7},{8,9},{9,10},{10,11},{11... | collective-permute-start | bytes 196616 | tf_op jit(solution)/shard_map/ppermute | solution.py:26
  40.1 0.8 bitcast_reduce_fusion.1
  40.9 0.8 bitcast_reduce_fusion
  41.7 2.0 %collective-permute-done.1 = bf16[4,64,128]{2,1,0:T(8,128)(2,1)S(1)} collective-permute-done((bf16[4,64,128]{2,1,0:T(8,128)(2,1)S(1)}, bf16[4,64,128]{2,1,0:T(8,128)(2,1)S(1)}, u32[]{:S(2)}, u32[]{:S(2)}) %collective-permute-start.1) | collective-permute-done | bytes 65568 | tf_op jit(solution)/shard_map/ppermute | solution.py:26
  43.7 0.8 bitcast_reduce_fusion.2
  44.5 0.1 maximum_add_fusion
  44.7 0.2 reshape.117
  44.9 0.7 copy-done.5
  45.6 0.3 fusion.55
  45.9 2.1 %collective-permute-start.2 = (bf16[4,32,128]{2,1,0:T(8,128)(2,1)S(1)}, bf16[4,32,128]{2,1,0:T(8,128)(2,1)S(1)}, u32[]{:S(2)}, u32[]{:S(2)}) collective-permute-start(bf16[4,32,128]{2,1,0:T(8,128)(2,1)S(1)} %slice.37), channel_id=1, source_target_pairs={{1,0},{2,1},{3,2},{4,3},{5,4},{6,5},{7,6},{9,8},{10,9},{11,10},{12... | collective-permute-start | bytes 98312 | tf_op jit(solution)/shard_map/ppermute | solution.py:26
  48.1 0.8 %fusion.32 = f32[4,32,2,8,128]{4,3,0,2,1:T(8,128)S(1)} fusion(s32[32,2,128]{2,1,0:T(2,128)S(1)} %iota_add_fusion, s32[128]{0:T(128)S(1)} %iota_add_fusion.1, bf16[4,32,8,128]{3,2,1,0:T(8,128)(2,1)S(1)} %bitcast.168), kind=kOutput, calls=%fused_computation.32 | convolution fusion | flops 68157440 | bytes 1344000 | tf_op jit(solution)/shard_map/rena,ekai->rekni/dot_general | solution.py:83
  48.9 0.2 slice.36
  49.1 1.5 %collective-permute-done.2 = bf16[4,32,128]{2,1,0:T(8,128)(2,1)S(1)} collective-permute-done((bf16[4,32,128]{2,1,0:T(8,128)(2,1)S(1)}, bf16[4,32,128]{2,1,0:T(8,128)(2,1)S(1)}, u32[]{:S(2)}, u32[]{:S(2)}) %collective-permute-start.2) | collective-permute-done | bytes 32800 | tf_op jit(solution)/shard_map/ppermute | solution.py:26
  50.6 0.8 fusion
  51.4 1.9 %fusion.42 = f32[4,32,2,8,128]{4,3,0,2,1:T(8,128)} fusion(s32[32,2,128]{2,1,0:T(2,128)S(1)} %iota_add_fusion, f32[4,32,2,1,128]{4,3,0,2,1:T(1,128)S(1)} %bitcast.173, f32[4,32,2,7,128]{4,3,0,2,1:T(8,128)S(1)} %slice.36, bf16[4,32,8,128]{3,2,1,0:T(8,128)(2,1)S(1)} %bitcast.169), kind=kOutput, calls=%fused_computation.36 | convolution fusion | flops 68943872 | bytes 2392064 | tf_op jit(solution)/shard_map/rena,ekai->rekni/dot_general | solution.py:82
  53.3 1.6 %reshape.118 = f32[4,64,1024]{2,0,1:T(4,128)S(1)} reshape(f32[4,32,2,8,128]{4,3,0,2,1:T(8,128)} %fusion.42) | data formatting | bytes 2097152 | tf_op jit(solution)/shard_map/mul | solution.py:368
  54.8 0.7 fusion.54.u_ref
  55.5 24.2 %shard_map.93 = bf16[128,2,1024]{2,1,0:T(2,128)(2,1)S(1)} custom-call(bf16[4,64,1024]{2,1,0:T(8,128)(2,1)S(1)} %fusion.54.u_ref, bf16[256,512]{1,0:T(8,128)(2,1)S(1)} %pad_maximum_fusion.refs_0_, bf16[1536,256]{1,0:T(8,128)(2,1)S(1)} %copy-done, bf16[128,128]{1,0:T(8,128)(2,1)S(1)} %copy-done.1, bf16[128,128]{1,0:T(8,128)(2,1)S(1)} %copy-done.2, ...), custom_call_target="tpu_custom_call" | custom-call | tf_op jit(solution)/shard_map/pallas_call | solution.py:242
  79.7 0.8 copy.115
  (14 shorter events, 0.2 us)
Async XLA Ops:
  0.0 28.2 %copy-start.6 = (s32[32,2]{0,1:T(2,128)S(1)}, s32[32,2]{0,1:T(2,128)}, u32[]{:S(2)}) copy-start(s32[32,2]{0,1:T(2,128)} %param.10) | copy-start | bytes 772
  24.1 6.4 %copy-start.7 = (f32[2,64]{1,0:T(2,128)S(1)}, f32[2,64]{1,0:T(2,128)}, u32[]{:S(2)}) copy-start(f32[2,64]{1,0:T(2,128)} %param.11) | copy-start | bytes 1540
  25.2 6.6 %collective-permute-start = (bf16[4,32,128]{2,1,0:T(8,128)(2,1)S(1)}, bf16[4,32,128]{2,1,0:T(8,128)(2,1)S(1)}, u32[]{:S(2)}, u32[]{:S(2)}) collective-permute-start(bf16[4,32,128]{2,1,0:T(8,128)(2,1)S(1)} %slice.33), channel_id=1, source_target_pairs={{1,0},{2,1},{3,2},{4,3},{5,4},{6,5},{7,6},{9,8},{10,9},{11,10},{12... | collective-permute-start | bytes 98312 | tf_op jit(solution)/shard_map/ppermute | solution.py:26
  33.6 1.1 %copy-start = (bf16[1536,256]{1,0:T(8,128)(2,1)S(1)}, bf16[1536,256]{1,0:T(8,128)(2,1)}, u32[]{:S(2)}) copy-start(bf16[1536,256]{1,0:T(8,128)(2,1)} %constant.43.refs_1_) | copy-start | bytes 2359300
  33.6 1.1 %copy-start.1 = (bf16[128,128]{1,0:T(8,128)(2,1)S(1)}, bf16[128,128]{1,0:T(8,128)(2,1)}, u32[]{:S(2)}) copy-start(bf16[128,128]{1,0:T(8,128)(2,1)} %constant.38.clone.refs_2_) | copy-start | bytes 98308
  33.6 1.1 %copy-start.2 = (bf16[128,128]{1,0:T(8,128)(2,1)S(1)}, bf16[128,128]{1,0:T(8,128)(2,1)}, u32[]{:S(2)}) copy-start(bf16[128,128]{1,0:T(8,128)(2,1)} %constant.39.clone.refs_3_) | copy-start | bytes 98308
  33.6 1.1 %copy-start.3 = (bf16[128,128]{1,0:T(8,128)(2,1)S(1)}, bf16[128,128]{1,0:T(8,128)(2,1)}, u32[]{:S(2)}) copy-start(bf16[128,128]{1,0:T(8,128)(2,1)} %constant.40.clone.refs_4_) | copy-start | bytes 98308
  33.6 1.1 %copy-start.4 = (bf16[128,128]{1,0:T(8,128)(2,1)S(1)}, bf16[128,128]{1,0:T(8,128)(2,1)}, u32[]{:S(2)}) copy-start(bf16[128,128]{1,0:T(8,128)(2,1)} %constant.41.clone.refs_5_) | copy-start | bytes 98308
  37.8 5.9 %collective-permute-start.1 = (bf16[4,64,128]{2,1,0:T(8,128)(2,1)S(1)}, bf16[4,64,128]{2,1,0:T(8,128)(2,1)S(1)}, u32[]{:S(2)}, u32[]{:S(2)}) collective-permute-start(bf16[4,64,128]{2,1,0:T(8,128)(2,1)S(1)} %slice.34), channel_id=1, source_target_pairs={{0,1},{1,2},{2,3},{3,4},{4,5},{5,6},{6,7},{8,9},{9,10},{10,11},{11... | collective-permute-start | bytes 196616 | tf_op jit(solution)/shard_map/ppermute | solution.py:26
  44.5 1.0 %copy-start.5 = (f32[4,32,1024]{2,1,0:T(8,128)S(1)}, f32[4,32,1024]{2,1,0:T(8,128)}, u32[]{:S(2)}) copy-start(f32[4,32,1024]{2,1,0:T(8,128)} %shard_map.91) | copy-start | bytes 1572868
  45.9 4.7 %collective-permute-start.2 = (bf16[4,32,128]{2,1,0:T(8,128)(2,1)S(1)}, bf16[4,32,128]{2,1,0:T(8,128)(2,1)S(1)}, u32[]{:S(2)}, u32[]{:S(2)}) collective-permute-start(bf16[4,32,128]{2,1,0:T(8,128)(2,1)S(1)} %slice.37), channel_id=1, source_target_pairs={{1,0},{2,1},{3,2},{4,3},{5,4},{6,5},{7,6},{9,8},{10,9},{11,10},{12... | collective-permute-start | bytes 98312 | tf_op jit(solution)/shard_map/ppermute | solution.py:26

commit v7 on v6

--- a/solution.py
+++ b/solution.py
@@ -45,11 +45,10 @@
     return (cos_forward, sin_forward, cos_inverse, sin_inverse, cos_source, sin_source)
 
 
-def blend(estimate, own_delays):
+def blend(estimate, earlier, own_delays):
     receivers, sources, samples = estimate.shape
     blocks = samples // BLK
     experiments = sources // SRC_EXP
-    earlier = shifted(estimate[:, :, samples - BLK :], "tm", 1)
     upper = estimate.reshape(receivers, sources, blocks, BLK)
     shifts = own_delays.reshape(-1)
     row_index = jnp.arange(BLK, dtype=jnp.int32)[None, :, None]
@@ -68,10 +67,9 @@
     return (same + carried).reshape(receivers, experiments, samples)
 
 
-def spread(residual, own_delays):
+def spread(residual, later, own_delays):
     receivers, experiments, samples = residual.shape
     blocks = samples // BLK
-    later = shifted(residual[:, :, :BLK], "tm", -1)
     lower = residual.reshape(receivers, experiments, blocks, BLK)
     row_index = jnp.arange(BLK, dtype=jnp.int32)[None, None, :, None]
     column_index = jnp.arange(BLK, dtype=jnp.int32)[None, None, None, :]
@@ -173,6 +171,81 @@
 
 def filter_kernel(u_ref, *refs):
     filter_block(u_ref, 0, u_ref.shape[0], refs[:7], refs[7])
+
+
+def filter_halo_kernel(stages, u_ref, *refs):
+    tables = refs[:7]
+    out_ref, before_ref, after_ref, send_sem, recv_sem = refs[7:]
+    samples = u_ref.shape[2]
+    shot = lax.axis_index("shot")
+    row = lax.axis_index("tm")
+    has_prev = row > 0
+    has_next = row < stages - 1
+    barrier = pltpu.get_barrier_semaphore()
+    mesh_id = pl.DeviceIdType.MESH
+
+    @pl.when(has_prev)
+    def _():
+        pl.semaphore_signal(barrier, 1, device_id=(shot, row - 1), device_id_type=mesh_id)
+
+    @pl.when(has_next)
+    def _():
+        pl.semaphore_signal(barrier, 1, device_id=(shot, row + 1), device_id_type=mesh_id)
+
+    filter_block(u_ref, 0, u_ref.shape[0], tables, out_ref)
+    pl.semaphore_wait(barrier, has_prev.astype(jnp.int32) + has_next.astype(jnp.int32))
+
+    def to_prev():
+        return pltpu.make_async_remote_copy(
+            src_ref=out_ref.at[:, :, pl.ds(0, BLK)],
+            dst_ref=after_ref,
+            send_sem=send_sem.at[0],
+            recv_sem=recv_sem.at[0],
+            device_id=(shot, row - 1),
+            device_id_type=mesh_id,
+        )
+
+    def to_next():
+        return pltpu.make_async_remote_copy(
+            src_ref=out_ref.at[:, :, pl.ds(samples - BLK, BLK)],
+            dst_ref=before_ref,
+            send_sem=send_sem.at[1],
+            recv_sem=recv_sem.at[1],
+            device_id=(shot, row + 1),
+            device_id_type=mesh_id,
+        )
+
+    pl.when(has_prev)(lambda: to_prev().start())
+    pl.when(has_next)(lambda: to_next().start())
+
+    @pl.when(has_prev)
+    def _():
+        to_prev().wait_send()
+        to_next().wait_recv()
+
+    @pl.when(has_next)
+    def _():
+        to_next().wait_send()
+        to_prev().wait_recv()
+
+
+def filter_with_halos(gathers, limits, tables):
+    forward, inverse, mix_forward, mix_inverse = tables
+    receivers, sources, samples = gathers.shape
+    stages = lax.axis_size("tm")
+    vmem = pl.BlockSpec(memory_space=pltpu.VMEM)
+    anywhere = pl.BlockSpec(memory_space=pl.ANY)
+    edge = jax.ShapeDtypeStruct((receivers, sources, BLK), jnp.bfloat16)
+    return pl.pallas_call(
+        functools.partial(filter_halo_kernel, stages),
+        in_specs=[vmem] * 8,
+        out_specs=(vmem, anywhere, anywhere),
+        out_shape=(jax.ShapeDtypeStruct(gathers.shape, jnp.bfloat16), edge, edge),
+        scratch_shapes=[pltpu.SemaphoreType.DMA((2,)), pltpu.SemaphoreType.DMA((2,))],
+        compiler_params=pltpu.CompilerParams(
+            collective_id=3, has_side_effects=True, vmem_limit_bytes=48 * 1024 * 1024
+        ),
+    )(gathers, forward, inverse, *mix_forward, *mix_inverse, limits.reshape(sources, 1))
 
 
 def filter_send_kernel(count, halves, u_ref, *refs):
@@ -358,19 +431,22 @@
 def local(blended, delays, thresholds):
     tables = filter_tables()
     records = to_receivers(blended)
-    estimate = None
-    for sweep in range(ITERS):
-        if sweep == 0:
-            residual = records.astype(jnp.bfloat16)
-            update = (RELAX * spread(residual, delays)).astype(jnp.bfloat16)
-        else:
-            residual = (records - blend(estimate, delays)).astype(jnp.bfloat16)
-            update = (estimate.astype(jnp.float32) + RELAX * spread(residual, delays)).astype(
-                jnp.bfloat16
-            )
-        if sweep == ITERS - 1:
-            return filter_and_send(update, thresholds[sweep], tables)
-        estimate = coherence(update, thresholds[sweep], tables)
+    samples = records.shape[2]
+    row = lax.axis_index("tm")
+    following = shifted(records[:, :, :BLK], "tm", -1)
+    residual = records.astype(jnp.bfloat16)
+    update = (RELAX * spread(residual, following.astype(jnp.bfloat16), delays)).astype(jnp.bfloat16)
+    estimate, before, after = filter_with_halos(update, thresholds[0], tables)
+    before = jnp.where(row == 0, jnp.zeros_like(before), before)
+    last = row == lax.axis_size("tm") - 1
+    after = jnp.where(last, jnp.zeros_like(after), after)
+    blended_part = blend(jnp.concatenate([estimate, after], axis=2), before, delays)
+    residual = (jnp.concatenate([records, following], axis=2) - blended_part).astype(jnp.bfloat16)
+    tail = jnp.where(last, jnp.zeros_like(residual[:, :, samples:]), residual[:, :, samples:])
+    update = (
+        estimate.astype(jnp.float32) + RELAX * spread(residual[:, :, :samples], tail, delays)
+    ).astype(jnp.bfloat16)
+    return filter_and_send(update, thresholds[1], tables)
 
 
 def solution(mesh):

time: 81.4 us -> 80.8 us (level)
  starting transfers between devices: 7.38 us -> 2.95 us
  waiting for transfers between devices: 3.54 us -> 0.01 us
  Pallas kernels: 51.3 us -> 53.9 us
  local copies, waits for them, and re-layouts: 5.27 us -> 7.24 us
  other arithmetic: 4.37 us -> 5.95 us
  matrix products: 8.36 us -> 9.45 us
    pallas_call x1, Pallas kernels: 2.96 us -> 7.67 us  [filter_with_halos(): pl.pallas_call(functools.partial(filter_halo_kernel, stages), in_specs=[v...]
    ppermute x3 -> x1, starting transfers between devices: 7.38 us -> 2.95 us  [shifted(): return lax.ppermute(array, axis, pairs)]
    ppermute x3 -> x1, waiting for transfers between devices: 3.54 us -> 0.01 us  [shifted(): return lax.ppermute(array, axis, pairs)]
    pallas_call x1, Pallas kernels: 24.2 us -> 22 us  [filter_and_send(): pl.pallas_call(functools.partial(filter_send_kernel, count, halves), in_s...]
    slice x3, local copies, waits for them, and re-layouts: 0.04 us -> 0.9 us  [the longest x1 0.85 us: local(): following = shifted(records[:, :, :BLK], 'tm', -1)]
    add x1, local copies, waits for them, and re-layouts: 0.18 us -> 1.04 us  [blend(): return (same + carried).reshape(receivers, experiments, samples)]
    convert_element_type x2 -> x3, other arithmetic: 0.98 us -> 1.8 us  [the longest x1 1.13 us: local(): (jnp.concatenate([records, following], axis=2) - blended_part).astype(jnp...]
    unnamed x21 -> x24, local copies, waits for them, and re-layouts: 2.59 us -> 2.51 us
  transfers between devices with their start and end apart: 3 -> 1, of which waited for: 2 -> 0; matrix products, arithmetic and copies ran while one was open for 8% -> 7% of each run, Pallas kernels for 0% -> 0%
where the time goes in v7:
time: 80.8 us; the launch traced here: 79.8 us
  Pallas kernels  53.9 us (67%)
  matrix products  9.45 us (12%)
  local copies, waits for them, and re-layouts  7.24 us (9%)
  other arithmetic  5.95 us (7%)
  starting transfers between devices  2.95 us (4%)
    pallas_call x1, Pallas kernels, exchange(): pl.pallas_call(functools.partial(exchange_kernel, count, outgoing, incomi...  24.2 us
    pallas_call x1, Pallas kernels, filter_and_send(): pl.pallas_call(functools.partial(filter_send_kernel, count, halves), in_s...  22 us
    pallas_call x1, Pallas kernels, filter_with_halos(): pl.pallas_call(functools.partial(filter_halo_kernel, stages), in_specs=[v...  7.67 us
    ppermute x1, starting transfers between devices, shifted(): return lax.ppermute(array, axis, pairs)  2.95 us
    dot_general x2, matrix products, spread(): jnp.einsum('rena,ekai->rekni', lower, select_same, preferred_element_type...  2.82 us
    unnamed x24, local copies, waits for them, and re-layouts  2.51 us
    dot_general x2, matrix products, spread(): jnp.einsum('rena,ekai->rekni', lower, select_next, preferred_element_type...  1.63 us
  transfers between devices with their start and end apart: 1, of which 0 were waited for; matrix products, arithmetic and copies ran while one was open for 7% of the time, Pallas kernels for 0%

profile of v7, /device:TPU:3, one launch (start us, length us, event | category | flops | bytes accessed | tf_op | source)
XLA Modules:
  0.0 79.8 jit_solution(6585573436302019943)
XLA Ops:
  0.0 24.2 %shard_map.91 = f32[4,32,1024]{2,1,0:T(8,128)} custom-call(f32[128,1,1024]{2,1,0:T(1,128)} %src_ref.1), custom_call_target="tpu_custom_call" | custom-call | tf_op jit(solution)/shard_map/pallas_call | solution.py:391
  24.2 0.8 %slice.25 = f32[4,32,128]{2,1,0:T(8,128)S(1)} slice(f32[4,32,1024]{2,1,0:T(8,128)} %shard_map.91), slice={[0:4], [0:32], [0:128]} | slice | bytes 131072 | tf_op jit(solution)/shard_map/slice | solution.py:436
  25.0 2.9 %collective-permute-start = (f32[4,32,128]{2,1,0:T(8,128)S(1)}, f32[4,32,128]{2,1,0:T(8,128)S(1)}, u32[]{:S(2)}, u32[]{:S(2)}) collective-permute-start(f32[4,32,128]{2,1,0:T(8,128)S(1)} %slice.25), channel_id=1, source_target_pairs={{1,0},{2,1},{3,2},{4,3},{5,4},{6,5},{7,6},{9,8},{10,9},{11,10},{12... | collective-permute-start | bytes 196616 | tf_op jit(solution)/shard_map/ppermute | solution.py:26
  28.0 0.1 copy.40
  28.1 0.1 sub.40
  28.2 0.1 iota_add_fusion
  28.3 1.0 %fusion.72 = bf16[256,256]{1,0:T(8,128)(2,1)S(1)} fusion(), kind=kLoop, calls=%fused_computation.68 | loop fusion | flops 1179648 | bytes 131072 | tf_op jit(solution)/shard_map/neg | solution.py:103
  29.3 1.0 %cosine_convert_fusion = bf16[256,256]{1,0:T(8,128)(2,1)S(1)} fusion(), kind=kLoop, calls=%fused_computation.60 | loop fusion | flops 983040 | bytes 131072 | tf_op jit(solution)/shard_map/convert_element_type | solution.py:103
  30.3 1.1 %convert_element_type.37 = bf16[4,32,1024]{2,1,0:T(8,128)(2,1)S(1)} convert(f32[4,32,1024]{2,1,0:T(8,128)} %shard_map.91) | non-fusion elementwise | flops 131072 | bytes 786432 | tf_op jit(solution)/shard_map/convert_element_type | solution.py:437
  31.4 0.0 copy-done.9
  31.4 0.1 copy.55.refs_6_
  31.5 0.1 copy.45.refs_6_
  31.6 0.7 broadcast_subtract_fusion
  32.4 0.8 %fusion.31 = f32[4,32,2,8,128]{4,3,0,2,1:T(8,128)S(1)} fusion(s32[32,2,128]{2,1,0:T(2,128)S(1)} %iota_add_fusion, s32[128]{0:T(128)S(1)} %iota_add_fusion.1, bf16[4,32,8,128]{3,2,1,0:T(8,128)(2,1)S(1)} %bitcast.145), kind=kOutput, calls=%fused_computation.33 | convolution fusion | flops 68157440 | bytes 1344000 | tf_op jit(solution)/shard_map/rena,ekai->rekni/dot_general | solution.py:81
  33.2 0.1 slice.32
  33.3 0.0 collective-permute-done
  33.4 0.8 fusion.2
  34.2 0.9 %fusion.51 = bf16[4,32,2,8,128]{4,3,0,2,1:T(8,128)(2,1)S(1)} fusion(s32[32,2,128]{2,1,0:T(2,128)S(1)} %iota_add_fusion, f32[4,32,2,1,128]{4,3,0,2,1:T(1,128)S(1)} %bitcast.151, f32[4,32,2,7,128]{4,3,0,2,1:T(8,128)S(1)} %slice.32, bf16[4,32,8,128]{3,2,1,0:T(8,128)(2,1)S(1)} %bitcast.146), kind=kOutput, calls=%fused_computation.41 | convolution fusion | flops 69206016 | bytes 1867776 | tf_op jit(solution)/shard_map/rena,ekai->rekni/dot_general | solution.py:80
  35.1 0.0 copy-start
  35.1 0.0 copy-start.1
  35.1 0.0 copy-start.2
  35.1 0.0 copy-start.3
  35.2 0.0 copy-start.4
  35.2 0.1 reshape.116
  35.3 0.2 copy.72.u_ref
  35.5 0.8 copy-done
  36.2 0.0 copy-done.1
  36.2 0.0 copy-done.3
  36.3 7.7 %shard_map.92 = (bf16[4,64,1024]{2,1,0:T(8,128)(2,1)S(1)}, bf16[4,64,128]{2,1,0:T(8,128)(2,1)S(1)}, bf16[4,64,128]{2,1,0:T(8,128)(2,1)S(1)}) custom-call(bf16[4,64,1024]{2,1,0:T(8,128)(2,1)S(1)} %copy.72.u_ref, bf16[256,512]{1,0:T(8,128)(2,1)S(1)} %pad_maximum_fusion.1.refs_0_, bf16[1536,256]{1,0:T(8,128)(2,1)S(1)} %copy-done, ...), custom_call_target="tpu_custom_call" | custom-call | tf_op jit(solution)/shard_map/pallas_call | solution.py:239
  44.0 0.1 pad_maximum_fusion
  44.0 0.3 reshape.101
  44.4 0.0 copy-start.7
  44.4 1.6 %bitcast_reduce_fusion.2 = f32[4,32,128]{2,0,1:T(4,128)S(1)} fusion(bf16[4,64,128]{2,1,0:T(8,128)(2,1)S(1)} %get-tuple-element.15, s32[64,128]{1,0:T(8,128)} %get-tuple-element.13), kind=kOutput, calls=%fused_computation.69 | convolution fusion | flops 9453568 | bytes 163840 | tf_op jit(solution)/shard_map/rsb,sbi->rsi/dot_general | solution.py:60
  46.0 0.9 %bitcast_reduce_fusion = f32[4,32,9,128]{3,2,0,1:T(8,128)S(1)} fusion(s32[64,128]{1,0:T(8,128)S(1)} %copy-done.7, bf16[4,64,9,128]{3,2,1,0:T(8,128)(2,1)S(1)} %reshape.101), kind=kOutput, calls=%fused_computation.18 | convolution fusion | flops 76693504 | bytes 1212416 | tf_op jit(solution)/shard_map/rsnb,sbi->rsni/dot_general | solution.py:59
  46.9 0.7 copy-done.6
  47.6 0.9 %bitcast_reduce_fusion.1 = f32[4,32,9,128]{3,2,0,1:T(8,128)S(1)} fusion(s32[64,128]{1,0:T(8,128)S(1)} %copy-done.6, bf16[4,64,9,128]{3,2,1,0:T(8,128)(2,1)S(1)} %reshape.101), kind=kOutput, calls=%fused_computation.19 | convolution fusion | flops 76693504 | bytes 1212416 | tf_op jit(solution)/shard_map/rsnb,sbi->rsni/dot_general | solution.py:58
  48.6 0.2 maximum_add_fusion
  48.8 1.0 %reshape.117 = f32[4,32,1152]{2,0,1:T(4,128)} reshape(f32[4,32,9,128]{3,2,0,1:T(8,128)S(1)} %maximum_add_fusion) | data formatting | bytes 1179648 | tf_op jit(solution)/shard_map/add | solution.py:67
  49.8 0.0 copy-done.5
  49.8 1.1 %fusion.61 = bf16[4,32,1152]{2,1,0:T(8,128)(2,1)S(1)} fusion(f32[4,32,128]{2,1,0:T(8,128)S(1)} %collective-permute-done, f32[4,32,1024]{2,1,0:T(8,128)S(1)} %copy-done.5, f32[4,32,1152]{2,0,1:T(4,128)} %reshape.117), kind=kLoop, calls=%fused_computation.48 | loop fusion | flops 442368 | bytes 1474560 | tf_op jit(solution)/shard_map/convert_element_type | solution.py:444
  51.1 0.8 fusion
  51.9 0.8 %fusion.32 = f32[4,32,2,8,128]{4,3,0,2,1:T(8,128)S(1)} fusion(s32[32,2,128]{2,1,0:T(2,128)S(1)} %iota_add_fusion, s32[128]{0:T(128)S(1)} %iota_add_fusion.1, bf16[4,32,8,128]{3,2,1,0:T(8,128)(2,1)S(1)} %bitcast.147), kind=kOutput, calls=%fused_computation.34 | convolution fusion | flops 68157440 | bytes 1344000 | tf_op jit(solution)/shard_map/rena,ekai->rekni/dot_general | solution.py:81
  52.7 0.2 slice.35
  52.9 1.9 %fusion.42 = f32[4,32,2,8,128]{4,3,0,2,1:T(8,128)} fusion(s32[32,2,128]{2,1,0:T(2,128)S(1)} %iota_add_fusion, f32[4,32,2,1,128]{4,3,0,2,1:T(1,128)S(1)} %bitcast.150, f32[4,32,2,7,128]{4,3,0,2,1:T(8,128)S(1)} %slice.35, bf16[4,32,8,128]{3,2,1,0:T(8,128)(2,1)S(1)} %bitcast.148), kind=kOutput, calls=%fused_computation.38 | convolution fusion | flops 68943872 | bytes 2392064 | tf_op jit(solution)/shard_map/rena,ekai->rekni/dot_general | solution.py:80
  54.8 1.6 %reshape.118 = f32[4,64,1024]{2,0,1:T(4,128)S(1)} reshape(f32[4,32,2,8,128]{4,3,0,2,1:T(8,128)} %fusion.42) | data formatting | bytes 2097152 | tf_op jit(solution)/shard_map/mul | solution.py:447
  56.3 0.7 fusion.54.u_ref
  57.0 22.0 %shard_map.93 = bf16[128,2,1024]{2,1,0:T(2,128)(2,1)S(1)} custom-call(bf16[4,64,1024]{2,1,0:T(8,128)(2,1)S(1)} %fusion.54.u_ref, bf16[256,512]{1,0:T(8,128)(2,1)S(1)} %pad_maximum_fusion.1.refs_0_, bf16[1536,256]{1,0:T(8,128)(2,1)S(1)} %copy-done, bf16[128,128]{1,0:T(8,128)(2,1)S(1)} %copy-done.4, bf16[128,128]{1,0:T(8,128)(2,1)S(1)} %copy-done.3, ...), custom_call_target="tpu_custom_call" | custom-call | tf_op jit(solution)/shard_map/pallas_call | solution.py:315
  79.0 0.8 copy.108
  (18 shorter events, 0.2 us)
Async XLA Ops:
  0.0 28.0 %copy-start.8 = (s32[32,2]{0,1:T(2,128)S(1)}, s32[32,2]{0,1:T(2,128)}, u32[]{:S(2)}) copy-start(s32[32,2]{0,1:T(2,128)} %param.10) | copy-start | bytes 772
  0.0 31.4 %copy-start.9 = (f32[2,64]{1,0:T(2,128)S(1)}, f32[2,64]{1,0:T(2,128)}, u32[]{:S(2)}) copy-start(f32[2,64]{1,0:T(2,128)} %param.11) | copy-start | bytes 1540
  25.0 8.3 %collective-permute-start = (f32[4,32,128]{2,1,0:T(8,128)S(1)}, f32[4,32,128]{2,1,0:T(8,128)S(1)}, u32[]{:S(2)}, u32[]{:S(2)}) collective-permute-start(f32[4,32,128]{2,1,0:T(8,128)S(1)} %slice.25), channel_id=1, source_target_pairs={{1,0},{2,1},{3,2},{4,3},{5,4},{6,5},{7,6},{9,8},{10,9},{11,10},{12... | collective-permute-start | bytes 196616 | tf_op jit(solution)/shard_map/ppermute | solution.py:26
  35.1 1.1 %copy-start = (bf16[1536,256]{1,0:T(8,128)(2,1)S(1)}, bf16[1536,256]{1,0:T(8,128)(2,1)}, u32[]{:S(2)}) copy-start(bf16[1536,256]{1,0:T(8,128)(2,1)} %constant.53.refs_1_) | copy-start | bytes 2359300
  35.1 1.1 %copy-start.1 = (bf16[128,128]{1,0:T(8,128)(2,1)S(1)}, bf16[128,128]{1,0:T(8,128)(2,1)}, u32[]{:S(2)}) copy-start(bf16[128,128]{1,0:T(8,128)(2,1)} %constant.51.clone.refs_5_) | copy-start | bytes 98308
  35.1 1.1 %copy-start.2 = (bf16[128,128]{1,0:T(8,128)(2,1)S(1)}, bf16[128,128]{1,0:T(8,128)(2,1)}, u32[]{:S(2)}) copy-start(bf16[128,128]{1,0:T(8,128)(2,1)} %constant.50.clone.refs_4_) | copy-start | bytes 98308
  35.1 1.1 %copy-start.3 = (bf16[128,128]{1,0:T(8,128)(2,1)S(1)}, bf16[128,128]{1,0:T(8,128)(2,1)}, u32[]{:S(2)}) copy-start(bf16[128,128]{1,0:T(8,128)(2,1)} %constant.49.clone.refs_3_) | copy-start | bytes 98308
  35.2 1.1 %copy-start.4 = (bf16[128,128]{1,0:T(8,128)(2,1)S(1)}, bf16[128,128]{1,0:T(8,128)(2,1)}, u32[]{:S(2)}) copy-start(bf16[128,128]{1,0:T(8,128)(2,1)} %constant.48.clone.refs_2_) | copy-start | bytes 98308
  44.4 1.6 %copy-start.7 = (s32[64,128]{1,0:T(8,128)S(1)}, s32[64,128]{1,0:T(8,128)}, u32[]{:S(2)}) copy-start(s32[64,128]{1,0:T(8,128)} %get-tuple-element.13) | copy-start | bytes 98308
  46.9 0.8 copy-start.6
  48.8 1.1 %copy-start.5 = (f32[4,32,1024]{2,1,0:T(8,128)S(1)}, f32[4,32,1024]{2,1,0:T(8,128)}, u32[]{:S(2)}) copy-start(f32[4,32,1024]{2,1,0:T(8,128)} %shard_map.91) | copy-start | bytes 1572868

commit v8 on v7

--- a/solution.py
+++ b/solution.py
@@ -24,25 +24,6 @@
     count = lax.axis_size(axis)
     pairs = [(i, i + by) for i in range(count) if 0 <= i + by < count]
     return lax.ppermute(array, axis, pairs)
-
-
-def phase_table(length_first, length_second, period):
-    first_index = jnp.arange(length_first, dtype=jnp.int32)[:, None]
-    second_index = jnp.arange(length_second, dtype=jnp.int32)[None, :]
-    return (first_index * second_index % period).astype(jnp.float32) * (2.0 * math.pi / period)
-
-
-def make_tables():
-    time_angle = phase_table(WIN, WIN, WIN)
-    time_scale = 1.0 / math.sqrt(WIN)
-    cos_forward = jnp.cos(time_angle).astype(jnp.bfloat16)
-    sin_forward = -jnp.sin(time_angle).astype(jnp.bfloat16)
-    cos_inverse = jnp.cos(time_angle) * time_scale
-    sin_inverse = -jnp.sin(time_angle) * time_scale
-    source_angle = phase_table(SRC, SRC, SRC)
-    cos_source = jnp.cos(source_angle) / math.sqrt(SRC)
-    sin_source = jnp.sin(source_angle) / math.sqrt(SRC)
-    return (cos_forward, sin_forward, cos_inverse, sin_inverse, cos_source, sin_source)
 
 
 def blend(estimate, earlier, own_delays):
@@ -98,13 +79,11 @@
 
 
 def filter_tables():
-    time_angle = phase_table(WIN, WIN, WIN)
-    forward = jnp.concatenate(
-        [jnp.cos(time_angle).astype(jnp.bfloat16), -jnp.sin(time_angle).astype(jnp.bfloat16)],
-        axis=1,
-    )
     turn = lambda n: (np.arange(n)[:, None] * np.arange(n)[None, :] % n) * (2.0 * np.pi / n)
     time_turn = turn(WIN)
+    forward = jnp.asarray(
+        np.concatenate([np.cos(time_turn), -np.sin(time_turn)], axis=1).astype(ml_dtypes.bfloat16)
+    )
     inverse_high, inverse_low = exact_split(
         np.concatenate([np.cos(time_turn), -np.sin(time_turn)], axis=0) / math.sqrt(WIN)
     )

time: 80.8 us -> 79 us (0.978)
  other arithmetic: 5.95 us -> 3.95 us
    pallas_call x1, Pallas kernels: 22 us -> 23.7 us  [filter_and_send(): pl.pallas_call(functools.partial(filter_send_kernel, count, halves), in_s...]
    pallas_call x1, Pallas kernels: 7.67 us -> 6.36 us  [filter_with_halos(): pl.pallas_call(functools.partial(filter_halo_kernel, stages), in_specs=[v...]
    neg x1 -> x0, other arithmetic: 0.99 us -> none  [filter_tables(): -jnp.sin(time_angle).astype(jnp.bfloat16)]
    convert_element_type x1 -> x0, other arithmetic: 0.98 us -> none  [filter_tables(): jnp.cos(time_angle).astype(jnp.bfloat16)]
    unnamed x24 -> x26, local copies, waits for them, and re-layouts: 2.51 us -> 2.56 us
  transfers between devices with their start and end apart: 1 -> 1, of which waited for: 0 -> 0; matrix products, arithmetic and copies ran while one was open for 7% -> 4% of each run, Pallas kernels for 0% -> 0%
where the time goes in v8:
time: 79 us; the launch traced here: 78.1 us
  Pallas kernels  54.2 us (69%)
  matrix products  9.45 us (12%)
  local copies, waits for them, and re-layouts  7.25 us (9%)
  other arithmetic  3.95 us (5%)
  starting transfers between devices  2.95 us (4%)
    pallas_call x1, Pallas kernels, exchange(): pl.pallas_call(functools.partial(exchange_kernel, count, outgoing, incomi...  24.1 us
    pallas_call x1, Pallas kernels, filter_and_send(): pl.pallas_call(functools.partial(filter_send_kernel, count, halves), in_s...  23.7 us
    pallas_call x1, Pallas kernels, filter_with_halos(): pl.pallas_call(functools.partial(filter_halo_kernel, stages), in_specs=[v...  6.36 us
    ppermute x1, starting transfers between devices, shifted(): return lax.ppermute(array, axis, pairs)  2.95 us
    dot_general x2, matrix products, spread(): jnp.einsum('rena,ekai->rekni', lower, select_same, preferred_element_type...  2.81 us
    unnamed x26, local copies, waits for them, and re-layouts  2.56 us
    dot_general x2, matrix products, spread(): jnp.einsum('rena,ekai->rekni', lower, select_next, preferred_element_type...  1.63 us
    dot_general x1, matrix products, blend(): jnp.einsum('rsb,sbi->rsi', earlier, select_prior, preferred_element_type=...  1.6 us
  transfers between devices with their start and end apart: 1, of which 0 were waited for; matrix products, arithmetic and copies ran while one was open for 4% of the time, Pallas kernels for 0%

profile of v8, /device:TPU:3, one launch (start us, length us, event | category | flops | bytes accessed | tf_op | source)
XLA Modules:
  0.0 78.1 jit_solution(6382367950624057914)
XLA Ops:
  0.0 24.1 %shard_map.100 = f32[4,32,1024]{2,1,0:T(8,128)} custom-call(f32[128,1,1024]{2,1,0:T(1,128)} %src_ref.1), custom_call_target="tpu_custom_call" | custom-call | tf_op jit(solution)/shard_map/pallas_call | solution.py:370
  24.1 0.8 %slice.25 = f32[4,32,128]{2,1,0:T(8,128)S(1)} slice(f32[4,32,1024]{2,1,0:T(8,128)} %shard_map.100), slice={[0:4], [0:32], [0:128]} | slice | bytes 131072 | tf_op jit(solution)/shard_map/slice | solution.py:415
  25.0 2.9 %collective-permute-start = (f32[4,32,128]{2,1,0:T(8,128)S(1)}, f32[4,32,128]{2,1,0:T(8,128)S(1)}, u32[]{:S(2)}, u32[]{:S(2)}) collective-permute-start(f32[4,32,128]{2,1,0:T(8,128)S(1)} %slice.25), channel_id=1, source_target_pairs={{1,0},{2,1},{3,2},{4,3},{5,4},{6,5},{7,6},{9,8},{10,9},{11,10},{12... | collective-permute-start | bytes 196616 | tf_op jit(solution)/shard_map/ppermute | solution.py:26
  27.9 0.0 copy-done.9
  27.9 0.1 copy.41
  28.0 0.1 sub.40
  28.1 0.1 iota_add_fusion
  28.2 1.1 %convert_element_type.26 = bf16[4,32,1024]{2,1,0:T(8,128)(2,1)S(1)} convert(f32[4,32,1024]{2,1,0:T(8,128)} %shard_map.100) | non-fusion elementwise | flops 131072 | bytes 786432 | tf_op jit(solution)/shard_map/convert_element_type | solution.py:416
  29.4 0.7 broadcast_subtract_fusion
  30.1 0.8 %fusion.31 = f32[4,32,2,8,128]{4,3,0,2,1:T(8,128)S(1)} fusion(s32[32,2,128]{2,1,0:T(2,128)S(1)} %iota_add_fusion, s32[128]{0:T(128)S(1)} %iota_add_fusion.1, bf16[4,32,8,128]{3,2,1,0:T(8,128)(2,1)S(1)} %bitcast.145), kind=kOutput, calls=%fused_computation.33 | convolution fusion | flops 68157440 | bytes 1344000 | tf_op jit(solution)/shard_map/rena,ekai->rekni/dot_general | solution.py:62
  30.9 0.0 copy-done.10
  30.9 0.1 copy.56.refs_6_
  31.0 0.1 copy.46.refs_6_
  31.1 0.1 slice.32
  31.2 0.0 collective-permute-done
  31.3 0.8 %fusion.2 = f32[32,2,128,4]{2,3,1,0:T(4,128)S(1)} fusion(s32[32,2,128]{2,1,0:T(2,128)S(1)} %iota_add_fusion, s32[128]{0:T(128)S(1)} %iota_add_fusion.1, bf16[4,32,128,1]{2,1,0,3:T(8,128)(2,1)S(1)} %convert_bitcast_fusion), kind=kOutput, calls=%fused_computation.2 | convolution fusion | flops 9437184 | bytes 197120 | tf_op jit(solution)/shard_map/rea,ekai->reki/dot_general | solution.py:65
  32.1 0.9 %fusion.51 = bf16[4,32,2,8,128]{4,3,0,2,1:T(8,128)(2,1)S(1)} fusion(s32[32,2,128]{2,1,0:T(2,128)S(1)} %iota_add_fusion, f32[4,32,2,1,128]{4,3,0,2,1:T(1,128)S(1)} %bitcast.151, f32[4,32,2,7,128]{4,3,0,2,1:T(8,128)S(1)} %slice.32, bf16[4,32,8,128]{3,2,1,0:T(8,128)(2,1)S(1)} %bitcast.146), kind=kOutput, calls=%fused_computation.41 | convolution fusion | flops 69206016 | bytes 1867776 | tf_op jit(solution)/shard_map/rena,ekai->rekni/dot_general | solution.py:61
  33.0 0.0 copy-start
  33.0 0.0 copy-start.1
  33.0 0.0 copy-start.2
  33.0 0.0 copy-start.3
  33.1 0.0 copy-start.4
  33.1 0.0 copy-start.5
  33.1 0.1 reshape.116
  33.2 0.2 copy.73.u_ref
  33.4 0.8 copy-done
  34.1 0.1 copy-done.1
  34.2 0.0 copy-done.3
  34.2 6.4 %shard_map.101 = (bf16[4,64,1024]{2,1,0:T(8,128)(2,1)S(1)}, bf16[4,64,128]{2,1,0:T(8,128)(2,1)S(1)}, bf16[4,64,128]{2,1,0:T(8,128)(2,1)S(1)}) custom-call(bf16[4,64,1024]{2,1,0:T(8,128)(2,1)S(1)} %copy.73.u_ref, bf16[256,512]{1,0:T(8,128)(2,1)S(1)} %copy-done.1, bf16[1536,256]{1,0:T(8,128)(2,1)S(1)} %copy-done, bf16[128,128]{1,0:T(8,128)(2,1)S(1)} %copy-done.5, ...), custom_call_target="tpu_custom_call" | custom-call | tf_op jit(solution)/shard_map/pallas_call | solution.py:218
  40.6 0.1 pad_maximum_fusion
  40.7 0.3 reshape.101
  41.0 0.0 copy-start.8
  41.0 1.6 %bitcast_reduce_fusion.2 = f32[4,32,128]{2,0,1:T(4,128)S(1)} fusion(bf16[4,64,128]{2,1,0:T(8,128)(2,1)S(1)} %get-tuple-element.15, s32[64,128]{1,0:T(8,128)} %get-tuple-element.13), kind=kOutput, calls=%fused_computation.56 | convolution fusion | flops 9453568 | bytes 163840 | tf_op jit(solution)/shard_map/rsb,sbi->rsi/dot_general | solution.py:41
  42.6 0.9 %bitcast_reduce_fusion = f32[4,32,9,128]{3,2,0,1:T(8,128)S(1)} fusion(s32[64,128]{1,0:T(8,128)S(1)} %copy-done.8, bf16[4,64,9,128]{3,2,1,0:T(8,128)(2,1)S(1)} %reshape.101), kind=kOutput, calls=%fused_computation.18 | convolution fusion | flops 76693504 | bytes 1212416 | tf_op jit(solution)/shard_map/rsnb,sbi->rsni/dot_general | solution.py:40
  43.6 0.7 copy-done.7
  44.3 0.9 %bitcast_reduce_fusion.1 = f32[4,32,9,128]{3,2,0,1:T(8,128)S(1)} fusion(s32[64,128]{1,0:T(8,128)S(1)} %copy-done.7, bf16[4,64,9,128]{3,2,1,0:T(8,128)(2,1)S(1)} %reshape.101), kind=kOutput, calls=%fused_computation.19 | convolution fusion | flops 76693504 | bytes 1212416 | tf_op jit(solution)/shard_map/rsnb,sbi->rsni/dot_general | solution.py:39
  45.2 0.2 maximum_add_fusion
  45.4 1.0 %reshape.117 = f32[4,32,1152]{2,0,1:T(4,128)} reshape(f32[4,32,9,128]{3,2,0,1:T(8,128)S(1)} %maximum_add_fusion) | data formatting | bytes 1179648 | tf_op jit(solution)/shard_map/add | solution.py:48
  46.4 0.0 copy-done.6
  46.4 1.1 %fusion.61 = bf16[4,32,1152]{2,1,0:T(8,128)(2,1)S(1)} fusion(f32[4,32,128]{2,1,0:T(8,128)S(1)} %collective-permute-done, f32[4,32,1024]{2,1,0:T(8,128)S(1)} %copy-done.6, f32[4,32,1152]{2,0,1:T(4,128)} %reshape.117), kind=kLoop, calls=%fused_computation.48 | loop fusion | flops 442368 | bytes 1474560 | tf_op jit(solution)/shard_map/convert_element_type | solution.py:423
  47.7 0.8 %fusion = f32[32,2,128,4]{2,3,1,0:T(4,128)S(1)} fusion(s32[32,2,128]{2,1,0:T(2,128)S(1)} %iota_add_fusion, s32[128]{0:T(128)S(1)} %iota_add_fusion.1, bf16[4,32,128,1]{2,1,0,3:T(8,128)(2,1)S(1)} %fusion.69), kind=kOutput, calls=%fused_computation | convolution fusion | flops 9437184 | bytes 197120 | tf_op jit(solution)/shard_map/rea,ekai->reki/dot_general | solution.py:65
  48.5 0.8 %fusion.32 = f32[4,32,2,8,128]{4,3,0,2,1:T(8,128)S(1)} fusion(s32[32,2,128]{2,1,0:T(2,128)S(1)} %iota_add_fusion, s32[128]{0:T(128)S(1)} %iota_add_fusion.1, bf16[4,32,8,128]{3,2,1,0:T(8,128)(2,1)S(1)} %bitcast.147), kind=kOutput, calls=%fused_computation.34 | convolution fusion | flops 68157440 | bytes 1344000 | tf_op jit(solution)/shard_map/rena,ekai->rekni/dot_general | solution.py:62
  49.3 0.2 slice.35
  49.5 1.9 %fusion.42 = f32[4,32,2,8,128]{4,3,0,2,1:T(8,128)} fusion(s32[32,2,128]{2,1,0:T(2,128)S(1)} %iota_add_fusion, f32[4,32,2,1,128]{4,3,0,2,1:T(1,128)S(1)} %bitcast.150, f32[4,32,2,7,128]{4,3,0,2,1:T(8,128)S(1)} %slice.35, bf16[4,32,8,128]{3,2,1,0:T(8,128)(2,1)S(1)} %bitcast.148), kind=kOutput, calls=%fused_computation.38 | convolution fusion | flops 68943872 | bytes 2392064 | tf_op jit(solution)/shard_map/rena,ekai->rekni/dot_general | solution.py:61
  51.4 1.6 %reshape.118 = f32[4,64,1024]{2,0,1:T(4,128)S(1)} reshape(f32[4,32,2,8,128]{4,3,0,2,1:T(8,128)} %fusion.42) | data formatting | bytes 2097152 | tf_op jit(solution)/shard_map/mul | solution.py:426
  52.9 0.7 fusion.54.u_ref
  53.6 23.7 %shard_map.102 = bf16[128,2,1024]{2,1,0:T(2,128)(2,1)S(1)} custom-call(bf16[4,64,1024]{2,1,0:T(8,128)(2,1)S(1)} %fusion.54.u_ref, bf16[256,512]{1,0:T(8,128)(2,1)S(1)} %copy-done.1, bf16[1536,256]{1,0:T(8,128)(2,1)S(1)} %copy-done, bf16[128,128]{1,0:T(8,128)(2,1)S(1)} %copy-done.5, bf16[128,128]{1,0:T(8,128)(2,1)S(1)} %copy-done.4, ...), custom_call_target="tpu_custom_call" | custom-call | tf_op jit(solution)/shard_map/pallas_call | solution.py:294
  77.3 0.8 %copy.109 = bf16[128,2,1024]{2,1,0:T(2,128)(2,1)} copy(bf16[128,2,1024]{2,1,0:T(2,128)(2,1)S(1)} %shard_map.102) | data formatting | bytes 1048576
  (17 shorter events, 0.2 us)
Async XLA Ops:
  0.0 27.9 %copy-start.9 = (s32[32,2]{0,1:T(2,128)S(1)}, s32[32,2]{0,1:T(2,128)}, u32[]{:S(2)}) copy-start(s32[32,2]{0,1:T(2,128)} %param.11) | copy-start | bytes 772
  25.0 6.3 %collective-permute-start = (f32[4,32,128]{2,1,0:T(8,128)S(1)}, f32[4,32,128]{2,1,0:T(8,128)S(1)}, u32[]{:S(2)}, u32[]{:S(2)}) collective-permute-start(f32[4,32,128]{2,1,0:T(8,128)S(1)} %slice.25), channel_id=1, source_target_pairs={{1,0},{2,1},{3,2},{4,3},{5,4},{6,5},{7,6},{9,8},{10,9},{11,10},{12... | collective-permute-start | bytes 196616 | tf_op jit(solution)/shard_map/ppermute | solution.py:26
  30.1 0.8 %copy-start.10 = (f32[2,64]{1,0:T(2,128)S(1)}, f32[2,64]{1,0:T(2,128)}, u32[]{:S(2)}) copy-start(f32[2,64]{1,0:T(2,128)} %param.12) | copy-start | bytes 1540
  33.0 1.1 %copy-start = (bf16[1536,256]{1,0:T(8,128)(2,1)S(1)}, bf16[1536,256]{1,0:T(8,128)(2,1)}, u32[]{:S(2)}) copy-start(bf16[1536,256]{1,0:T(8,128)(2,1)} %constant.40.refs_1_) | copy-start | bytes 2359300
  33.0 1.2 %copy-start.1 = (bf16[256,512]{1,0:T(8,128)(2,1)S(1)}, bf16[256,512]{1,0:T(8,128)(2,1)}, u32[]{:S(2)}) copy-start(bf16[256,512]{1,0:T(8,128)(2,1)} %constant.12.clone.refs_0_) | copy-start | bytes 786436
  33.0 1.2 %copy-start.2 = (bf16[128,128]{1,0:T(8,128)(2,1)S(1)}, bf16[128,128]{1,0:T(8,128)(2,1)}, u32[]{:S(2)}) copy-start(bf16[128,128]{1,0:T(8,128)(2,1)} %constant.38.clone.refs_5_) | copy-start | bytes 98308
  33.0 1.2 %copy-start.3 = (bf16[128,128]{1,0:T(8,128)(2,1)S(1)}, bf16[128,128]{1,0:T(8,128)(2,1)}, u32[]{:S(2)}) copy-start(bf16[128,128]{1,0:T(8,128)(2,1)} %constant.37.clone.refs_4_) | copy-start | bytes 98308
  33.1 1.1 %copy-start.4 = (bf16[128,128]{1,0:T(8,128)(2,1)S(1)}, bf16[128,128]{1,0:T(8,128)(2,1)}, u32[]{:S(2)}) copy-start(bf16[128,128]{1,0:T(8,128)(2,1)} %constant.36.clone.refs_3_) | copy-start | bytes 98308
  33.1 1.1 %copy-start.5 = (bf16[128,128]{1,0:T(8,128)(2,1)S(1)}, bf16[128,128]{1,0:T(8,128)(2,1)}, u32[]{:S(2)}) copy-start(bf16[128,128]{1,0:T(8,128)(2,1)} %constant.35.clone.refs_2_) | copy-start | bytes 98308
  41.0 1.6 %copy-start.8 = (s32[64,128]{1,0:T(8,128)S(1)}, s32[64,128]{1,0:T(8,128)}, u32[]{:S(2)}) copy-start(s32[64,128]{1,0:T(8,128)} %get-tuple-element.13) | copy-start | bytes 98308
  43.5 0.8 copy-start.7
  45.4 1.0 %copy-start.6 = (f32[4,32,1024]{2,1,0:T(8,128)S(1)}, f32[4,32,1024]{2,1,0:T(8,128)}, u32[]{:S(2)}) copy-start(f32[4,32,1024]{2,1,0:T(8,128)} %shard_map.100) | copy-start | bytes 1572868

commit v9 on v8

--- a/solution.py
+++ b/solution.py
@@ -148,13 +148,35 @@
         out_ref[r, :, w * WIN : (w + 1) * WIN] = restored[block(g)].astype(out_ref.dtype)
 
 
+def spread_update(res_ref, shift_ref, dup_ref, est_ref, u_ref):
+    receivers, sources, samples = u_ref.shape
+    width = res_ref.shape[2]
+    shift = shift_ref[...]
+    for r in range(receivers):
+        moved = jnp.dot(dup_ref[...], res_ref[r], preferred_element_type=jnp.float32)
+        for bit in range((BLK - 1).bit_length()):
+            amount = 1 << bit
+            rolled = pltpu.roll(moved, width - amount, 1)
+            moved = jnp.where((shift & amount) != 0, rolled, moved)
+        value = RELAX * moved[:, :samples]
+        if est_ref is not None:
+            value = est_ref[r].astype(jnp.float32) + value
+        u_ref[r] = value.astype(u_ref.dtype)
+
+
+def spread_inputs(residual, delays):
+    experiments = residual.shape[1]
+    dup = (np.arange(experiments * SRC_EXP)[:, None] // SRC_EXP == np.arange(experiments)[None, :])
+    return [residual, delays.reshape(-1, 1), jnp.asarray(dup.astype(ml_dtypes.bfloat16))]
+
+
 def filter_kernel(u_ref, *refs):
     filter_block(u_ref, 0, u_ref.shape[0], refs[:7], refs[7])
 
 
-def filter_halo_kernel(stages, u_ref, *refs):
+def filter_halo_kernel(stages, res_ref, shift_ref, dup_ref, *refs):
     tables = refs[:7]
-    out_ref, before_ref, after_ref, send_sem, recv_sem = refs[7:]
+    out_ref, before_ref, after_ref, u_ref, send_sem, recv_sem = refs[7:]
     samples = u_ref.shape[2]
     shot = lax.axis_index("shot")
     row = lax.axis_index("tm")
@@ -171,6 +193,7 @@
     def _():
         pl.semaphore_signal(barrier, 1, device_id=(shot, row + 1), device_id_type=mesh_id)
 
+    spread_update(res_ref, shift_ref, dup_ref, None, u_ref)
     filter_block(u_ref, 0, u_ref.shape[0], tables, out_ref)
     pl.semaphore_wait(barrier, has_prev.astype(jnp.int32) + has_next.astype(jnp.int32))
 
@@ -208,28 +231,37 @@
         to_prev().wait_recv()
 
 
-def filter_with_halos(gathers, limits, tables):
+def filter_with_halos(residual, delays, limits, tables):
     forward, inverse, mix_forward, mix_inverse = tables
-    receivers, sources, samples = gathers.shape
+    receivers = residual.shape[0]
+    sources = delays.size
+    samples = residual.shape[2] - BLK
     stages = lax.axis_size("tm")
     vmem = pl.BlockSpec(memory_space=pltpu.VMEM)
     anywhere = pl.BlockSpec(memory_space=pl.ANY)
     edge = jax.ShapeDtypeStruct((receivers, sources, BLK), jnp.bfloat16)
     return pl.pallas_call(
         functools.partial(filter_halo_kernel, stages),
-        in_specs=[vmem] * 8,
+        in_specs=[vmem] * 10,
         out_specs=(vmem, anywhere, anywhere),
-        out_shape=(jax.ShapeDtypeStruct(gathers.shape, jnp.bfloat16), edge, edge),
-        scratch_shapes=[pltpu.SemaphoreType.DMA((2,)), pltpu.SemaphoreType.DMA((2,))],
+        out_shape=(jax.ShapeDtypeStruct((receivers, sources, samples), jnp.bfloat16), edge, edge),
+        scratch_shapes=[
+            pltpu.VMEM((receivers, sources, samples), jnp.bfloat16),
+            pltpu.SemaphoreType.DMA((2,)),
+            pltpu.SemaphoreType.DMA((2,)),
+        ],
         compiler_params=pltpu.CompilerParams(
             collective_id=3, has_side_effects=True, vmem_limit_bytes=48 * 1024 * 1024
         ),
-    )(gathers, forward, inverse, *mix_forward, *mix_inverse, limits.reshape(sources, 1))
-
-
-def filter_send_kernel(count, halves, u_ref, *refs):
+    )(
+        *spread_inputs(residual, delays),
+        forward, inverse, *mix_forward, *mix_inverse, limits.reshape(sources, 1),
+    )
+
+
+def filter_send_kernel(count, halves, est_ref, res_ref, shift_ref, dup_ref, *refs):
     tables = refs[:7]
-    out_ref, done_ref, send_sem, recv_sem, own_sem = refs[7:]
+    out_ref, done_ref, u_ref, send_sem, recv_sem, own_sem = refs[7:]
     receivers, sources, samples = u_ref.shape
     own = sources // count
     per = receivers // halves
@@ -243,6 +275,7 @@
         return carry
 
     lax.fori_loop(1, count, greet, 0)
+    spread_update(res_ref, shift_ref, dup_ref, est_ref, u_ref)
 
     def remote(half, peer, sender):
         return pltpu.make_async_remote_copy(
@@ -285,21 +318,22 @@
         locals_[half].wait()
 
 
-def filter_and_send(gathers, limits, tables):
+def filter_and_send(estimate, residual, delays, limits, tables):
     forward, inverse, mix_forward, mix_inverse = tables
-    receivers, sources, samples = gathers.shape
+    receivers, sources, samples = estimate.shape
     count = lax.axis_size("shot")
     halves = 2
     vmem = pl.BlockSpec(memory_space=pltpu.VMEM)
     return pl.pallas_call(
         functools.partial(filter_send_kernel, count, halves),
-        in_specs=[vmem] * 8,
+        in_specs=[vmem] * 11,
         out_specs=pl.BlockSpec(memory_space=pl.ANY),
         out_shape=jax.ShapeDtypeStruct(
             (receivers * count, sources // count, samples), jnp.bfloat16
         ),
         scratch_shapes=[
-            pltpu.VMEM(gathers.shape, jnp.bfloat16),
+            pltpu.VMEM(estimate.shape, jnp.bfloat16),
+            pltpu.VMEM(estimate.shape, jnp.bfloat16),
             pltpu.SemaphoreType.DMA((halves, count)),
             pltpu.SemaphoreType.DMA((halves, count)),
             pltpu.SemaphoreType.DMA((halves,)),
@@ -307,7 +341,11 @@
         compiler_params=pltpu.CompilerParams(
             collective_id=2, has_side_effects=True, vmem_limit_bytes=48 * 1024 * 1024
         ),
-    )(gathers, forward, inverse, *mix_forward, *mix_inverse, limits.reshape(sources, 1))
+    )(
+        estimate,
+        *spread_inputs(residual, delays),
+        forward, inverse, *mix_forward, *mix_inverse, limits.reshape(sources, 1),
+    )
 
 
 def coherence(gathers, limits, tables):
@@ -413,19 +451,18 @@
     samples = records.shape[2]
     row = lax.axis_index("tm")
     following = shifted(records[:, :, :BLK], "tm", -1)
-    residual = records.astype(jnp.bfloat16)
-    update = (RELAX * spread(residual, following.astype(jnp.bfloat16), delays)).astype(jnp.bfloat16)
-    estimate, before, after = filter_with_halos(update, thresholds[0], tables)
+    extended = jnp.concatenate([records, following], axis=2)
+    estimate, before, after = filter_with_halos(
+        extended.astype(jnp.bfloat16), delays, thresholds[0], tables
+    )
     before = jnp.where(row == 0, jnp.zeros_like(before), before)
     last = row == lax.axis_size("tm") - 1
     after = jnp.where(last, jnp.zeros_like(after), after)
     blended_part = blend(jnp.concatenate([estimate, after], axis=2), before, delays)
-    residual = (jnp.concatenate([records, following], axis=2) - blended_part).astype(jnp.bfloat16)
-    tail = jnp.where(last, jnp.zeros_like(residual[:, :, samples:]), residual[:, :, samples:])
-    update = (
-        estimate.astype(jnp.float32) + RELAX * spread(residual[:, :, :samples], tail, delays)
-    ).astype(jnp.bfloat16)
-    return filter_and_send(update, thresholds[1], tables)
+    residual = (extended - blended_part).astype(jnp.bfloat16)
+    keep = jnp.logical_or(jnp.arange(samples + BLK) < samples, jnp.logical_not(last))
+    residual = jnp.where(keep[None, None, :], residual, jnp.zeros_like(residual))
+    return filter_and_send(estimate, residual, delays, thresholds[1], tables)
 
 
 def solution(mesh):

time: 79 us -> 74.8 us (0.947)
  matrix products: 9.45 us -> 3.47 us
  Pallas kernels: 54.2 us -> 58.7 us
  local copies, waits for them, and re-layouts: 7.25 us -> 5.19 us
    dot_general x6 -> x0, matrix products: 6.04 us -> none  [the longest x2 2.81 us: spread(): jnp.einsum('rena,ekai->rekni', lower, select_same, preferred_element_type...]
    pallas_call x1, Pallas kernels: 6.36 us -> 9.19 us  [filter_with_halos(): pl.pallas_call(functools.partial(filter_halo_kernel, stages), in_specs=[v...]
    convert_element_type x4 -> x1, other arithmetic: 2.87 us -> 1.08 us  [local(): extended.astype(jnp.bfloat16)]
    mul x1 -> x0, local copies, waits for them, and re-layouts: 1.56 us -> none  [local(): RELAX * spread(residual[:, :, :samples], tail, delays)]
    pallas_call x1, Pallas kernels: 23.7 us -> 25.1 us  [filter_and_send(): pl.pallas_call(functools.partial(filter_send_kernel, count, halves), in_s...]
    select_n x1, other arithmetic: 0.01 us -> 1.14 us  [local(): jnp.where(keep[None, None, :], residual, jnp.zeros_like(residual))]
    dot_general x1, matrix products: 0.91 us -> 1.76 us  [blend(): jnp.einsum('rsnb,sbi->rsni', upper, select_prior, preferred_element_type=...]
    dot_general x1, matrix products: 1.6 us -> 0.8 us  [blend(): jnp.einsum('rsb,sbi->rsi', earlier, select_prior, preferred_element_type=...]
  transfers between devices with their start and end apart: 1 -> 1, of which waited for: 0 -> 0; matrix products, arithmetic and copies ran while one was open for 4% -> 3% of each run, Pallas kernels for 0% -> 0%
where the time goes in v9:
time: 74.8 us; the launch traced here: 74.4 us
  Pallas kernels  58.7 us (78%)
  local copies, waits for them, and re-layouts  5.19 us (7%)
  other arithmetic  3.81 us (5%)
  matrix products  3.47 us (5%)
  starting transfers between devices  2.95 us (4%)
    pallas_call x1, Pallas kernels, filter_and_send(): pl.pallas_call(functools.partial(filter_send_kernel, count, halves), in_s...  25.1 us
    pallas_call x1, Pallas kernels, exchange(): pl.pallas_call(functools.partial(exchange_kernel, count, outgoing, incomi...  24.4 us
    pallas_call x1, Pallas kernels, filter_with_halos(): pl.pallas_call(functools.partial(filter_halo_kernel, stages), in_specs=[v...  9.19 us
    ppermute x1, starting transfers between devices, shifted(): return lax.ppermute(array, axis, pairs)  2.95 us
    unnamed x28, local copies, waits for them, and re-layouts  2.39 us
    dot_general x1, matrix products, blend(): jnp.einsum('rsnb,sbi->rsni', upper, select_prior, preferred_element_type=...  1.76 us
  transfers between devices with their start and end apart: 1, of which 0 were waited for; matrix products, arithmetic and copies ran while one was open for 3% of the time, Pallas kernels for 0%

profile of v9, /device:TPU:3, one launch (start us, length us, event | category | flops | bytes accessed | tf_op | source)
XLA Modules:
  0.0 74.4 jit_solution(7805973308815801569)
XLA Ops:
  0.0 0.0 copy-start
  0.0 0.0 copy-start.3
  0.0 0.0 copy-start.4
  0.0 0.0 copy-start.5
  0.0 0.0 copy-start.6
  0.1 0.0 copy-start.12
  0.1 24.4 %shard_map.118 = f32[4,32,1024]{2,1,0:T(8,128)} custom-call(f32[128,1,1024]{2,1,0:T(1,128)} %src_ref.1), custom_call_target="tpu_custom_call" | custom-call | tf_op jit(solution)/shard_map/pallas_call | solution.py:408
  24.4 0.8 %slice.12 = f32[4,32,128]{2,1,0:T(8,128)S(1)} slice(f32[4,32,1024]{2,1,0:T(8,128)} %shard_map.118), slice={[0:4], [0:32], [0:128]} | slice | bytes 131072 | tf_op jit(solution)/shard_map/slice | solution.py:453
  25.3 2.9 %collective-permute-start = (f32[4,32,128]{2,1,0:T(8,128)S(1)}, f32[4,32,128]{2,1,0:T(8,128)S(1)}, u32[]{:S(2)}, u32[]{:S(2)}) collective-permute-start(f32[4,32,128]{2,1,0:T(8,128)S(1)} %slice.12), channel_id=1, source_target_pairs={{1,0},{2,1},{3,2},{4,3},{5,4},{6,5},{7,6},{9,8},{10,9},{11,10},{12... | collective-permute-start | bytes 196616 | tf_op jit(solution)/shard_map/ppermute | solution.py:26
  28.2 0.8 %copy.31 = s32[32,2]{1,0:T(8,128)S(1)} copy(s32[32,2]{0,1:T(2,128)} %param.13) | data formatting | bytes 512 | tf_op args[1]
  29.0 0.1 reshape.91.shift_ref
  29.1 0.1 sub.40
  29.2 0.0 copy-done.12
  29.2 0.1 copy.33.refs_6_
  29.3 0.1 copy.40.refs_6_
  29.4 0.7 broadcast_subtract_fusion
  30.1 0.6 fusion.22
  30.7 0.0 collective-permute-done
  30.7 1.1 %fusion.17.res_ref = bf16[4,32,1152]{2,1,0:T(8,128)(2,1)S(1)} fusion(f32[4,32,128]{2,1,0:T(8,128)S(1)} %collective-permute-done, f32[4,32,1024]{2,1,0:T(8,128)} %shard_map.118), kind=kLoop, calls=%fused_computation.19 | loop fusion | flops 589824 | bytes 884736 | tf_op jit(solution)/shard_map/convert_element_type | solution.py:456
  31.8 0.0 copy-done
  31.8 0.0 copy-done.1
  31.8 0.0 copy-done.2
  31.8 0.0 copy-done.3
  31.8 0.0 copy-done.4
  31.8 0.0 copy-done.5
  31.8 0.0 copy-done.6
  31.8 9.2 %shard_map.119 = (bf16[4,64,1024]{2,1,0:T(8,128)(2,1)S(1)}, bf16[4,64,128]{2,1,0:T(8,128)(2,1)S(1)}, bf16[4,64,128]{2,1,0:T(8,128)(2,1)S(1)}) custom-call(bf16[4,32,1152]{2,1,0:T(8,128)(2,1)S(1)} %fusion.17.res_ref, s32[64,1]{1,0:T(8,128)S(1)} %reshape.91.shift_ref, bf16[64,32]{1,0:T(8,128)(2,1)S(1)} %copy-done.6, bf16[256,512]{1,0:T(8,128)(2,1)S(1)} %copy-done.1, ...), custom_call_target="tpu_custom_call" | custom-call | tf_op jit(solution)/shard_map/pallas_call | solution.py:243
  41.1 0.1 pad_maximum_fusion.1
  41.1 0.3 reshape.84
  41.5 1.8 %bitcast_reduce_fusion = f32[4,32,9,128]{3,2,0,1:T(8,128)S(1)} fusion(s32[64,128]{1,0:T(8,128)} %get-tuple-element.13, bf16[4,64,9,128]{3,2,1,0:T(8,128)(2,1)S(1)} %reshape.84), kind=kOutput, calls=%fused_computation.7 | convolution fusion | flops 76693504 | bytes 1212416 | tf_op jit(solution)/shard_map/rsnb,sbi->rsni/dot_general | solution.py:40
  43.2 0.0 copy-start.8
  43.2 0.0 copy-start.10
  43.3 0.8 %copy-done.10 = s32[64,128]{1,0:T(8,128)S(1)} copy-done((s32[64,128]{1,0:T(8,128)S(1)}, s32[64,128]{1,0:T(8,128)}, u32[]{:S(2)}) %copy-start.10) | copy-done | bytes 32792
  44.0 0.9 %bitcast_reduce_fusion.1 = f32[4,32,9,128]{3,2,0,1:T(8,128)S(1)} fusion(s32[64,128]{1,0:T(8,128)S(1)} %copy-done.10, bf16[4,64,9,128]{3,2,1,0:T(8,128)(2,1)S(1)} %reshape.84), kind=kOutput, calls=%fused_computation.8 | convolution fusion | flops 76693504 | bytes 1212416 | tf_op jit(solution)/shard_map/rsnb,sbi->rsni/dot_general | solution.py:39
  44.9 0.0 copy-done.8
  44.9 0.0 copy-done.9
  45.0 0.0 slice-start
  45.0 0.8 %bitcast_reduce_fusion.2 = f32[4,32,128]{2,0,1:T(4,128)S(1)} fusion(bf16[4,64,128]{2,1,0:T(8,128)(2,1)S(1)} %get-tuple-element.15, s32[64,128]{1,0:T(8,128)S(1)} %copy-done.9), kind=kOutput, calls=%fused_computation.21 | convolution fusion | flops 9453568 | bytes 163840 | tf_op jit(solution)/shard_map/rsb,sbi->rsi/dot_general | solution.py:41
  45.8 0.2 slice-done
  46.0 0.2 maximum_add_fusion
  46.2 0.0 copy-start.7
  46.2 0.0 copy-start.11
  46.3 1.0 %reshape.90 = f32[4,32,1152]{2,0,1:T(4,128)} reshape(f32[4,32,9,128]{3,2,0,1:T(8,128)S(1)} %maximum_add_fusion) | data formatting | bytes 1179648 | tf_op jit(solution)/shard_map/add | solution.py:48
  47.3 0.0 copy-done.7
  47.3 0.0 copy-done.11
  47.3 1.1 %fusion.18.res_ref = bf16[4,32,1152]{2,1,0:T(8,128)(2,1)S(1)} fusion(f32[4,32,1152]{2,0,1:T(4,128)} %reshape.90, f32[4,32,128]{2,1,0:T(8,128)S(1)} %collective-permute-done, f32[4,32,1024]{2,1,0:T(8,128)S(1)} %copy-done.7, pred[1152]{0:T(1024)(128)(4,1)S(1)} %copy-done.11), kind=kLoop, calls=%fused_computation.20 | loop fusion | flops 589824 | bytes 1475712 | tf_op jit(solution)/shard_map/jit(_where)/select_n | solution.py:464
  48.4 25.1 %shard_map.120 = bf16[128,2,1024]{2,1,0:T(2,128)(2,1)S(1)} custom-call(bf16[4,64,1024]{2,1,0:T(8,128)(2,1)S(1)} %get-tuple-element.8.est_ref, bf16[4,32,1152]{2,1,0:T(8,128)(2,1)S(1)} %fusion.18.res_ref, s32[64,1]{1,0:T(8,128)S(1)} %reshape.91.shift_ref, bf16[64,32]{1,0:T(8,128)(2,1)S(1)} %copy-done.6, bf16[256,512]{1,0:T(8,128)(2,1)S(1)} %copy-done.1, ...), custom_call_target="tpu_custom_call" | custom-call | tf_op jit(solution)/shard_map/pallas_call | solution.py:327
  73.6 0.8 %copy.58 = bf16[128,2,1024]{2,1,0:T(2,128)(2,1)} copy(bf16[128,2,1024]{2,1,0:T(2,128)(2,1)S(1)} %shard_map.120) | data formatting | bytes 1048576
  (6 shorter events, 0.0 us)
Async XLA Ops:
  0.0 31.8 %copy-start = (bf16[1536,256]{1,0:T(8,128)(2,1)S(1)}, bf16[1536,256]{1,0:T(8,128)(2,1)}, u32[]{:S(2)}) copy-start(bf16[1536,256]{1,0:T(8,128)(2,1)} %constant.42.refs_1_) | copy-start | bytes 2359300
  0.0 31.8 %copy-start.1 = (bf16[256,512]{1,0:T(8,128)(2,1)S(1)}, bf16[256,512]{1,0:T(8,128)(2,1)}, u32[]{:S(2)}) copy-start(bf16[256,512]{1,0:T(8,128)(2,1)} %constant.14.clone.refs_0_) | copy-start | bytes 786436
  0.0 31.8 %copy-start.2 = (bf16[128,128]{1,0:T(8,128)(2,1)S(1)}, bf16[128,128]{1,0:T(8,128)(2,1)}, u32[]{:S(2)}) copy-start(bf16[128,128]{1,0:T(8,128)(2,1)} %constant.36.clone.refs_2_) | copy-start | bytes 98308
  0.0 31.8 %copy-start.3 = (bf16[128,128]{1,0:T(8,128)(2,1)S(1)}, bf16[128,128]{1,0:T(8,128)(2,1)}, u32[]{:S(2)}) copy-start(bf16[128,128]{1,0:T(8,128)(2,1)} %constant.37.clone.refs_3_) | copy-start | bytes 98308
  0.0 31.8 %copy-start.4 = (bf16[128,128]{1,0:T(8,128)(2,1)S(1)}, bf16[128,128]{1,0:T(8,128)(2,1)}, u32[]{:S(2)}) copy-start(bf16[128,128]{1,0:T(8,128)(2,1)} %constant.38.clone.refs_4_) | copy-start | bytes 98308
  0.0 31.8 %copy-start.5 = (bf16[128,128]{1,0:T(8,128)(2,1)S(1)}, bf16[128,128]{1,0:T(8,128)(2,1)}, u32[]{:S(2)}) copy-start(bf16[128,128]{1,0:T(8,128)(2,1)} %constant.39.clone.refs_5_) | copy-start | bytes 98308
  0.0 31.8 %copy-start.6 = (bf16[64,32]{1,0:T(8,128)(2,1)S(1)}, bf16[64,32]{1,0:T(8,128)(2,1)}, u32[]{:S(2)}) copy-start(bf16[64,32]{1,0:T(8,128)(2,1)} %constant.40.clone.dup_ref) | copy-start | bytes 12292
  0.1 29.1 %copy-start.12 = (f32[2,64]{1,0:T(2,128)S(1)}, f32[2,64]{1,0:T(2,128)}, u32[]{:S(2)}) copy-start(f32[2,64]{1,0:T(2,128)} %param.14) | copy-start | bytes 1540
  25.3 5.4 %collective-permute-start = (f32[4,32,128]{2,1,0:T(8,128)S(1)}, f32[4,32,128]{2,1,0:T(8,128)S(1)}, u32[]{:S(2)}, u32[]{:S(2)}) collective-permute-start(f32[4,32,128]{2,1,0:T(8,128)S(1)} %slice.12), channel_id=1, source_target_pairs={{1,0},{2,1},{3,2},{4,3},{5,4},{6,5},{7,6},{9,8},{10,9},{11,10},{12... | collective-permute-start | bytes 196616 | tf_op jit(solution)/shard_map/ppermute | solution.py:26
  43.2 1.7 %copy-start.8 = (f32[4,32,9,128]{3,2,0,1:T(8,128)}, f32[4,32,9,128]{3,2,0,1:T(8,128)S(1)}, u32[]{:S(2)}) copy-start(f32[4,32,9,128]{3,2,0,1:T(8,128)S(1)} %bitcast_reduce_fusion) | copy-start | bytes 1769476
  43.2 0.8 %copy-start.10 = (s32[64,128]{1,0:T(8,128)S(1)}, s32[64,128]{1,0:T(8,128)}, u32[]{:S(2)}) copy-start(s32[64,128]{1,0:T(8,128)} %get-tuple-element.14) | copy-start | bytes 98308
  44.0 0.9 %copy-start.9 = (s32[64,128]{1,0:T(8,128)S(1)}, s32[64,128]{1,0:T(8,128)}, u32[]{:S(2)}) copy-start(s32[64,128]{1,0:T(8,128)} %get-tuple-element.13) | copy-start | bytes 98308
  45.0 1.0 %slice-start = ((f32[4,32,9,128]{3,2,0,1:T(8,128)}), f32[4,32,8,128]{3,2,0,1:T(8,128)S(1)}, s32[]{:S(2)}) async-start(f32[4,32,9,128]{3,2,0,1:T(8,128)} %copy-done.8), calls=%async_computation | async-start | bytes 1048576 | tf_op jit(solution)/shard_map/slice | solution.py:47
  46.2 1.0 %copy-start.7 = (f32[4,32,1024]{2,1,0:T(8,128)S(1)}, f32[4,32,1024]{2,1,0:T(8,128)}, u32[]{:S(2)}) copy-start(f32[4,32,1024]{2,1,0:T(8,128)} %shard_map.118) | copy-start | bytes 1572868
  46.2 1.0 %copy-start.11 = (pred[1152]{0:T(1024)(128)(4,1)S(1)}, pred[1152]{0:T(1024)(128)(4,1)}, u32[]{:S(2)}) copy-start(pred[1152]{0:T(1024)(128)(4,1)} %fusion.22) | copy-start | bytes 3460

commit v10 on v9

--- a/solution.py
+++ b/solution.py
@@ -148,6 +148,25 @@
         out_ref[r, :, w * WIN : (w + 1) * WIN] = restored[block(g)].astype(out_ref.dtype)
 
 
+def blend_residual(rec_ref, est_ref, before_ref, after_ref, shift_ref, pair_ref, last, res_ref):
+    receivers, experiments, width = rec_ref.shape
+    shift = shift_ref[...]
+    lane = lax.broadcasted_iota(jnp.int32, (experiments, width), 1)
+    drop = jnp.logical_and(lane >= width - BLK, last)
+    for r in range(receivers):
+        moved = jnp.concatenate([before_ref[r], est_ref[r], after_ref[r]], axis=1).astype(jnp.float32)
+        full = moved.shape[1]
+        for bit in range((BLK - 1).bit_length()):
+            amount = 1 << bit
+            moved = jnp.where((shift & amount) != 0, pltpu.roll(moved, amount, 1), moved)
+        summed = jnp.dot(
+            pair_ref[...], moved[:, full - width :].astype(jnp.bfloat16),
+            preferred_element_type=jnp.float32,
+        )
+        residual = (rec_ref[r] - summed).astype(res_ref.dtype)
+        res_ref[r] = jnp.where(drop, jnp.zeros_like(residual), residual)
+
+
 def spread_update(res_ref, shift_ref, dup_ref, est_ref, u_ref):
     receivers, sources, samples = u_ref.shape
     width = res_ref.shape[2]
@@ -164,10 +183,13 @@
         u_ref[r] = value.astype(u_ref.dtype)
 
 
+def pairing(experiments):
+    source = np.arange(experiments * SRC_EXP)[:, None] // SRC_EXP
+    return (source == np.arange(experiments)[None, :]).astype(ml_dtypes.bfloat16)
+
+
 def spread_inputs(residual, delays):
-    experiments = residual.shape[1]
-    dup = (np.arange(experiments * SRC_EXP)[:, None] // SRC_EXP == np.arange(experiments)[None, :])
-    return [residual, delays.reshape(-1, 1), jnp.asarray(dup.astype(ml_dtypes.bfloat16))]
+    return [residual, delays.reshape(-1, 1), jnp.asarray(pairing(residual.shape[1]))]
 
 
 def filter_kernel(u_ref, *refs):
@@ -259,9 +281,11 @@
     )
 
 
-def filter_send_kernel(count, halves, est_ref, res_ref, shift_ref, dup_ref, *refs):
+def filter_send_kernel(
+    count, stages, halves, est_ref, before_ref, after_ref, rec_ref, pair_ref, shift_ref, dup_ref, *refs
+):
     tables = refs[:7]
-    out_ref, done_ref, u_ref, send_sem, recv_sem, own_sem = refs[7:]
+    out_ref, done_ref, u_ref, res_ref, send_sem, recv_sem, own_sem = refs[7:]
     receivers, sources, samples = u_ref.shape
     own = sources // count
     per = receivers // halves
@@ -275,6 +299,8 @@
         return carry
 
     lax.fori_loop(1, count, greet, 0)
+    last = lax.axis_index("tm") == stages - 1
+    blend_residual(rec_ref, est_ref, before_ref, after_ref, shift_ref, pair_ref, last, res_ref)
     spread_update(res_ref, shift_ref, dup_ref, est_ref, u_ref)
 
     def remote(half, peer, sender):
@@ -318,15 +344,15 @@
         locals_[half].wait()
 
 
-def filter_and_send(estimate, residual, delays, limits, tables):
+def filter_and_send(estimate, before, after, records, delays, limits, tables):
     forward, inverse, mix_forward, mix_inverse = tables
     receivers, sources, samples = estimate.shape
     count = lax.axis_size("shot")
     halves = 2
     vmem = pl.BlockSpec(memory_space=pltpu.VMEM)
     return pl.pallas_call(
-        functools.partial(filter_send_kernel, count, halves),
-        in_specs=[vmem] * 11,
+        functools.partial(filter_send_kernel, count, lax.axis_size("tm"), halves),
+        in_specs=[vmem] * 14,
         out_specs=pl.BlockSpec(memory_space=pl.ANY),
         out_shape=jax.ShapeDtypeStruct(
             (receivers * count, sources // count, samples), jnp.bfloat16
@@ -334,6 +360,7 @@
         scratch_shapes=[
             pltpu.VMEM(estimate.shape, jnp.bfloat16),
             pltpu.VMEM(estimate.shape, jnp.bfloat16),
+            pltpu.VMEM(records.shape, jnp.bfloat16),
             pltpu.SemaphoreType.DMA((halves, count)),
             pltpu.SemaphoreType.DMA((halves, count)),
             pltpu.SemaphoreType.DMA((halves,)),
@@ -343,7 +370,11 @@
         ),
     )(
         estimate,
-        *spread_inputs(residual, delays),
+        before,
+        after,
+        records,
+        jnp.asarray(np.ascontiguousarray(pairing(records.shape[1]).T)),
+        *spread_inputs(records, delays)[1:],
         forward, inverse, *mix_forward, *mix_inverse, limits.reshape(sources, 1),
     )
 
@@ -458,11 +489,7 @@
     before = jnp.where(row == 0, jnp.zeros_like(before), before)
     last = row == lax.axis_size("tm") - 1
     after = jnp.where(last, jnp.zeros_like(after), after)
-    blended_part = blend(jnp.concatenate([estimate, after], axis=2), before, delays)
-    residual = (extended - blended_part).astype(jnp.bfloat16)
-    keep = jnp.logical_or(jnp.arange(samples + BLK) < samples, jnp.logical_not(last))
-    residual = jnp.where(keep[None, None, :], residual, jnp.zeros_like(residual))
-    return filter_and_send(estimate, residual, delays, thresholds[1], tables)
+    return filter_and_send(estimate, before, after, extended, delays, thresholds[1], tables)
 
 
 def solution(mesh):

time: 74.8 us -> 71.1 us (0.951)
  Pallas kernels: 58.7 us -> 62.2 us
  matrix products: 3.47 us -> 0 us
  other arithmetic: 3.81 us -> 1.13 us
  local copies, waits for them, and re-layouts: 5.19 us -> 2.76 us
  waiting for transfers between devices: 0.01 us -> 1.6 us
    dot_general x3 -> x0, matrix products: 3.47 us -> none  [the longest x1 1.76 us: blend(): jnp.einsum('rsnb,sbi->rsni', upper, select_prior, preferred_element_type=...]
    pallas_call x1, Pallas kernels: 25.1 us -> 28.2 us  [filter_and_send(): pl.pallas_call(functools.partial(filter_send_kernel, count, lax.axis_size...]
    ppermute x1, waiting for transfers between devices: 0.01 us -> 1.6 us  [shifted(): return lax.ppermute(array, axis, pairs)]
    select_n x2 -> x1, other arithmetic: 1.16 us -> 0.02 us  [local(): after = jnp.where(last, jnp.zeros_like(after), after)]
    add x1 -> x0, local copies, waits for them, and re-layouts: 1.03 us -> none  [blend(): return (same + carried).reshape(receivers, experiments, samples)]
    unnamed x28 -> x24, local copies, waits for them, and re-layouts: 2.39 us -> 1.57 us
  transfers between devices with their start and end apart: 1 -> 1, of which waited for: 0 -> 1; matrix products, arithmetic and copies ran while one was open for 3% -> 1% of each run, Pallas kernels for 0% -> 0%
where the time goes in v10:
time: 71.1 us; the launch traced here: 70.8 us
  Pallas kernels  62.2 us (87%)
  starting transfers between devices  2.95 us (4%)
  local copies, waits for them, and re-layouts  2.76 us (4%)
  waiting for transfers between devices  1.6 us (2%)
  other arithmetic  1.13 us (2%)
    pallas_call x1, Pallas kernels, filter_and_send(): pl.pallas_call(functools.partial(filter_send_kernel, count, lax.axis_size...  28.2 us
    pallas_call x1, Pallas kernels, exchange(): pl.pallas_call(functools.partial(exchange_kernel, count, outgoing, incomi...  24.4 us
    pallas_call x1, Pallas kernels, filter_with_halos(): pl.pallas_call(functools.partial(filter_halo_kernel, stages), in_specs=[v...  9.62 us
    ppermute x1, starting transfers between devices, shifted(): return lax.ppermute(array, axis, pairs)  2.95 us
    ppermute x1, waiting for transfers between devices, shifted(): return lax.ppermute(array, axis, pairs)  1.6 us
    unnamed x24, local copies, waits for them, and re-layouts  1.57 us
  transfers between devices with their start and end apart: 1, of which 1 were waited for; matrix products, arithmetic and copies ran while one was open for 1% of the time, Pallas kernels for 0%

profile of v10, /device:TPU:3, one launch (start us, length us, event | category | flops | bytes accessed | tf_op | source)
XLA Modules:
  0.0 70.8 jit_solution(1353560979316986602)
XLA Ops:
  0.0 0.0 copy-start.10
  0.0 0.0 copy-start.9
  0.0 0.0 copy-start.5
  0.0 24.4 %shard_map.127 = f32[4,32,1024]{2,1,0:T(8,128)} custom-call(f32[128,1,1024]{2,1,0:T(1,128)} %src_ref.1), custom_call_target="tpu_custom_call" | custom-call | tf_op jit(solution)/shard_map/pallas_call | solution.py:439
  24.4 0.0 copy-start
  24.4 0.9 %slice.9 = f32[4,32,128]{2,1,0:T(8,128)S(1)} slice(f32[4,32,1024]{2,1,0:T(8,128)} %shard_map.127), slice={[0:4], [0:32], [0:128]} | slice | bytes 131072 | tf_op jit(solution)/shard_map/slice | solution.py:484
  25.3 2.9 %collective-permute-start = (f32[4,32,128]{2,1,0:T(8,128)S(1)}, f32[4,32,128]{2,1,0:T(8,128)S(1)}, u32[]{:S(2)}, u32[]{:S(2)}) collective-permute-start(f32[4,32,128]{2,1,0:T(8,128)S(1)} %slice.9), channel_id=1, source_target_pairs={{1,0},{2,1},{3,2},{4,3},{5,4},{6,5},{7,6},{9,8},{10,9},{11,10},{12... | collective-permute-start | bytes 196616 | tf_op jit(solution)/shard_map/ppermute | solution.py:26
  28.3 0.0 copy-done.10
  28.3 0.0 copy-done.9
  28.3 0.1 copy.19
  28.4 0.1 reshape.5.shift_ref
  28.5 0.1 copy.23.refs_6_
  28.6 0.1 copy.21.refs_6_
  28.6 0.0 copy-start.1
  28.7 0.0 copy-start.2
  28.7 0.0 copy-start.3
  28.7 0.0 copy-start.4
  28.7 0.0 copy-start.6
  28.7 1.6 %collective-permute-done = f32[4,32,128]{2,1,0:T(8,128)S(1)} collective-permute-done((f32[4,32,128]{2,1,0:T(8,128)S(1)}, f32[4,32,128]{2,1,0:T(8,128)S(1)}, u32[]{:S(2)}, u32[]{:S(2)}) %collective-permute-start) | collective-permute-done | bytes 65568 | tf_op jit(solution)/shard_map/ppermute | solution.py:26
  30.3 1.1 %fusion.res_ref = bf16[4,32,1152]{2,1,0:T(8,128)(2,1)S(1)} fusion(f32[4,32,128]{2,1,0:T(8,128)S(1)} %collective-permute-done, f32[4,32,1024]{2,1,0:T(8,128)} %shard_map.127), kind=kLoop, calls=%fused_computation.5 | loop fusion | flops 589824 | bytes 884736 | tf_op jit(solution)/shard_map/convert_element_type | solution.py:487
  31.4 0.0 copy-done.5
  31.4 0.0 copy-done
  31.4 0.0 copy-done.1
  31.4 0.0 copy-done.2
  31.4 0.0 copy-done.3
  31.4 0.0 copy-done.4
  31.4 0.0 copy-done.6
  31.4 0.0 copy-start.8
  31.5 9.6 %shard_map.128 = (bf16[4,64,1024]{2,1,0:T(8,128)(2,1)S(1)}, bf16[4,64,128]{2,1,0:T(8,128)(2,1)S(1)}, bf16[4,64,128]{2,1,0:T(8,128)(2,1)S(1)}) custom-call(bf16[4,32,1152]{2,1,0:T(8,128)(2,1)S(1)} %fusion.res_ref, s32[64,1]{1,0:T(8,128)S(1)} %reshape.5.shift_ref, bf16[64,32]{1,0:T(8,128)(2,1)S(1)} %copy-done.6, bf16[256,512]{1,0:T(8,128)(2,1)S(1)} %copy-done.1, ...), custom_call_target="tpu_custom_call" | custom-call | tf_op jit(solution)/shard_map/pallas_call | solution.py:265
  41.1 0.0 copy-done.8
  41.1 0.0 copy-start.7
  41.2 0.6 copy-done.7
  41.8 28.2 %shard_map.129 = bf16[128,2,1024]{2,1,0:T(2,128)(2,1)S(1)} custom-call(bf16[4,64,1024]{2,1,0:T(8,128)(2,1)S(1)} %get-tuple-element.8.est_ref, bf16[4,64,128]{2,1,0:T(8,128)(2,1)S(1)} %get-tuple-element.14.before_ref, bf16[4,64,128]{2,1,0:T(8,128)(2,1)S(1)} %get-tuple-element.13.after_ref, f32[4,32,1152]{2,1,0:T(8,128)S(1)} %pad_maximum_fusion.rec_ref, ...), custom_call_target="tpu_custom_call" | custom-call | tf_op jit(solution)/shard_map/pallas_call | solution.py:353
  70.0 0.8 %copy.25 = bf16[128,2,1024]{2,1,0:T(2,128)(2,1)} copy(bf16[128,2,1024]{2,1,0:T(2,128)(2,1)S(1)} %shard_map.129) | data formatting | bytes 1048576
  (3 shorter events, 0.1 us)
Async XLA Ops:
  0.0 28.3 %copy-start.10 = (f32[2,64]{1,0:T(2,128)S(1)}, f32[2,64]{1,0:T(2,128)}, u32[]{:S(2)}) copy-start(f32[2,64]{1,0:T(2,128)} %param.15) | copy-start | bytes 1540
  0.0 28.3 %copy-start.9 = (s32[32,2]{0,1:T(2,128)S(1)}, s32[32,2]{0,1:T(2,128)}, u32[]{:S(2)}) copy-start(s32[32,2]{0,1:T(2,128)} %param.14) | copy-start | bytes 772
  0.0 31.4 %copy-start.5 = (bf16[128,128]{1,0:T(8,128)(2,1)S(1)}, bf16[128,128]{1,0:T(8,128)(2,1)}, u32[]{:S(2)}) copy-start(bf16[128,128]{1,0:T(8,128)(2,1)} %constant.31.clone.refs_2_) | copy-start | bytes 98308
  24.4 7.0 %copy-start = (bf16[1536,256]{1,0:T(8,128)(2,1)S(1)}, bf16[1536,256]{1,0:T(8,128)(2,1)}, u32[]{:S(2)}) copy-start(bf16[1536,256]{1,0:T(8,128)(2,1)} %constant.38.refs_1_) | copy-start | bytes 2359300
  25.3 5.0 %collective-permute-start = (f32[4,32,128]{2,1,0:T(8,128)S(1)}, f32[4,32,128]{2,1,0:T(8,128)S(1)}, u32[]{:S(2)}, u32[]{:S(2)}) collective-permute-start(f32[4,32,128]{2,1,0:T(8,128)S(1)} %slice.9), channel_id=1, source_target_pairs={{1,0},{2,1},{3,2},{4,3},{5,4},{6,5},{7,6},{9,8},{10,9},{11,10},{12... | collective-permute-start | bytes 196616 | tf_op jit(solution)/shard_map/ppermute | solution.py:26
  28.6 2.7 %copy-start.1 = (bf16[256,512]{1,0:T(8,128)(2,1)S(1)}, bf16[256,512]{1,0:T(8,128)(2,1)}, u32[]{:S(2)}) copy-start(bf16[256,512]{1,0:T(8,128)(2,1)} %constant.28.clone.refs_0_) | copy-start | bytes 786436
  28.7 2.8 %copy-start.2 = (bf16[128,128]{1,0:T(8,128)(2,1)S(1)}, bf16[128,128]{1,0:T(8,128)(2,1)}, u32[]{:S(2)}) copy-start(bf16[128,128]{1,0:T(8,128)(2,1)} %constant.34.clone.refs_5_) | copy-start | bytes 98308
  28.7 2.8 %copy-start.3 = (bf16[128,128]{1,0:T(8,128)(2,1)S(1)}, bf16[128,128]{1,0:T(8,128)(2,1)}, u32[]{:S(2)}) copy-start(bf16[128,128]{1,0:T(8,128)(2,1)} %constant.33.clone.refs_4_) | copy-start | bytes 98308
  28.7 2.8 %copy-start.4 = (bf16[128,128]{1,0:T(8,128)(2,1)S(1)}, bf16[128,128]{1,0:T(8,128)(2,1)}, u32[]{:S(2)}) copy-start(bf16[128,128]{1,0:T(8,128)(2,1)} %constant.32.clone.refs_3_) | copy-start | bytes 98308
  28.7 2.8 %copy-start.6 = (bf16[64,32]{1,0:T(8,128)(2,1)S(1)}, bf16[64,32]{1,0:T(8,128)(2,1)}, u32[]{:S(2)}) copy-start(bf16[64,32]{1,0:T(8,128)(2,1)} %constant.35.clone.dup_ref) | copy-start | bytes 12292
  31.4 9.7 %copy-start.8 = (f32[4,32,1024]{2,1,0:T(8,128)S(1)}, f32[4,32,1024]{2,1,0:T(8,128)}, u32[]{:S(2)}) copy-start(f32[4,32,1024]{2,1,0:T(8,128)} %shard_map.127) | copy-start | bytes 1572868
  41.1 0.7 copy-start.7

commit v11 on v10

--- a/solution.py
+++ b/solution.py
@@ -167,12 +167,17 @@
         res_ref[r] = jnp.where(drop, jnp.zeros_like(residual), residual)
 
 
-def spread_update(res_ref, shift_ref, dup_ref, est_ref, u_ref):
+def spread_update(res_ref, shift_ref, dup_ref, est_ref, u_ref, last=None):
     receivers, sources, samples = u_ref.shape
-    width = res_ref.shape[2]
+    experiments, width = res_ref.shape[1:]
     shift = shift_ref[...]
     for r in range(receivers):
-        moved = jnp.dot(dup_ref[...], res_ref[r], preferred_element_type=jnp.float32)
+        residual = res_ref[r]
+        if last is not None:
+            lane = lax.broadcasted_iota(jnp.int32, (experiments, width), 1)
+            drop = jnp.logical_and(lane >= samples, last)
+            residual = jnp.where(drop, jnp.zeros_like(residual), residual).astype(jnp.bfloat16)
+        moved = jnp.dot(dup_ref[...], residual, preferred_element_type=jnp.float32)
         for bit in range((BLK - 1).bit_length()):
             amount = 1 << bit
             rolled = pltpu.roll(moved, width - amount, 1)
@@ -215,7 +220,7 @@
     def _():
         pl.semaphore_signal(barrier, 1, device_id=(shot, row + 1), device_id_type=mesh_id)
 
-    spread_update(res_ref, shift_ref, dup_ref, None, u_ref)
+    spread_update(res_ref, shift_ref, dup_ref, None, u_ref, jnp.logical_not(has_next))
     filter_block(u_ref, 0, u_ref.shape[0], tables, out_ref)
     pl.semaphore_wait(barrier, has_prev.astype(jnp.int32) + has_next.astype(jnp.int32))
 
@@ -463,29 +468,130 @@
     )
 
 
+def receive_kernel(count, stages, src_ref, out_ref, halo_ref, send_sem, recv_sem, edge_sem, own_sem):
+    part, own, samples = out_ref.shape[0], src_ref.shape[1], src_ref.shape[2]
+    me = lax.axis_index("shot")
+    row = lax.axis_index("tm")
+    has_prev = row > 0
+    has_next = row < stages - 1
+    mesh_id = pl.DeviceIdType.MESH
+    barrier = pltpu.get_barrier_semaphore()
+
+    def greet(step, carry):
+        peer = lax.rem(me + step, count)
+        pl.semaphore_signal(barrier, 1, device_id=(peer, row), device_id_type=mesh_id)
+        return carry
+
+    lax.fori_loop(1, count, greet, 0)
+
+    @pl.when(has_prev)
+    def _():
+        pl.semaphore_signal(barrier, 1, device_id=(me, row - 1), device_id_type=mesh_id)
+
+    @pl.when(has_next)
+    def _():
+        pl.semaphore_signal(barrier, 1, device_id=(me, row + 1), device_id_type=mesh_id)
+
+    pl.semaphore_wait(
+        barrier, count - 1 + has_prev.astype(jnp.int32) + has_next.astype(jnp.int32)
+    )
+    body = (slice(None), pl.ds(me * own, own), pl.ds(0, samples))
+    tail = (slice(None), pl.ds(me * own, own), pl.ds(samples, BLK))
+
+    def chunk(peer, sender, stage):
+        source = src_ref if stage == 0 else halo_ref
+        target = body if stage == 0 else tail
+        target = (target[0], pl.ds(sender * own, own), target[2])
+        return pltpu.make_async_remote_copy(
+            src_ref=source.at[pl.ds(peer * part, part)],
+            dst_ref=out_ref.at[target],
+            send_sem=send_sem.at[stage, peer],
+            recv_sem=recv_sem.at[stage, sender],
+            device_id=(peer, row),
+            device_id_type=mesh_id,
+        )
+
+    mine = pltpu.make_async_copy(src_ref.at[pl.ds(me * part, part)], out_ref.at[body], own_sem.at[0])
+    mine.start()
+
+    def send_body(step, carry):
+        chunk(lax.rem(me + step, count), me, 0).start()
+        return carry
+
+    lax.fori_loop(1, count, send_body, 0)
+
+    def edge(target_row):
+        return pltpu.make_async_remote_copy(
+            src_ref=src_ref.at[:, :, pl.ds(0, BLK)],
+            dst_ref=halo_ref,
+            send_sem=edge_sem.at[0],
+            recv_sem=edge_sem.at[1],
+            device_id=(me, target_row),
+            device_id_type=mesh_id,
+        )
+
+    pl.when(has_prev)(lambda: edge(row - 1).start())
+
+    @pl.when(has_next)
+    def _():
+        edge(row + 1).wait_recv()
+        theirs = pltpu.make_async_copy(
+            halo_ref.at[pl.ds(me * part, part)], out_ref.at[tail], own_sem.at[1]
+        )
+        theirs.start()
+
+        def send_tail(step, carry):
+            chunk(lax.rem(me + step, count), me, 1).start()
+            return carry
+
+        lax.fori_loop(1, count, send_tail, 0)
+
+        def finish_tail(step, carry):
+            peer = lax.rem(me + step, count)
+            chunk(peer, me, 1).wait_send()
+            chunk(me, peer, 1).wait_recv()
+            return carry
+
+        lax.fori_loop(1, count, finish_tail, 0)
+        theirs.wait()
+
+    pl.when(has_prev)(lambda: edge(row - 1).wait_send())
+
+    def finish_body(step, carry):
+        peer = lax.rem(me + step, count)
+        chunk(peer, me, 0).wait_send()
+        chunk(me, peer, 0).wait_recv()
+        return carry
+
+    lax.fori_loop(1, count, finish_body, 0)
+    mine.wait()
+
+
 def to_receivers(records):
     receivers, own, samples = records.shape
     count = lax.axis_size("shot")
     part = receivers // count
-    return exchange(
-        records,
-        (part, own * count, samples),
-        lambda peer: (pl.ds(peer * part, part), slice(None), slice(None)),
-        lambda sender: (slice(None), pl.ds(sender * own, own), slice(None)),
-        1,
-    )
+    return pl.pallas_call(
+        functools.partial(receive_kernel, count, lax.axis_size("tm")),
+        in_specs=[pl.BlockSpec(memory_space=pl.ANY)],
+        out_specs=pl.BlockSpec(memory_space=pl.ANY),
+        out_shape=jax.ShapeDtypeStruct((part, own * count, samples + BLK), records.dtype),
+        scratch_shapes=[
+            pltpu.VMEM((receivers, own, BLK), records.dtype),
+            pltpu.SemaphoreType.DMA((2, count)),
+            pltpu.SemaphoreType.DMA((2, count)),
+            pltpu.SemaphoreType.DMA((2,)),
+            pltpu.SemaphoreType.DMA((2,)),
+        ],
+        compiler_params=pltpu.CompilerParams(collective_id=1, has_side_effects=True),
+    )(records)
 
 
 def local(blended, delays, thresholds):
     tables = filter_tables()
-    records = to_receivers(blended)
-    samples = records.shape[2]
+    extended = to_receivers(blended)
     row = lax.axis_index("tm")
-    following = shifted(records[:, :, :BLK], "tm", -1)
-    extended = jnp.concatenate([records, following], axis=2)
-    estimate, before, after = filter_with_halos(
-        extended.astype(jnp.bfloat16), delays, thresholds[0], tables
-    )
+    estimate, before, after = filter_with_halos(extended, delays, thresholds[0], tables)
     before = jnp.where(row == 0, jnp.zeros_like(before), before)
     last = row == lax.axis_size("tm") - 1
     after = jnp.where(last, jnp.zeros_like(after), after)

time: 71.1 us -> 69 us (0.970)
  starting transfers between devices: 2.95 us -> 0 us
  Pallas kernels: 62.2 us -> 64.3 us
  waiting for transfers between devices: 1.6 us -> 0 us
  local copies, waits for them, and re-layouts: 2.76 us -> 4.35 us
  other arithmetic: 1.13 us -> 0.02 us
    pallas_call x1, Pallas kernels: 24.4 us -> 27.6 us  [to_receivers(): pl.pallas_call(functools.partial(receive_kernel, count, lax.axis_size('tm...]
    ppermute x1 -> x0, starting transfers between devices: 2.95 us -> none  [shifted(): return lax.ppermute(array, axis, pairs)]
    unnamed x24 -> x20, local copies, waits for them, and re-layouts: 1.57 us -> 3.32 us
    pallas_call x1, Pallas kernels: 28.2 us -> 26.6 us  [filter_and_send(): pl.pallas_call(functools.partial(filter_send_kernel, count, lax.axis_size...]
    ppermute x1 -> x0, waiting for transfers between devices: 1.6 us -> none  [shifted(): return lax.ppermute(array, axis, pairs)]
    convert_element_type x1 -> x0, other arithmetic: 1.07 us -> none  [local(): extended.astype(jnp.bfloat16)]
    slice x1 -> x0, local copies, waits for them, and re-layouts: 0.92 us -> none  [local(): following = shifted(records[:, :, :BLK], 'tm', -1)]
    another operation x2, local copies, waits for them, and re-layouts: 0.1 us -> 0.87 us  [filter_and_send(): limits.reshape(sources, 1)]
  transfers between devices with their start and end apart: 1 -> 0, of which waited for: 1 -> 0; matrix products, arithmetic and copies ran while one was open for 1% -> 0% of each run, Pallas kernels for 0% -> 0%
where the time goes in v11:
time: 69 us; the launch traced here: 68.8 us
  Pallas kernels  64.3 us (93%)
  local copies, waits for them, and re-layouts  4.35 us (6%)
    pallas_call x1, Pallas kernels, to_receivers(): pl.pallas_call(functools.partial(receive_kernel, count, lax.axis_size('tm...  27.6 us
    pallas_call x1, Pallas kernels, filter_and_send(): pl.pallas_call(functools.partial(filter_send_kernel, count, lax.axis_size...  26.6 us
    pallas_call x1, Pallas kernels, filter_with_halos(): pl.pallas_call(functools.partial(filter_halo_kernel, stages), in_specs=[v...  10.2 us
    unnamed x20, local copies, waits for them, and re-layouts  3.32 us

profile of v11, /device:TPU:3, one launch (start us, length us, event | category | flops | bytes accessed | tf_op | source)
XLA Modules:
  0.0 68.8 jit_solution(12809574601233348216)
XLA Ops:
  0.0 0.0 copy-start.1
  0.0 0.8 %slice_bitcast_fusion = (f32[64,1]{0,1:T(1,128)S(1)}, f32[64,1]{0,1:T(1,128)S(1)}) fusion(f32[2,64]{1,0:T(2,128)} %param.15), kind=kLoop, calls=%fused_computation.2 | loop fusion | bytes 1024 | tf_op jit(solution)/shard_map/reshape;squeeze | solution.py:383
  0.8 0.8 %copy.19 = s32[32,2]{1,0:T(8,128)S(1)} copy(s32[32,2]{0,1:T(2,128)} %param.14) | data formatting | bytes 512 | tf_op args[1]
  1.5 0.1 reshape.5.shift_ref
  1.6 0.1 copy.23.refs_6_
  1.7 0.1 copy.21.refs_6_
  1.8 0.0 copy-start.2
  1.8 0.0 copy-start.3
  1.8 0.0 copy-start.4
  1.8 0.0 copy-start.5
  1.8 0.0 copy-start.6
  1.8 0.0 copy-start.7
  1.9 27.6 %shard_map.127.res_ref.rec_ref = f32[4,32,1152]{2,1,0:T(8,128)} custom-call(f32[128,1,1024]{2,1,0:T(1,128)} %src_ref.1), custom_call_target="tpu_custom_call" | custom-call | tf_op jit(solution)/shard_map/pallas_call | solution.py:574
  29.4 0.0 copy-done.1
  29.5 0.0 copy-done.2
  29.5 0.0 copy-done.3
  29.5 0.0 copy-done.4
  29.5 0.0 copy-done.5
  29.5 0.0 copy-done.6
  29.5 0.0 copy-done.7
  29.5 0.0 copy-start
  29.5 1.1 %copy-done = f32[4,32,1152]{2,1,0:T(8,128)S(1)} copy-done((f32[4,32,1152]{2,1,0:T(8,128)S(1)}, f32[4,32,1152]{2,1,0:T(8,128)}, u32[]{:S(2)}) %copy-start) | copy-done | bytes 589848
  30.6 10.2 %shard_map.128 = (bf16[4,64,1024]{2,1,0:T(8,128)(2,1)S(1)}, bf16[4,64,128]{2,1,0:T(8,128)(2,1)S(1)}, bf16[4,64,128]{2,1,0:T(8,128)(2,1)S(1)}) custom-call(f32[4,32,1152]{2,1,0:T(8,128)S(1)} %copy-done, s32[64,1]{1,0:T(8,128)S(1)} %reshape.5.shift_ref, bf16[64,32]{1,0:T(8,128)(2,1)S(1)} %copy-done.7, bf16[256,512]{1,0:T(8,128)(2,1)S(1)} %copy-done.2, ...), custom_call_target="tpu_custom_call" | custom-call | tf_op jit(solution)/shard_map/pallas_call | solution.py:270
  40.7 0.0 copy-start.8
  40.8 0.7 copy-done.8
  41.4 26.6 %shard_map.129 = bf16[128,2,1024]{2,1,0:T(2,128)(2,1)S(1)} custom-call(bf16[4,64,1024]{2,1,0:T(8,128)(2,1)S(1)} %get-tuple-element.8.est_ref, bf16[4,64,128]{2,1,0:T(8,128)(2,1)S(1)} %get-tuple-element.14.before_ref, bf16[4,64,128]{2,1,0:T(8,128)(2,1)S(1)} %get-tuple-element.13.after_ref, f32[4,32,1152]{2,1,0:T(8,128)S(1)} %copy-done, ...), custom_call_target="tpu_custom_call" | custom-call | tf_op jit(solution)/shard_map/pallas_call | solution.py:358
  68.0 0.8 %copy.25 = bf16[128,2,1024]{2,1,0:T(2,128)(2,1)} copy(bf16[128,2,1024]{2,1,0:T(2,128)(2,1)S(1)} %shard_map.129) | data formatting | bytes 1048576
  (1 shorter events, 0.0 us)
Async XLA Ops:
  0.0 29.4 %copy-start.1 = (bf16[1536,256]{1,0:T(8,128)(2,1)S(1)}, bf16[1536,256]{1,0:T(8,128)(2,1)}, u32[]{:S(2)}) copy-start(bf16[1536,256]{1,0:T(8,128)(2,1)} %constant.38.refs_1_) | copy-start | bytes 2359300
  1.8 27.7 %copy-start.2 = (bf16[256,512]{1,0:T(8,128)(2,1)S(1)}, bf16[256,512]{1,0:T(8,128)(2,1)}, u32[]{:S(2)}) copy-start(bf16[256,512]{1,0:T(8,128)(2,1)} %constant.28.clone.refs_0_) | copy-start | bytes 786436
  1.8 27.7 %copy-start.3 = (bf16[128,128]{1,0:T(8,128)(2,1)S(1)}, bf16[128,128]{1,0:T(8,128)(2,1)}, u32[]{:S(2)}) copy-start(bf16[128,128]{1,0:T(8,128)(2,1)} %constant.34.clone.refs_5_) | copy-start | bytes 98308
  1.8 27.7 %copy-start.4 = (bf16[128,128]{1,0:T(8,128)(2,1)S(1)}, bf16[128,128]{1,0:T(8,128)(2,1)}, u32[]{:S(2)}) copy-start(bf16[128,128]{1,0:T(8,128)(2,1)} %constant.33.clone.refs_4_) | copy-start | bytes 98308
  1.8 27.7 %copy-start.5 = (bf16[128,128]{1,0:T(8,128)(2,1)S(1)}, bf16[128,128]{1,0:T(8,128)(2,1)}, u32[]{:S(2)}) copy-start(bf16[128,128]{1,0:T(8,128)(2,1)} %constant.32.clone.refs_3_) | copy-start | bytes 98308
  1.8 27.7 %copy-start.6 = (bf16[128,128]{1,0:T(8,128)(2,1)S(1)}, bf16[128,128]{1,0:T(8,128)(2,1)}, u32[]{:S(2)}) copy-start(bf16[128,128]{1,0:T(8,128)(2,1)} %constant.31.clone.refs_2_) | copy-start | bytes 98308
  1.8 27.7 %copy-start.7 = (bf16[64,32]{1,0:T(8,128)(2,1)S(1)}, bf16[64,32]{1,0:T(8,128)(2,1)}, u32[]{:S(2)}) copy-start(bf16[64,32]{1,0:T(8,128)(2,1)} %constant.35.clone.dup_ref) | copy-start | bytes 12292
  29.5 1.1 %copy-start = (f32[4,32,1152]{2,1,0:T(8,128)S(1)}, f32[4,32,1152]{2,1,0:T(8,128)}, u32[]{:S(2)}) copy-start(f32[4,32,1152]{2,1,0:T(8,128)} %shard_map.127.res_ref.rec_ref) | copy-start | bytes 1769476
  40.7 0.7 %copy-start.8 = (bf16[32,64]{1,0:T(8,128)(2,1)S(1)}, bf16[32,64]{1,0:T(8,128)(2,1)}, u32[]{:S(2)}) copy-start(bf16[32,64]{1,0:T(8,128)(2,1)} %constant.36.clone.pair_ref) | copy-start | bytes 12292

commit v12 on v11

--- a/solution.py
+++ b/solution.py
@@ -148,36 +148,45 @@
         out_ref[r, :, w * WIN : (w + 1) * WIN] = restored[block(g)].astype(out_ref.dtype)
 
 
-def blend_residual(rec_ref, est_ref, before_ref, after_ref, shift_ref, pair_ref, last, res_ref):
+def pairs(rows, cols, transpose):
+    row = lax.broadcasted_iota(jnp.int32, (rows, cols), 0)
+    col = lax.broadcasted_iota(jnp.int32, (rows, cols), 1)
+    hit = (col // SRC_EXP == row) if transpose else (row // SRC_EXP == col)
+    return jnp.where(hit, 1.0, 0.0).astype(jnp.bfloat16)
+
+
+def blend_residual(rec_ref, est_ref, before_ref, after_ref, shift_ref, last, res_ref, rows):
     receivers, experiments, width = rec_ref.shape
+    pair = pairs(experiments, est_ref.shape[1], True)
     shift = shift_ref[...]
     lane = lax.broadcasted_iota(jnp.int32, (experiments, width), 1)
     drop = jnp.logical_and(lane >= width - BLK, last)
-    for r in range(receivers):
+    for r in rows:
         moved = jnp.concatenate([before_ref[r], est_ref[r], after_ref[r]], axis=1).astype(jnp.float32)
         full = moved.shape[1]
         for bit in range((BLK - 1).bit_length()):
             amount = 1 << bit
             moved = jnp.where((shift & amount) != 0, pltpu.roll(moved, amount, 1), moved)
         summed = jnp.dot(
-            pair_ref[...], moved[:, full - width :].astype(jnp.bfloat16),
+            pair, moved[:, full - width :].astype(jnp.bfloat16),
             preferred_element_type=jnp.float32,
         )
         residual = (rec_ref[r] - summed).astype(res_ref.dtype)
         res_ref[r] = jnp.where(drop, jnp.zeros_like(residual), residual)
 
 
-def spread_update(res_ref, shift_ref, dup_ref, est_ref, u_ref, last=None):
+def spread_update(res_ref, shift_ref, est_ref, u_ref, rows, last=None):
     receivers, sources, samples = u_ref.shape
     experiments, width = res_ref.shape[1:]
     shift = shift_ref[...]
-    for r in range(receivers):
+    dup = pairs(sources, experiments, False)
+    for r in rows:
         residual = res_ref[r]
         if last is not None:
             lane = lax.broadcasted_iota(jnp.int32, (experiments, width), 1)
             drop = jnp.logical_and(lane >= samples, last)
             residual = jnp.where(drop, jnp.zeros_like(residual), residual).astype(jnp.bfloat16)
-        moved = jnp.dot(dup_ref[...], residual, preferred_element_type=jnp.float32)
+        moved = jnp.dot(dup, residual, preferred_element_type=jnp.float32)
         for bit in range((BLK - 1).bit_length()):
             amount = 1 << bit
             rolled = pltpu.roll(moved, width - amount, 1)
@@ -188,20 +197,15 @@
         u_ref[r] = value.astype(u_ref.dtype)
 
 
-def pairing(experiments):
-    source = np.arange(experiments * SRC_EXP)[:, None] // SRC_EXP
-    return (source == np.arange(experiments)[None, :]).astype(ml_dtypes.bfloat16)
-
-
 def spread_inputs(residual, delays):
-    return [residual, delays.reshape(-1, 1), jnp.asarray(pairing(residual.shape[1]))]
+    return [residual, delays.reshape(-1, 1)]
 
 
 def filter_kernel(u_ref, *refs):
     filter_block(u_ref, 0, u_ref.shape[0], refs[:7], refs[7])
 
 
-def filter_halo_kernel(stages, res_ref, shift_ref, dup_ref, *refs):
+def filter_halo_kernel(stages, res_ref, shift_ref, *refs):
     tables = refs[:7]
     out_ref, before_ref, after_ref, u_ref, send_sem, recv_sem = refs[7:]
     samples = u_ref.shape[2]
@@ -220,7 +224,7 @@
     def _():
         pl.semaphore_signal(barrier, 1, device_id=(shot, row + 1), device_id_type=mesh_id)
 
-    spread_update(res_ref, shift_ref, dup_ref, None, u_ref, jnp.logical_not(has_next))
+    spread_update(res_ref, shift_ref, None, u_ref, range(u_ref.shape[0]), jnp.logical_not(has_next))
     filter_block(u_ref, 0, u_ref.shape[0], tables, out_ref)
     pl.semaphore_wait(barrier, has_prev.astype(jnp.int32) + has_next.astype(jnp.int32))
 
@@ -269,7 +273,7 @@
     edge = jax.ShapeDtypeStruct((receivers, sources, BLK), jnp.bfloat16)
     return pl.pallas_call(
         functools.partial(filter_halo_kernel, stages),
-        in_specs=[vmem] * 10,
+        in_specs=[vmem] * 9,
         out_specs=(vmem, anywhere, anywhere),
         out_shape=(jax.ShapeDtypeStruct((receivers, sources, samples), jnp.bfloat16), edge, edge),
         scratch_shapes=[
@@ -287,7 +291,7 @@
 
 
 def filter_send_kernel(
-    count, stages, halves, est_ref, before_ref, after_ref, rec_ref, pair_ref, shift_ref, dup_ref, *refs
+    count, stages, halves, est_ref, before_ref, after_ref, rec_ref, shift_ref, *refs
 ):
     tables = refs[:7]
     out_ref, done_ref, u_ref, res_ref, send_sem, recv_sem, own_sem = refs[7:]
@@ -305,8 +309,6 @@
 
     lax.fori_loop(1, count, greet, 0)
     last = lax.axis_index("tm") == stages - 1
-    blend_residual(rec_ref, est_ref, before_ref, after_ref, shift_ref, pair_ref, last, res_ref)
-    spread_update(res_ref, shift_ref, dup_ref, est_ref, u_ref)
 
     def remote(half, peer, sender):
         return pltpu.make_async_remote_copy(
@@ -320,6 +322,9 @@
 
     locals_ = []
     for half in range(halves):
+        rows = range(half * per, (half + 1) * per)
+        blend_residual(rec_ref, est_ref, before_ref, after_ref, shift_ref, last, res_ref, rows)
+        spread_update(res_ref, shift_ref, est_ref, u_ref, rows)
         filter_block(u_ref, half * per, per, tables, done_ref)
         if half == 0:
             pl.semaphore_wait(barrier, count - 1)
@@ -357,7 +362,7 @@
     vmem = pl.BlockSpec(memory_space=pltpu.VMEM)
     return pl.pallas_call(
         functools.partial(filter_send_kernel, count, lax.axis_size("tm"), halves),
-        in_specs=[vmem] * 14,
+        in_specs=[vmem] * 12,
         out_specs=pl.BlockSpec(memory_space=pl.ANY),
         out_shape=jax.ShapeDtypeStruct(
             (receivers * count, sources // count, samples), jnp.bfloat16
@@ -378,7 +383,6 @@
         before,
         after,
         records,
-        jnp.asarray(np.ascontiguousarray(pairing(records.shape[1]).T)),
         *spread_inputs(records, delays)[1:],
         forward, inverse, *mix_forward, *mix_inverse, limits.reshape(sources, 1),
     )

time: 69 us -> 66.1 us (0.958)
  Pallas kernels: 64.3 us -> 62.2 us
    pallas_call x1, Pallas kernels: 26.6 us -> 24.4 us  [filter_and_send(): pl.pallas_call(functools.partial(filter_send_kernel, count, lax.axis_size...]
    unnamed x20 -> x16, local copies, waits for them, and re-layouts: 3.32 us -> 2.64 us
where the time goes in v12:
time: 66.1 us; the launch traced here: 66 us
  Pallas kernels  62.2 us (94%)
  local copies, waits for them, and re-layouts  3.68 us (6%)
    pallas_call x1, Pallas kernels, to_receivers(): pl.pallas_call(functools.partial(receive_kernel, count, lax.axis_size('tm...  27.6 us
    pallas_call x1, Pallas kernels, filter_and_send(): pl.pallas_call(functools.partial(filter_send_kernel, count, lax.axis_size...  24.4 us
    pallas_call x1, Pallas kernels, filter_with_halos(): pl.pallas_call(functools.partial(filter_halo_kernel, stages), in_specs=[v...  10.2 us
    unnamed x16, local copies, waits for them, and re-layouts  2.64 us

profile of v12, /device:TPU:3, one launch (start us, length us, event | category | flops | bytes accessed | tf_op | source)
XLA Modules:
  0.0 66.0 jit_solution(606286951007658985)
XLA Ops:
  0.0 0.0 copy-start.1
  0.0 0.8 %slice_bitcast_fusion = (f32[64,1]{0,1:T(1,128)S(1)}, f32[64,1]{0,1:T(1,128)S(1)}) fusion(f32[2,64]{1,0:T(2,128)} %param.12), kind=kLoop, calls=%fused_computation.2 | loop fusion | bytes 1024 | tf_op jit(solution)/shard_map/reshape;squeeze | solution.py:387
  0.8 0.8 %copy.16 = s32[32,2]{1,0:T(8,128)S(1)} copy(s32[32,2]{0,1:T(2,128)} %param.11) | data formatting | bytes 512 | tf_op args[1]
  1.5 0.1 reshape.5.shift_ref
  1.6 0.1 copy.20.refs_6_
  1.7 0.1 copy.18.refs_6_
  1.8 0.0 copy-start.2
  1.8 0.0 copy-start.3
  1.8 0.0 copy-start.4
  1.8 0.0 copy-start.5
  1.8 0.0 copy-start.6
  1.8 27.6 %shard_map.100.res_ref.rec_ref = f32[4,32,1152]{2,1,0:T(8,128)} custom-call(f32[128,1,1024]{2,1,0:T(1,128)} %src_ref.1), custom_call_target="tpu_custom_call" | custom-call | tf_op jit(solution)/shard_map/pallas_call | solution.py:578
  29.4 0.0 copy-done.1
  29.4 0.0 copy-done.2
  29.5 0.0 copy-done.3
  29.5 0.0 copy-done.4
  29.5 0.0 copy-done.5
  29.5 0.0 copy-done.6
  29.5 0.0 copy-start
  29.5 1.1 %copy-done = f32[4,32,1152]{2,1,0:T(8,128)S(1)} copy-done((f32[4,32,1152]{2,1,0:T(8,128)S(1)}, f32[4,32,1152]{2,1,0:T(8,128)}, u32[]{:S(2)}) %copy-start) | copy-done | bytes 589848
  30.6 10.2 %shard_map.101 = (bf16[4,64,1024]{2,1,0:T(8,128)(2,1)S(1)}, bf16[4,64,128]{2,1,0:T(8,128)(2,1)S(1)}, bf16[4,64,128]{2,1,0:T(8,128)(2,1)S(1)}) custom-call(f32[4,32,1152]{2,1,0:T(8,128)S(1)} %copy-done, s32[64,1]{1,0:T(8,128)S(1)} %reshape.5.shift_ref, bf16[256,512]{1,0:T(8,128)(2,1)S(1)} %copy-done.2, bf16[1536,256]{1,0:T(8,128)(2,1)S(1)} %copy-done.1, ...), custom_call_target="tpu_custom_call" | custom-call | tf_op jit(solution)/shard_map/pallas_call | solution.py:274
  40.7 24.4 %shard_map.102 = bf16[128,2,1024]{2,1,0:T(2,128)(2,1)S(1)} custom-call(bf16[4,64,1024]{2,1,0:T(8,128)(2,1)S(1)} %get-tuple-element.8.est_ref, bf16[4,64,128]{2,1,0:T(8,128)(2,1)S(1)} %get-tuple-element.14.before_ref, bf16[4,64,128]{2,1,0:T(8,128)(2,1)S(1)} %get-tuple-element.13.after_ref, f32[4,32,1152]{2,1,0:T(8,128)S(1)} %copy-done, ...), custom_call_target="tpu_custom_call" | custom-call | tf_op jit(solution)/shard_map/pallas_call | solution.py:363
  65.2 0.8 %copy.22 = bf16[128,2,1024]{2,1,0:T(2,128)(2,1)} copy(bf16[128,2,1024]{2,1,0:T(2,128)(2,1)S(1)} %shard_map.102) | data formatting | bytes 1048576
  (1 shorter events, 0.0 us)
Async XLA Ops:
  0.0 29.4 %copy-start.1 = (bf16[1536,256]{1,0:T(8,128)(2,1)S(1)}, bf16[1536,256]{1,0:T(8,128)(2,1)}, u32[]{:S(2)}) copy-start(bf16[1536,256]{1,0:T(8,128)(2,1)} %constant.32.refs_1_) | copy-start | bytes 2359300
  1.8 27.6 %copy-start.2 = (bf16[256,512]{1,0:T(8,128)(2,1)S(1)}, bf16[256,512]{1,0:T(8,128)(2,1)}, u32[]{:S(2)}) copy-start(bf16[256,512]{1,0:T(8,128)(2,1)} %constant.24.clone.refs_0_) | copy-start | bytes 786436
  1.8 27.7 %copy-start.3 = (bf16[128,128]{1,0:T(8,128)(2,1)S(1)}, bf16[128,128]{1,0:T(8,128)(2,1)}, u32[]{:S(2)}) copy-start(bf16[128,128]{1,0:T(8,128)(2,1)} %constant.30.clone.refs_5_) | copy-start | bytes 98308
  1.8 27.7 %copy-start.4 = (bf16[128,128]{1,0:T(8,128)(2,1)S(1)}, bf16[128,128]{1,0:T(8,128)(2,1)}, u32[]{:S(2)}) copy-start(bf16[128,128]{1,0:T(8,128)(2,1)} %constant.29.clone.refs_4_) | copy-start | bytes 98308
  1.8 27.7 %copy-start.5 = (bf16[128,128]{1,0:T(8,128)(2,1)S(1)}, bf16[128,128]{1,0:T(8,128)(2,1)}, u32[]{:S(2)}) copy-start(bf16[128,128]{1,0:T(8,128)(2,1)} %constant.28.clone.refs_3_) | copy-start | bytes 98308
  1.8 27.7 %copy-start.6 = (bf16[128,128]{1,0:T(8,128)(2,1)S(1)}, bf16[128,128]{1,0:T(8,128)(2,1)}, u32[]{:S(2)}) copy-start(bf16[128,128]{1,0:T(8,128)(2,1)} %constant.27.clone.refs_2_) | copy-start | bytes 98308
  29.5 1.1 %copy-start = (f32[4,32,1152]{2,1,0:T(8,128)S(1)}, f32[4,32,1152]{2,1,0:T(8,128)}, u32[]{:S(2)}) copy-start(f32[4,32,1152]{2,1,0:T(8,128)} %shard_map.100.res_ref.rec_ref) | copy-start | bytes 1769476

commit v13 on v12

--- a/solution.py
+++ b/solution.py
@@ -175,12 +175,14 @@
         res_ref[r] = jnp.where(drop, jnp.zeros_like(residual), residual)
 
 
-def spread_update(res_ref, shift_ref, est_ref, u_ref, rows, last=None):
+def spread_update(res_ref, shift_ref, est_ref, u_ref, rows, last=None, wait=None):
     receivers, sources, samples = u_ref.shape
     experiments, width = res_ref.shape[1:]
     shift = shift_ref[...]
     dup = pairs(sources, experiments, False)
     for r in rows:
+        if wait is not None:
+            wait(r)
         residual = res_ref[r]
         if last is not None:
             lane = lax.broadcasted_iota(jnp.int32, (experiments, width), 1)
@@ -207,8 +209,14 @@
 
 def filter_halo_kernel(stages, res_ref, shift_ref, *refs):
     tables = refs[:7]
-    out_ref, before_ref, after_ref, u_ref, send_sem, recv_sem = refs[7:]
+    out_ref, before_ref, after_ref, u_ref, res_vmem, load_sem, send_sem, recv_sem = refs[7:]
     samples = u_ref.shape[2]
+    loads = [
+        pltpu.make_async_copy(res_ref.at[r], res_vmem.at[r], load_sem.at[r])
+        for r in range(res_ref.shape[0])
+    ]
+    for load in loads:
+        load.start()
     shot = lax.axis_index("shot")
     row = lax.axis_index("tm")
     has_prev = row > 0
@@ -224,7 +232,10 @@
     def _():
         pl.semaphore_signal(barrier, 1, device_id=(shot, row + 1), device_id_type=mesh_id)
 
-    spread_update(res_ref, shift_ref, None, u_ref, range(u_ref.shape[0]), jnp.logical_not(has_next))
+    spread_update(
+        res_vmem, shift_ref, None, u_ref, range(u_ref.shape[0]), jnp.logical_not(has_next),
+        lambda r: loads[r].wait(),
+    )
     filter_block(u_ref, 0, u_ref.shape[0], tables, out_ref)
     pl.semaphore_wait(barrier, has_prev.astype(jnp.int32) + has_next.astype(jnp.int32))
 
@@ -273,11 +284,13 @@
     edge = jax.ShapeDtypeStruct((receivers, sources, BLK), jnp.bfloat16)
     return pl.pallas_call(
         functools.partial(filter_halo_kernel, stages),
-        in_specs=[vmem] * 9,
+        in_specs=[anywhere] + [vmem] * 8,
         out_specs=(vmem, anywhere, anywhere),
         out_shape=(jax.ShapeDtypeStruct((receivers, sources, samples), jnp.bfloat16), edge, edge),
         scratch_shapes=[
             pltpu.VMEM((receivers, sources, samples), jnp.bfloat16),
+            pltpu.VMEM(residual.shape, residual.dtype),
+            pltpu.SemaphoreType.DMA((receivers,)),
             pltpu.SemaphoreType.DMA((2,)),
             pltpu.SemaphoreType.DMA((2,)),
         ],

time: 66.1 us -> 67.6 us (1.023)
  Pallas kernels: 62.2 us -> 63.6 us
    pallas_call x1, Pallas kernels: 10.2 us -> 11.6 us  [filter_with_halos(): pl.pallas_call(functools.partial(filter_halo_kernel, stages), in_specs=[a...]
where the time goes in v13:
time: 67.6 us; the launch traced here: 67.4 us
  Pallas kernels  63.6 us (94%)
  local copies, waits for them, and re-layouts  3.68 us (5%)
    pallas_call x1, Pallas kernels, to_receivers(): pl.pallas_call(functools.partial(receive_kernel, count, lax.axis_size('tm...  27.6 us
    pallas_call x1, Pallas kernels, filter_and_send(): pl.pallas_call(functools.partial(filter_send_kernel, count, lax.axis_size...  24.4 us
    pallas_call x1, Pallas kernels, filter_with_halos(): pl.pallas_call(functools.partial(filter_halo_kernel, stages), in_specs=[a...  11.6 us
    unnamed x16, local copies, waits for them, and re-layouts  2.64 us

profile of v13, /device:TPU:3, one launch (start us, length us, event | category | flops | bytes accessed | tf_op | source)
XLA Modules:
  0.0 67.4 jit_solution(757061060935028625)
XLA Ops:
  0.0 0.0 copy-start.1
  0.0 0.8 %slice_bitcast_fusion = (f32[64,1]{0,1:T(1,128)S(1)}, f32[64,1]{0,1:T(1,128)S(1)}) fusion(f32[2,64]{1,0:T(2,128)} %param.12), kind=kLoop, calls=%fused_computation.2 | loop fusion | bytes 1024 | tf_op jit(solution)/shard_map/reshape;squeeze | solution.py:400
  0.8 0.8 %copy.16 = s32[32,2]{1,0:T(8,128)S(1)} copy(s32[32,2]{0,1:T(2,128)} %param.11) | data formatting | bytes 512 | tf_op args[1]
  1.5 0.1 reshape.5.shift_ref
  1.6 0.1 copy.20.refs_6_
  1.7 0.1 copy.18.refs_6_
  1.8 0.0 copy-start.2
  1.8 0.0 copy-start.3
  1.8 0.0 copy-start.4
  1.8 0.0 copy-start.5
  1.8 0.0 copy-start.6
  1.8 27.6 %shard_map.100.res_ref.rec_ref = f32[4,32,1152]{2,1,0:T(8,128)} custom-call(f32[128,1,1024]{2,1,0:T(1,128)} %src_ref.1), custom_call_target="tpu_custom_call" | custom-call | tf_op jit(solution)/shard_map/pallas_call | solution.py:591
  29.4 0.0 copy-done.1
  29.4 0.0 copy-done.2
  29.5 0.0 copy-done.3
  29.5 0.0 copy-done.4
  29.5 0.0 copy-done.5
  29.5 0.0 copy-done.6
  29.5 0.0 copy-start
  29.5 1.1 %copy-done = f32[4,32,1152]{2,1,0:T(8,128)S(1)} copy-done((f32[4,32,1152]{2,1,0:T(8,128)S(1)}, f32[4,32,1152]{2,1,0:T(8,128)}, u32[]{:S(2)}) %copy-start) | copy-done | bytes 589848
  30.6 11.6 %shard_map.101 = (bf16[4,64,1024]{2,1,0:T(8,128)(2,1)S(1)}, bf16[4,64,128]{2,1,0:T(8,128)(2,1)S(1)}, bf16[4,64,128]{2,1,0:T(8,128)(2,1)S(1)}) custom-call(f32[4,32,1152]{2,1,0:T(8,128)S(1)} %copy-done, s32[64,1]{1,0:T(8,128)S(1)} %reshape.5.shift_ref, bf16[256,512]{1,0:T(8,128)(2,1)S(1)} %copy-done.2, bf16[1536,256]{1,0:T(8,128)(2,1)S(1)} %copy-done.1, ...), custom_call_target="tpu_custom_call" | custom-call | tf_op jit(solution)/shard_map/pallas_call | solution.py:285
  42.2 24.4 %shard_map.102 = bf16[128,2,1024]{2,1,0:T(2,128)(2,1)S(1)} custom-call(bf16[4,64,1024]{2,1,0:T(8,128)(2,1)S(1)} %get-tuple-element.8.est_ref, bf16[4,64,128]{2,1,0:T(8,128)(2,1)S(1)} %get-tuple-element.14.before_ref, bf16[4,64,128]{2,1,0:T(8,128)(2,1)S(1)} %get-tuple-element.13.after_ref, f32[4,32,1152]{2,1,0:T(8,128)S(1)} %copy-done, ...), custom_call_target="tpu_custom_call" | custom-call | tf_op jit(solution)/shard_map/pallas_call | solution.py:376
  66.6 0.8 %copy.22 = bf16[128,2,1024]{2,1,0:T(2,128)(2,1)} copy(bf16[128,2,1024]{2,1,0:T(2,128)(2,1)S(1)} %shard_map.102) | data formatting | bytes 1048576
  (1 shorter events, 0.0 us)
Async XLA Ops:
  0.0 29.4 %copy-start.1 = (bf16[1536,256]{1,0:T(8,128)(2,1)S(1)}, bf16[1536,256]{1,0:T(8,128)(2,1)}, u32[]{:S(2)}) copy-start(bf16[1536,256]{1,0:T(8,128)(2,1)} %constant.32.refs_1_) | copy-start | bytes 2359300
  1.8 27.6 %copy-start.2 = (bf16[256,512]{1,0:T(8,128)(2,1)S(1)}, bf16[256,512]{1,0:T(8,128)(2,1)}, u32[]{:S(2)}) copy-start(bf16[256,512]{1,0:T(8,128)(2,1)} %constant.24.clone.refs_0_) | copy-start | bytes 786436
  1.8 27.7 %copy-start.3 = (bf16[128,128]{1,0:T(8,128)(2,1)S(1)}, bf16[128,128]{1,0:T(8,128)(2,1)}, u32[]{:S(2)}) copy-start(bf16[128,128]{1,0:T(8,128)(2,1)} %constant.30.clone.refs_5_) | copy-start | bytes 98308
  1.8 27.7 %copy-start.4 = (bf16[128,128]{1,0:T(8,128)(2,1)S(1)}, bf16[128,128]{1,0:T(8,128)(2,1)}, u32[]{:S(2)}) copy-start(bf16[128,128]{1,0:T(8,128)(2,1)} %constant.29.clone.refs_4_) | copy-start | bytes 98308
  1.8 27.7 %copy-start.5 = (bf16[128,128]{1,0:T(8,128)(2,1)S(1)}, bf16[128,128]{1,0:T(8,128)(2,1)}, u32[]{:S(2)}) copy-start(bf16[128,128]{1,0:T(8,128)(2,1)} %constant.28.clone.refs_3_) | copy-start | bytes 98308
  1.8 27.7 %copy-start.6 = (bf16[128,128]{1,0:T(8,128)(2,1)S(1)}, bf16[128,128]{1,0:T(8,128)(2,1)}, u32[]{:S(2)}) copy-start(bf16[128,128]{1,0:T(8,128)(2,1)} %constant.27.clone.refs_2_) | copy-start | bytes 98308
  29.5 1.1 %copy-start = (f32[4,32,1152]{2,1,0:T(8,128)S(1)}, f32[4,32,1152]{2,1,0:T(8,128)}, u32[]{:S(2)}) copy-start(f32[4,32,1152]{2,1,0:T(8,128)} %shard_map.100.res_ref.rec_ref) | copy-start | bytes 1769476

commit v14 on v12

--- a/solution.py
+++ b/solution.py
@@ -358,7 +358,7 @@
     forward, inverse, mix_forward, mix_inverse = tables
     receivers, sources, samples = estimate.shape
     count = lax.axis_size("shot")
-    halves = 2
+    halves = 4
     vmem = pl.BlockSpec(memory_space=pltpu.VMEM)
     return pl.pallas_call(
         functools.partial(filter_send_kernel, count, lax.axis_size("tm"), halves),

time: 66.1 us -> 67.9 us (1.027)
  Pallas kernels: 62.2 us -> 63.9 us
    pallas_call x1, Pallas kernels: 24.4 us -> 26.2 us  [filter_and_send(): pl.pallas_call(functools.partial(filter_send_kernel, count, lax.axis_size...]
where the time goes in v14:
time: 67.9 us; the launch traced here: 67.8 us
  Pallas kernels  63.9 us (94%)
  local copies, waits for them, and re-layouts  3.68 us (5%)
    pallas_call x1, Pallas kernels, to_receivers(): pl.pallas_call(functools.partial(receive_kernel, count, lax.axis_size('tm...  27.6 us
    pallas_call x1, Pallas kernels, filter_and_send(): pl.pallas_call(functools.partial(filter_send_kernel, count, lax.axis_size...  26.2 us
    pallas_call x1, Pallas kernels, filter_with_halos(): pl.pallas_call(functools.partial(filter_halo_kernel, stages), in_specs=[v...  10.2 us
    unnamed x16, local copies, waits for them, and re-layouts  2.64 us

profile of v14, /device:TPU:3, one launch (start us, length us, event | category | flops | bytes accessed | tf_op | source)
XLA Modules:
  0.0 67.8 jit_solution(8477179289982850257)
XLA Ops:
  0.0 0.0 copy-start.1
  0.0 0.8 %slice_bitcast_fusion = (f32[64,1]{0,1:T(1,128)S(1)}, f32[64,1]{0,1:T(1,128)S(1)}) fusion(f32[2,64]{1,0:T(2,128)} %param.12), kind=kLoop, calls=%fused_computation.2 | loop fusion | bytes 1024 | tf_op jit(solution)/shard_map/reshape;squeeze | solution.py:387
  0.8 0.8 %copy.16 = s32[32,2]{1,0:T(8,128)S(1)} copy(s32[32,2]{0,1:T(2,128)} %param.11) | data formatting | bytes 512 | tf_op args[1]
  1.5 0.1 reshape.5.shift_ref
  1.6 0.1 copy.20.refs_6_
  1.7 0.1 copy.18.refs_6_
  1.8 0.0 copy-start.2
  1.8 0.0 copy-start.3
  1.8 0.0 copy-start.4
  1.8 0.0 copy-start.5
  1.8 0.0 copy-start.6
  1.8 27.6 %shard_map.100.res_ref.rec_ref = f32[4,32,1152]{2,1,0:T(8,128)} custom-call(f32[128,1,1024]{2,1,0:T(1,128)} %src_ref.1), custom_call_target="tpu_custom_call" | custom-call | tf_op jit(solution)/shard_map/pallas_call | solution.py:578
  29.4 0.0 copy-done.1
  29.4 0.0 copy-done.2
  29.5 0.0 copy-done.3
  29.5 0.0 copy-done.4
  29.5 0.0 copy-done.5
  29.5 0.0 copy-done.6
  29.5 0.0 copy-start
  29.5 1.1 %copy-done = f32[4,32,1152]{2,1,0:T(8,128)S(1)} copy-done((f32[4,32,1152]{2,1,0:T(8,128)S(1)}, f32[4,32,1152]{2,1,0:T(8,128)}, u32[]{:S(2)}) %copy-start) | copy-done | bytes 589848
  30.6 10.2 %shard_map.101 = (bf16[4,64,1024]{2,1,0:T(8,128)(2,1)S(1)}, bf16[4,64,128]{2,1,0:T(8,128)(2,1)S(1)}, bf16[4,64,128]{2,1,0:T(8,128)(2,1)S(1)}) custom-call(f32[4,32,1152]{2,1,0:T(8,128)S(1)} %copy-done, s32[64,1]{1,0:T(8,128)S(1)} %reshape.5.shift_ref, bf16[256,512]{1,0:T(8,128)(2,1)S(1)} %copy-done.2, bf16[1536,256]{1,0:T(8,128)(2,1)S(1)} %copy-done.1, ...), custom_call_target="tpu_custom_call" | custom-call | tf_op jit(solution)/shard_map/pallas_call | solution.py:274
  40.7 26.2 %shard_map.102 = bf16[128,2,1024]{2,1,0:T(2,128)(2,1)S(1)} custom-call(bf16[4,64,1024]{2,1,0:T(8,128)(2,1)S(1)} %get-tuple-element.8.est_ref, bf16[4,64,128]{2,1,0:T(8,128)(2,1)S(1)} %get-tuple-element.14.before_ref, bf16[4,64,128]{2,1,0:T(8,128)(2,1)S(1)} %get-tuple-element.13.after_ref, f32[4,32,1152]{2,1,0:T(8,128)S(1)} %copy-done, ...), custom_call_target="tpu_custom_call" | custom-call | tf_op jit(solution)/shard_map/pallas_call | solution.py:363
  67.0 0.8 %copy.22 = bf16[128,2,1024]{2,1,0:T(2,128)(2,1)} copy(bf16[128,2,1024]{2,1,0:T(2,128)(2,1)S(1)} %shard_map.102) | data formatting | bytes 1048576
  (1 shorter events, 0.0 us)
Async XLA Ops:
  0.0 29.4 %copy-start.1 = (bf16[1536,256]{1,0:T(8,128)(2,1)S(1)}, bf16[1536,256]{1,0:T(8,128)(2,1)}, u32[]{:S(2)}) copy-start(bf16[1536,256]{1,0:T(8,128)(2,1)} %constant.32.refs_1_) | copy-start | bytes 2359300
  1.8 27.6 %copy-start.2 = (bf16[256,512]{1,0:T(8,128)(2,1)S(1)}, bf16[256,512]{1,0:T(8,128)(2,1)}, u32[]{:S(2)}) copy-start(bf16[256,512]{1,0:T(8,128)(2,1)} %constant.24.clone.refs_0_) | copy-start | bytes 786436
  1.8 27.7 %copy-start.3 = (bf16[128,128]{1,0:T(8,128)(2,1)S(1)}, bf16[128,128]{1,0:T(8,128)(2,1)}, u32[]{:S(2)}) copy-start(bf16[128,128]{1,0:T(8,128)(2,1)} %constant.30.clone.refs_5_) | copy-start | bytes 98308
  1.8 27.7 %copy-start.4 = (bf16[128,128]{1,0:T(8,128)(2,1)S(1)}, bf16[128,128]{1,0:T(8,128)(2,1)}, u32[]{:S(2)}) copy-start(bf16[128,128]{1,0:T(8,128)(2,1)} %constant.29.clone.refs_4_) | copy-start | bytes 98308
  1.8 27.7 %copy-start.5 = (bf16[128,128]{1,0:T(8,128)(2,1)S(1)}, bf16[128,128]{1,0:T(8,128)(2,1)}, u32[]{:S(2)}) copy-start(bf16[128,128]{1,0:T(8,128)(2,1)} %constant.28.clone.refs_3_) | copy-start | bytes 98308
  1.8 27.7 %copy-start.6 = (bf16[128,128]{1,0:T(8,128)(2,1)S(1)}, bf16[128,128]{1,0:T(8,128)(2,1)}, u32[]{:S(2)}) copy-start(bf16[128,128]{1,0:T(8,128)(2,1)} %constant.27.clone.refs_2_) | copy-start | bytes 98308
  29.5 1.1 %copy-start = (f32[4,32,1152]{2,1,0:T(8,128)S(1)}, f32[4,32,1152]{2,1,0:T(8,128)}, u32[]{:S(2)}) copy-start(f32[4,32,1152]{2,1,0:T(8,128)} %shard_map.100.res_ref.rec_ref) | copy-start | bytes 1769476

commit v15 on v12

--- a/solution.py
+++ b/solution.py
@@ -515,15 +515,6 @@
             device_id_type=mesh_id,
         )
 
-    mine = pltpu.make_async_copy(src_ref.at[pl.ds(me * part, part)], out_ref.at[body], own_sem.at[0])
-    mine.start()
-
-    def send_body(step, carry):
-        chunk(lax.rem(me + step, count), me, 0).start()
-        return carry
-
-    lax.fori_loop(1, count, send_body, 0)
-
     def edge(target_row):
         return pltpu.make_async_remote_copy(
             src_ref=src_ref.at[:, :, pl.ds(0, BLK)],
@@ -535,6 +526,16 @@
         )
 
     pl.when(has_prev)(lambda: edge(row - 1).start())
+
+    mine = pltpu.make_async_copy(src_ref.at[pl.ds(me * part, part)], out_ref.at[body], own_sem.at[0])
+    mine.start()
+
+    def send_body(step, carry):
+        chunk(lax.rem(me + step, count), me, 0).start()
+        return carry
+
+    lax.fori_loop(1, count, send_body, 0)
+
 
     @pl.when(has_next)
     def _():

time: 66.1 us -> 66.1 us (level)
  no operation moved by 1% of the time
where the time goes in v15:
time: 66.1 us; the launch traced here: 66 us
  Pallas kernels  62.2 us (94%)
  local copies, waits for them, and re-layouts  3.68 us (6%)
    pallas_call x1, Pallas kernels, to_receivers(): pl.pallas_call(functools.partial(receive_kernel, count, lax.axis_size('tm...  27.5 us
    pallas_call x1, Pallas kernels, filter_and_send(): pl.pallas_call(functools.partial(filter_send_kernel, count, lax.axis_size...  24.4 us
    pallas_call x1, Pallas kernels, filter_with_halos(): pl.pallas_call(functools.partial(filter_halo_kernel, stages), in_specs=[v...  10.2 us
    unnamed x16, local copies, waits for them, and re-layouts  2.64 us

profile of v15, /device:TPU:3, one launch (start us, length us, event | category | flops | bytes accessed | tf_op | source)
XLA Modules:
  0.0 66.0 jit_solution(15103198639905792360)
XLA Ops:
  0.0 0.0 copy-start.1
  0.0 0.8 %slice_bitcast_fusion = (f32[64,1]{0,1:T(1,128)S(1)}, f32[64,1]{0,1:T(1,128)S(1)}) fusion(f32[2,64]{1,0:T(2,128)} %param.12), kind=kLoop, calls=%fused_computation.2 | loop fusion | bytes 1024 | tf_op jit(solution)/shard_map/reshape;squeeze | solution.py:387
  0.8 0.8 %copy.16 = s32[32,2]{1,0:T(8,128)S(1)} copy(s32[32,2]{0,1:T(2,128)} %param.11) | data formatting | bytes 512 | tf_op args[1]
  1.5 0.1 reshape.5.shift_ref
  1.6 0.1 copy.20.refs_6_
  1.7 0.1 copy.18.refs_6_
  1.8 0.0 copy-start.2
  1.8 0.0 copy-start.3
  1.8 0.0 copy-start.4
  1.8 0.0 copy-start.5
  1.8 0.0 copy-start.6
  1.8 27.5 %shard_map.100.res_ref.rec_ref = f32[4,32,1152]{2,1,0:T(8,128)} custom-call(f32[128,1,1024]{2,1,0:T(1,128)} %src_ref.1), custom_call_target="tpu_custom_call" | custom-call | tf_op jit(solution)/shard_map/pallas_call | solution.py:579
  29.4 0.0 copy-done.1
  29.4 0.0 copy-done.2
  29.4 0.0 copy-done.3
  29.4 0.0 copy-done.4
  29.4 0.0 copy-done.5
  29.4 0.0 copy-done.6
  29.5 0.0 copy-start
  29.5 1.1 %copy-done = f32[4,32,1152]{2,1,0:T(8,128)S(1)} copy-done((f32[4,32,1152]{2,1,0:T(8,128)S(1)}, f32[4,32,1152]{2,1,0:T(8,128)}, u32[]{:S(2)}) %copy-start) | copy-done | bytes 589848
  30.5 10.2 %shard_map.101 = (bf16[4,64,1024]{2,1,0:T(8,128)(2,1)S(1)}, bf16[4,64,128]{2,1,0:T(8,128)(2,1)S(1)}, bf16[4,64,128]{2,1,0:T(8,128)(2,1)S(1)}) custom-call(f32[4,32,1152]{2,1,0:T(8,128)S(1)} %copy-done, s32[64,1]{1,0:T(8,128)S(1)} %reshape.5.shift_ref, bf16[256,512]{1,0:T(8,128)(2,1)S(1)} %copy-done.2, bf16[1536,256]{1,0:T(8,128)(2,1)S(1)} %copy-done.1, ...), custom_call_target="tpu_custom_call" | custom-call | tf_op jit(solution)/shard_map/pallas_call | solution.py:274
  40.8 24.4 %shard_map.102 = bf16[128,2,1024]{2,1,0:T(2,128)(2,1)S(1)} custom-call(bf16[4,64,1024]{2,1,0:T(8,128)(2,1)S(1)} %get-tuple-element.8.est_ref, bf16[4,64,128]{2,1,0:T(8,128)(2,1)S(1)} %get-tuple-element.14.before_ref, bf16[4,64,128]{2,1,0:T(8,128)(2,1)S(1)} %get-tuple-element.13.after_ref, f32[4,32,1152]{2,1,0:T(8,128)S(1)} %copy-done, ...), custom_call_target="tpu_custom_call" | custom-call | tf_op jit(solution)/shard_map/pallas_call | solution.py:363
  65.2 0.8 %copy.22 = bf16[128,2,1024]{2,1,0:T(2,128)(2,1)} copy(bf16[128,2,1024]{2,1,0:T(2,128)(2,1)S(1)} %shard_map.102) | data formatting | bytes 1048576
  (1 shorter events, 0.0 us)
Async XLA Ops:
  0.0 29.4 %copy-start.1 = (bf16[1536,256]{1,0:T(8,128)(2,1)S(1)}, bf16[1536,256]{1,0:T(8,128)(2,1)}, u32[]{:S(2)}) copy-start(bf16[1536,256]{1,0:T(8,128)(2,1)} %constant.32.refs_1_) | copy-start | bytes 2359300
  1.8 27.6 %copy-start.2 = (bf16[256,512]{1,0:T(8,128)(2,1)S(1)}, bf16[256,512]{1,0:T(8,128)(2,1)}, u32[]{:S(2)}) copy-start(bf16[256,512]{1,0:T(8,128)(2,1)} %constant.24.clone.refs_0_) | copy-start | bytes 786436
  1.8 27.6 %copy-start.3 = (bf16[128,128]{1,0:T(8,128)(2,1)S(1)}, bf16[128,128]{1,0:T(8,128)(2,1)}, u32[]{:S(2)}) copy-start(bf16[128,128]{1,0:T(8,128)(2,1)} %constant.30.clone.refs_5_) | copy-start | bytes 98308
  1.8 27.6 %copy-start.4 = (bf16[128,128]{1,0:T(8,128)(2,1)S(1)}, bf16[128,128]{1,0:T(8,128)(2,1)}, u32[]{:S(2)}) copy-start(bf16[128,128]{1,0:T(8,128)(2,1)} %constant.29.clone.refs_4_) | copy-start | bytes 98308
  1.8 27.6 %copy-start.5 = (bf16[128,128]{1,0:T(8,128)(2,1)S(1)}, bf16[128,128]{1,0:T(8,128)(2,1)}, u32[]{:S(2)}) copy-start(bf16[128,128]{1,0:T(8,128)(2,1)} %constant.28.clone.refs_3_) | copy-start | bytes 98308
  1.8 27.6 %copy-start.6 = (bf16[128,128]{1,0:T(8,128)(2,1)S(1)}, bf16[128,128]{1,0:T(8,128)(2,1)}, u32[]{:S(2)}) copy-start(bf16[128,128]{1,0:T(8,128)(2,1)} %constant.27.clone.refs_2_) | copy-start | bytes 98308
  29.5 1.1 %copy-start = (f32[4,32,1152]{2,1,0:T(8,128)S(1)}, f32[4,32,1152]{2,1,0:T(8,128)}, u32[]{:S(2)}) copy-start(f32[4,32,1152]{2,1,0:T(8,128)} %shard_map.100.res_ref.rec_ref) | copy-start | bytes 1769476

commit v16 on v12

--- a/solution.py
+++ b/solution.py
@@ -104,11 +104,12 @@
     return jnp.dot(joined, stacked, preferred_element_type=jnp.float32)
 
 
-def filter_block(u_ref, first, count, tables, out_ref):
+def filter_block(u_ref, first, count, tables, out_ref, picked=None):
     forward_ref, inverse_ref, mfh_ref, mfl_ref, mih_ref, mil_ref, limit_ref = tables
     sources, samples = u_ref.shape[1:]
     windows = samples // WIN
-    groups = [(r, w) for r in range(first, first + count) for w in range(windows)]
+    picked = range(windows) if picked is None else picked
+    groups = [(r, w) for r in range(first, first + count) for w in picked]
     scale = 1.0 / math.sqrt(WIN)
     rows = jnp.concatenate(
         [u_ref[r, :, w * WIN : (w + 1) * WIN] for r, w in groups], axis=0
@@ -225,7 +226,8 @@
         pl.semaphore_signal(barrier, 1, device_id=(shot, row + 1), device_id_type=mesh_id)
 
     spread_update(res_ref, shift_ref, None, u_ref, range(u_ref.shape[0]), jnp.logical_not(has_next))
-    filter_block(u_ref, 0, u_ref.shape[0], tables, out_ref)
+    windows = samples // WIN
+    filter_block(u_ref, 0, u_ref.shape[0], tables, out_ref, (0, windows - 1))
     pl.semaphore_wait(barrier, has_prev.astype(jnp.int32) + has_next.astype(jnp.int32))
 
     def to_prev():
@@ -250,6 +252,7 @@
 
     pl.when(has_prev)(lambda: to_prev().start())
     pl.when(has_next)(lambda: to_next().start())
+    filter_block(u_ref, 0, u_ref.shape[0], tables, out_ref, tuple(range(1, windows - 1)))
 
     @pl.when(has_prev)
     def _():

time: 66.1 us -> 64.9 us (0.982)
  Pallas kernels: 62.2 us -> 61 us
    pallas_call x1, Pallas kernels: 10.2 us -> 8.97 us  [filter_with_halos(): pl.pallas_call(functools.partial(filter_halo_kernel, stages), in_specs=[v...]
where the time goes in v16:
time: 64.9 us; the launch traced here: 64.8 us
  Pallas kernels  61 us (94%)
  local copies, waits for them, and re-layouts  3.68 us (6%)
    pallas_call x1, Pallas kernels, to_receivers(): pl.pallas_call(functools.partial(receive_kernel, count, lax.axis_size('tm...  27.6 us
    pallas_call x1, Pallas kernels, filter_and_send(): pl.pallas_call(functools.partial(filter_send_kernel, count, lax.axis_size...  24.4 us
    pallas_call x1, Pallas kernels, filter_with_halos(): pl.pallas_call(functools.partial(filter_halo_kernel, stages), in_specs=[v...  8.97 us
    unnamed x16, local copies, waits for them, and re-layouts  2.64 us

profile of v16, /device:TPU:3, one launch (start us, length us, event | category | flops | bytes accessed | tf_op | source)
XLA Modules:
  0.0 64.8 jit_solution(10269496509995227280)
XLA Ops:
  0.0 0.0 copy-start.1
  0.0 0.8 %slice_bitcast_fusion = (f32[64,1]{0,1:T(1,128)S(1)}, f32[64,1]{0,1:T(1,128)S(1)}) fusion(f32[2,64]{1,0:T(2,128)} %param.12), kind=kLoop, calls=%fused_computation.2 | loop fusion | bytes 1024 | tf_op jit(solution)/shard_map/reshape;squeeze | solution.py:390
  0.8 0.8 %copy.16 = s32[32,2]{1,0:T(8,128)S(1)} copy(s32[32,2]{0,1:T(2,128)} %param.11) | data formatting | bytes 512 | tf_op args[1]
  1.5 0.1 reshape.5.shift_ref
  1.6 0.1 copy.20.refs_6_
  1.7 0.1 copy.18.refs_6_
  1.8 0.0 copy-start.2
  1.8 0.0 copy-start.3
  1.8 0.0 copy-start.4
  1.8 0.0 copy-start.5
  1.8 0.0 copy-start.6
  1.8 27.6 %shard_map.100.res_ref.rec_ref = f32[4,32,1152]{2,1,0:T(8,128)} custom-call(f32[128,1,1024]{2,1,0:T(1,128)} %src_ref.1), custom_call_target="tpu_custom_call" | custom-call | tf_op jit(solution)/shard_map/pallas_call | solution.py:581
  29.4 0.0 copy-done.1
  29.4 0.0 copy-done.2
  29.5 0.0 copy-done.3
  29.5 0.0 copy-done.4
  29.5 0.0 copy-done.5
  29.5 0.0 copy-done.6
  29.5 0.0 copy-start
  29.5 1.1 %copy-done = f32[4,32,1152]{2,1,0:T(8,128)S(1)} copy-done((f32[4,32,1152]{2,1,0:T(8,128)S(1)}, f32[4,32,1152]{2,1,0:T(8,128)}, u32[]{:S(2)}) %copy-start) | copy-done | bytes 589848
  30.6 9.0 %shard_map.101 = (bf16[4,64,1024]{2,1,0:T(8,128)(2,1)S(1)}, bf16[4,64,128]{2,1,0:T(8,128)(2,1)S(1)}, bf16[4,64,128]{2,1,0:T(8,128)(2,1)S(1)}) custom-call(f32[4,32,1152]{2,1,0:T(8,128)S(1)} %copy-done, s32[64,1]{1,0:T(8,128)S(1)} %reshape.5.shift_ref, bf16[256,512]{1,0:T(8,128)(2,1)S(1)} %copy-done.2, bf16[1536,256]{1,0:T(8,128)(2,1)S(1)} %copy-done.1, ...), custom_call_target="tpu_custom_call" | custom-call | tf_op jit(solution)/shard_map/pallas_call | solution.py:277
  39.6 24.4 %shard_map.102 = bf16[128,2,1024]{2,1,0:T(2,128)(2,1)S(1)} custom-call(bf16[4,64,1024]{2,1,0:T(8,128)(2,1)S(1)} %get-tuple-element.8.est_ref, bf16[4,64,128]{2,1,0:T(8,128)(2,1)S(1)} %get-tuple-element.14.before_ref, bf16[4,64,128]{2,1,0:T(8,128)(2,1)S(1)} %get-tuple-element.13.after_ref, f32[4,32,1152]{2,1,0:T(8,128)S(1)} %copy-done, ...), custom_call_target="tpu_custom_call" | custom-call | tf_op jit(solution)/shard_map/pallas_call | solution.py:366
  64.0 0.8 %copy.22 = bf16[128,2,1024]{2,1,0:T(2,128)(2,1)} copy(bf16[128,2,1024]{2,1,0:T(2,128)(2,1)S(1)} %shard_map.102) | data formatting | bytes 1048576
  (1 shorter events, 0.0 us)
Async XLA Ops:
  0.0 29.4 %copy-start.1 = (bf16[1536,256]{1,0:T(8,128)(2,1)S(1)}, bf16[1536,256]{1,0:T(8,128)(2,1)}, u32[]{:S(2)}) copy-start(bf16[1536,256]{1,0:T(8,128)(2,1)} %constant.32.refs_1_) | copy-start | bytes 2359300
  1.8 27.6 %copy-start.2 = (bf16[256,512]{1,0:T(8,128)(2,1)S(1)}, bf16[256,512]{1,0:T(8,128)(2,1)}, u32[]{:S(2)}) copy-start(bf16[256,512]{1,0:T(8,128)(2,1)} %constant.24.clone.refs_0_) | copy-start | bytes 786436
  1.8 27.7 %copy-start.3 = (bf16[128,128]{1,0:T(8,128)(2,1)S(1)}, bf16[128,128]{1,0:T(8,128)(2,1)}, u32[]{:S(2)}) copy-start(bf16[128,128]{1,0:T(8,128)(2,1)} %constant.30.clone.refs_5_) | copy-start | bytes 98308
  1.8 27.7 %copy-start.4 = (bf16[128,128]{1,0:T(8,128)(2,1)S(1)}, bf16[128,128]{1,0:T(8,128)(2,1)}, u32[]{:S(2)}) copy-start(bf16[128,128]{1,0:T(8,128)(2,1)} %constant.29.clone.refs_4_) | copy-start | bytes 98308
  1.8 27.7 %copy-start.5 = (bf16[128,128]{1,0:T(8,128)(2,1)S(1)}, bf16[128,128]{1,0:T(8,128)(2,1)}, u32[]{:S(2)}) copy-start(bf16[128,128]{1,0:T(8,128)(2,1)} %constant.28.clone.refs_3_) | copy-start | bytes 98308
  1.8 27.7 %copy-start.6 = (bf16[128,128]{1,0:T(8,128)(2,1)S(1)}, bf16[128,128]{1,0:T(8,128)(2,1)}, u32[]{:S(2)}) copy-start(bf16[128,128]{1,0:T(8,128)(2,1)} %constant.27.clone.refs_2_) | copy-start | bytes 98308
  29.5 1.1 %copy-start = (f32[4,32,1152]{2,1,0:T(8,128)S(1)}, f32[4,32,1152]{2,1,0:T(8,128)}, u32[]{:S(2)}) copy-start(f32[4,32,1152]{2,1,0:T(8,128)} %shard_map.100.res_ref.rec_ref) | copy-start | bytes 1769476

commit v17 on v16

--- a/solution.py
+++ b/solution.py
@@ -475,7 +475,7 @@
     )
 
 
-def receive_kernel(count, stages, src_ref, out_ref, halo_ref, send_sem, recv_sem, edge_sem, own_sem):
+def receive_kernel(count, stages, src_ref, out_ref, send_sem, recv_sem, own_sem):
     part, own, samples = out_ref.shape[0], src_ref.shape[1], src_ref.shape[2]
     me = lax.axis_index("shot")
     row = lax.axis_index("tm")
@@ -491,83 +491,83 @@
 
     lax.fori_loop(1, count, greet, 0)
 
+    def greet_row(target_row):
+        def one(peer, carry):
+            pl.semaphore_signal(barrier, 1, device_id=(peer, target_row), device_id_type=mesh_id)
+            return carry
+
+        lax.fori_loop(0, count, one, 0)
+
+    pl.when(has_prev)(lambda: greet_row(row - 1))
+    pl.when(has_next)(lambda: greet_row(row + 1))
+    pl.semaphore_wait(
+        barrier,
+        count - 1 + count * (has_prev.astype(jnp.int32) + has_next.astype(jnp.int32)),
+    )
+
+    def body(sender):
+        return (slice(None), pl.ds(sender * own, own), pl.ds(0, samples))
+
+    def tail(sender):
+        return (slice(None), pl.ds(sender * own, own), pl.ds(samples, BLK))
+
+    def chunk(peer, sender):
+        return pltpu.make_async_remote_copy(
+            src_ref=src_ref.at[pl.ds(peer * part, part)],
+            dst_ref=out_ref.at[body(sender)],
+            send_sem=send_sem.at[0, peer],
+            recv_sem=recv_sem.at[0, sender],
+            device_id=(peer, row),
+            device_id_type=mesh_id,
+        )
+
+    def edge(peer, sender, target_row):
+        return pltpu.make_async_remote_copy(
+            src_ref=src_ref.at[pl.ds(peer * part, part), :, pl.ds(0, BLK)],
+            dst_ref=out_ref.at[tail(sender)],
+            send_sem=send_sem.at[1, peer],
+            recv_sem=recv_sem.at[1, sender],
+            device_id=(peer, target_row),
+            device_id_type=mesh_id,
+        )
+
     @pl.when(has_prev)
     def _():
-        pl.semaphore_signal(barrier, 1, device_id=(me, row - 1), device_id_type=mesh_id)
+        def send_edge(peer, carry):
+            edge(peer, me, row - 1).start()
+            return carry
+
+        lax.fori_loop(0, count, send_edge, 0)
+
+    mine = pltpu.make_async_copy(src_ref.at[pl.ds(me * part, part)], out_ref.at[body(me)], own_sem)
+    mine.start()
+
+    def send_body(step, carry):
+        chunk(lax.rem(me + step, count), me).start()
+        return carry
+
+    lax.fori_loop(1, count, send_body, 0)
+
+    @pl.when(has_prev)
+    def _():
+        def finish_edge(peer, carry):
+            edge(peer, me, row - 1).wait_send()
+            return carry
+
+        lax.fori_loop(0, count, finish_edge, 0)
 
     @pl.when(has_next)
     def _():
-        pl.semaphore_signal(barrier, 1, device_id=(me, row + 1), device_id_type=mesh_id)
-
-    pl.semaphore_wait(
-        barrier, count - 1 + has_prev.astype(jnp.int32) + has_next.astype(jnp.int32)
-    )
-    body = (slice(None), pl.ds(me * own, own), pl.ds(0, samples))
-    tail = (slice(None), pl.ds(me * own, own), pl.ds(samples, BLK))
-
-    def chunk(peer, sender, stage):
-        source = src_ref if stage == 0 else halo_ref
-        target = body if stage == 0 else tail
-        target = (target[0], pl.ds(sender * own, own), target[2])
-        return pltpu.make_async_remote_copy(
-            src_ref=source.at[pl.ds(peer * part, part)],
-            dst_ref=out_ref.at[target],
-            send_sem=send_sem.at[stage, peer],
-            recv_sem=recv_sem.at[stage, sender],
-            device_id=(peer, row),
-            device_id_type=mesh_id,
-        )
-
-    mine = pltpu.make_async_copy(src_ref.at[pl.ds(me * part, part)], out_ref.at[body], own_sem.at[0])
-    mine.start()
-
-    def send_body(step, carry):
-        chunk(lax.rem(me + step, count), me, 0).start()
-        return carry
-
-    lax.fori_loop(1, count, send_body, 0)
-
-    def edge(target_row):
-        return pltpu.make_async_remote_copy(
-            src_ref=src_ref.at[:, :, pl.ds(0, BLK)],
-            dst_ref=halo_ref,
-            send_sem=edge_sem.at[0],
-            recv_sem=edge_sem.at[1],
-            device_id=(me, target_row),
-            device_id_type=mesh_id,
-        )
-
-    pl.when(has_prev)(lambda: edge(row - 1).start())
-
-    @pl.when(has_next)
-    def _():
-        edge(row + 1).wait_recv()
-        theirs = pltpu.make_async_copy(
-            halo_ref.at[pl.ds(me * part, part)], out_ref.at[tail], own_sem.at[1]
-        )
-        theirs.start()
-
-        def send_tail(step, carry):
-            chunk(lax.rem(me + step, count), me, 1).start()
+        def land_edge(sender, carry):
+            edge(me, sender, row + 1).wait_recv()
             return carry
 
-        lax.fori_loop(1, count, send_tail, 0)
-
-        def finish_tail(step, carry):
-            peer = lax.rem(me + step, count)
-            chunk(peer, me, 1).wait_send()
-            chunk(me, peer, 1).wait_recv()
-            return carry
-
-        lax.fori_loop(1, count, finish_tail, 0)
-        theirs.wait()
-
-    pl.when(has_prev)(lambda: edge(row - 1).wait_send())
+        lax.fori_loop(0, count, land_edge, 0)
 
     def finish_body(step, carry):
         peer = lax.rem(me + step, count)
-        chunk(peer, me, 0).wait_send()
-        chunk(me, peer, 0).wait_recv()
+        chunk(peer, me).wait_send()
+        chunk(me, peer).wait_recv()
         return carry
 
     lax.fori_loop(1, count, finish_body, 0)
@@ -584,11 +584,9 @@
         out_specs=pl.BlockSpec(memory_space=pl.ANY),
         out_shape=jax.ShapeDtypeStruct((part, own * count, samples + BLK), records.dtype),
         scratch_shapes=[
-            pltpu.VMEM((receivers, own, BLK), records.dtype),
             pltpu.SemaphoreType.DMA((2, count)),
             pltpu.SemaphoreType.DMA((2, count)),
-            pltpu.SemaphoreType.DMA((2,)),
-            pltpu.SemaphoreType.DMA((2,)),
+            pltpu.SemaphoreType.DMA,
         ],
         compiler_params=pltpu.CompilerParams(collective_id=1, has_side_effects=True),
     )(records)

time: 64.9 us -> 62.7 us (0.966)
  Pallas kernels: 61 us -> 58.2 us
    pallas_call x1, Pallas kernels: 24.4 us -> 22.2 us  [filter_and_send(): pl.pallas_call(functools.partial(filter_send_kernel, count, lax.axis_size...]
where the time goes in v17:
time: 62.7 us; the launch traced here: 62.1 us
  Pallas kernels  58.2 us (93%)
  local copies, waits for them, and re-layouts  3.68 us (6%)
    pallas_call x1, Pallas kernels, to_receivers(): pl.pallas_call(functools.partial(receive_kernel, count, lax.axis_size('tm...  27.7 us
    pallas_call x1, Pallas kernels, filter_and_send(): pl.pallas_call(functools.partial(filter_send_kernel, count, lax.axis_size...  22.2 us
    pallas_call x1, Pallas kernels, filter_with_halos(): pl.pallas_call(functools.partial(filter_halo_kernel, stages), in_specs=[v...  8.36 us
    unnamed x16, local copies, waits for them, and re-layouts  2.64 us

profile of v17, /device:TPU:3, one launch (start us, length us, event | category | flops | bytes accessed | tf_op | source)
XLA Modules:
  0.0 62.1 jit_solution(7877086280533489723)
XLA Ops:
  0.0 0.0 copy-start.1
  0.0 0.8 %slice_bitcast_fusion = (f32[64,1]{0,1:T(1,128)S(1)}, f32[64,1]{0,1:T(1,128)S(1)}) fusion(f32[2,64]{1,0:T(2,128)} %param.12), kind=kLoop, calls=%fused_computation.2 | loop fusion | bytes 1024 | tf_op jit(solution)/shard_map/reshape;squeeze | solution.py:390
  0.8 0.8 %copy.16 = s32[32,2]{1,0:T(8,128)S(1)} copy(s32[32,2]{0,1:T(2,128)} %param.11) | data formatting | bytes 512 | tf_op args[1]
  1.5 0.1 reshape.5.shift_ref
  1.6 0.1 copy.20.refs_6_
  1.7 0.1 copy.18.refs_6_
  1.8 0.0 copy-start.2
  1.8 0.0 copy-start.3
  1.8 0.0 copy-start.4
  1.8 0.0 copy-start.5
  1.8 0.0 copy-start.6
  1.8 27.7 %shard_map.100.res_ref.rec_ref = f32[4,32,1152]{2,1,0:T(8,128)} custom-call(f32[128,1,1024]{2,1,0:T(1,128)} %src_ref.1), custom_call_target="tpu_custom_call" | custom-call | tf_op jit(solution)/shard_map/pallas_call | solution.py:581
  29.6 0.0 copy-done.1
  29.6 0.0 copy-done.2
  29.6 0.0 copy-done.3
  29.6 0.0 copy-done.4
  29.6 0.0 copy-done.5
  29.6 0.0 copy-done.6
  29.6 0.0 copy-start
  29.6 1.1 %copy-done = f32[4,32,1152]{2,1,0:T(8,128)S(1)} copy-done((f32[4,32,1152]{2,1,0:T(8,128)S(1)}, f32[4,32,1152]{2,1,0:T(8,128)}, u32[]{:S(2)}) %copy-start) | copy-done | bytes 589848
  30.7 8.4 %shard_map.101 = (bf16[4,64,1024]{2,1,0:T(8,128)(2,1)S(1)}, bf16[4,64,128]{2,1,0:T(8,128)(2,1)S(1)}, bf16[4,64,128]{2,1,0:T(8,128)(2,1)S(1)}) custom-call(f32[4,32,1152]{2,1,0:T(8,128)S(1)} %copy-done, s32[64,1]{1,0:T(8,128)S(1)} %reshape.5.shift_ref, bf16[256,512]{1,0:T(8,128)(2,1)S(1)} %copy-done.2, bf16[1536,256]{1,0:T(8,128)(2,1)S(1)} %copy-done.1, ...), custom_call_target="tpu_custom_call" | custom-call | tf_op jit(solution)/shard_map/pallas_call | solution.py:277
  39.1 22.2 %shard_map.102 = bf16[128,2,1024]{2,1,0:T(2,128)(2,1)S(1)} custom-call(bf16[4,64,1024]{2,1,0:T(8,128)(2,1)S(1)} %get-tuple-element.8.est_ref, bf16[4,64,128]{2,1,0:T(8,128)(2,1)S(1)} %get-tuple-element.14.before_ref, bf16[4,64,128]{2,1,0:T(8,128)(2,1)S(1)} %get-tuple-element.13.after_ref, f32[4,32,1152]{2,1,0:T(8,128)S(1)} %copy-done, ...), custom_call_target="tpu_custom_call" | custom-call | tf_op jit(solution)/shard_map/pallas_call | solution.py:366
  61.3 0.8 %copy.22 = bf16[128,2,1024]{2,1,0:T(2,128)(2,1)} copy(bf16[128,2,1024]{2,1,0:T(2,128)(2,1)S(1)} %shard_map.102) | data formatting | bytes 1048576
  (1 shorter events, 0.0 us)
Async XLA Ops:
  0.0 29.6 %copy-start.1 = (bf16[1536,256]{1,0:T(8,128)(2,1)S(1)}, bf16[1536,256]{1,0:T(8,128)(2,1)}, u32[]{:S(2)}) copy-start(bf16[1536,256]{1,0:T(8,128)(2,1)} %constant.32.refs_1_) | copy-start | bytes 2359300
  1.8 27.8 %copy-start.2 = (bf16[256,512]{1,0:T(8,128)(2,1)S(1)}, bf16[256,512]{1,0:T(8,128)(2,1)}, u32[]{:S(2)}) copy-start(bf16[256,512]{1,0:T(8,128)(2,1)} %constant.24.clone.refs_0_) | copy-start | bytes 786436
  1.8 27.8 %copy-start.3 = (bf16[128,128]{1,0:T(8,128)(2,1)S(1)}, bf16[128,128]{1,0:T(8,128)(2,1)}, u32[]{:S(2)}) copy-start(bf16[128,128]{1,0:T(8,128)(2,1)} %constant.30.clone.refs_5_) | copy-start | bytes 98308
  1.8 27.8 %copy-start.4 = (bf16[128,128]{1,0:T(8,128)(2,1)S(1)}, bf16[128,128]{1,0:T(8,128)(2,1)}, u32[]{:S(2)}) copy-start(bf16[128,128]{1,0:T(8,128)(2,1)} %constant.29.clone.refs_4_) | copy-start | bytes 98308
  1.8 27.8 %copy-start.5 = (bf16[128,128]{1,0:T(8,128)(2,1)S(1)}, bf16[128,128]{1,0:T(8,128)(2,1)}, u32[]{:S(2)}) copy-start(bf16[128,128]{1,0:T(8,128)(2,1)} %constant.28.clone.refs_3_) | copy-start | bytes 98308
  1.8 27.8 %copy-start.6 = (bf16[128,128]{1,0:T(8,128)(2,1)S(1)}, bf16[128,128]{1,0:T(8,128)(2,1)}, u32[]{:S(2)}) copy-start(bf16[128,128]{1,0:T(8,128)(2,1)} %constant.27.clone.refs_2_) | copy-start | bytes 98308
  29.6 1.1 %copy-start = (f32[4,32,1152]{2,1,0:T(8,128)S(1)}, f32[4,32,1152]{2,1,0:T(8,128)}, u32[]{:S(2)}) copy-start(f32[4,32,1152]{2,1,0:T(8,128)} %shard_map.100.res_ref.rec_ref) | copy-start | bytes 1769476

commit v18 on v17

--- a/solution.py
+++ b/solution.py
@@ -300,7 +300,7 @@
     out_ref, done_ref, u_ref, res_ref, send_sem, recv_sem, own_sem = refs[7:]
     receivers, sources, samples = u_ref.shape
     own = sources // count
-    per = receivers // halves
+    parts = [(0, 1), (1, receivers - 1)]
     me = lax.axis_index("shot")
     row = lax.axis_index("tm")
     barrier = pltpu.get_barrier_semaphore()
@@ -315,8 +315,8 @@
 
     def remote(half, peer, sender):
         return pltpu.make_async_remote_copy(
-            src_ref=done_ref.at[pl.ds(half * per, per), pl.ds(peer * own, own), :],
-            dst_ref=out_ref.at[pl.ds(sender * receivers + half * per, per), :, :],
+            src_ref=done_ref.at[pl.ds(parts[half][0], parts[half][1]), pl.ds(peer * own, own), :],
+            dst_ref=out_ref.at[pl.ds(sender * receivers + parts[half][0], parts[half][1]), :, :],
             send_sem=send_sem.at[half, peer],
             recv_sem=recv_sem.at[half, sender],
             device_id=(peer, row),
@@ -325,15 +325,16 @@
 
     locals_ = []
     for half in range(halves):
-        rows = range(half * per, (half + 1) * per)
+        first, size = parts[half]
+        rows = range(first, first + size)
         blend_residual(rec_ref, est_ref, before_ref, after_ref, shift_ref, last, res_ref, rows)
         spread_update(res_ref, shift_ref, est_ref, u_ref, rows)
-        filter_block(u_ref, half * per, per, tables, done_ref)
+        filter_block(u_ref, first, size, tables, done_ref)
         if half == 0:
             pl.semaphore_wait(barrier, count - 1)
         mine = pltpu.make_async_copy(
-            done_ref.at[pl.ds(half * per, per), pl.ds(me * own, own), :],
-            out_ref.at[pl.ds(me * receivers + half * per, per), :, :],
+            done_ref.at[pl.ds(first, size), pl.ds(me * own, own), :],
+            out_ref.at[pl.ds(me * receivers + first, size), :, :],
             own_sem.at[half],
         )
         mine.start()

time: 62.7 us -> 65.4 us (1.043)
  Pallas kernels: 58.2 us -> 60.7 us
    pallas_call x1, Pallas kernels: 22.2 us -> 24.6 us  [filter_and_send(): pl.pallas_call(functools.partial(filter_send_kernel, count, lax.axis_size...]
where the time goes in v18:
time: 65.4 us; the launch traced here: 64.5 us
  Pallas kernels  60.7 us (93%)
  local copies, waits for them, and re-layouts  3.68 us (6%)
    pallas_call x1, Pallas kernels, to_receivers(): pl.pallas_call(functools.partial(receive_kernel, count, lax.axis_size('tm...  27.7 us
    pallas_call x1, Pallas kernels, filter_and_send(): pl.pallas_call(functools.partial(filter_send_kernel, count, lax.axis_size...  24.6 us
    pallas_call x1, Pallas kernels, filter_with_halos(): pl.pallas_call(functools.partial(filter_halo_kernel, stages), in_specs=[v...  8.36 us
    unnamed x16, local copies, waits for them, and re-layouts  2.64 us

profile of v18, /device:TPU:3, one launch (start us, length us, event | category | flops | bytes accessed | tf_op | source)
XLA Modules:
  0.0 64.5 jit_solution(2374088671686696045)
XLA Ops:
  0.0 0.0 copy-start.1
  0.0 0.8 %slice_bitcast_fusion = (f32[64,1]{0,1:T(1,128)S(1)}, f32[64,1]{0,1:T(1,128)S(1)}) fusion(f32[2,64]{1,0:T(2,128)} %param.12), kind=kLoop, calls=%fused_computation.2 | loop fusion | bytes 1024 | tf_op jit(solution)/shard_map/reshape;squeeze | solution.py:391
  0.8 0.8 %copy.16 = s32[32,2]{1,0:T(8,128)S(1)} copy(s32[32,2]{0,1:T(2,128)} %param.11) | data formatting | bytes 512 | tf_op args[1]
  1.5 0.1 reshape.5.shift_ref
  1.6 0.1 copy.20.refs_6_
  1.7 0.1 copy.18.refs_6_
  1.8 0.0 copy-start.2
  1.8 0.0 copy-start.3
  1.8 0.0 copy-start.4
  1.8 0.0 copy-start.5
  1.8 0.0 copy-start.6
  1.8 27.7 %shard_map.100.res_ref.rec_ref = f32[4,32,1152]{2,1,0:T(8,128)} custom-call(f32[128,1,1024]{2,1,0:T(1,128)} %src_ref.1), custom_call_target="tpu_custom_call" | custom-call | tf_op jit(solution)/shard_map/pallas_call | solution.py:582
  29.6 0.0 copy-done.1
  29.6 0.0 copy-done.2
  29.6 0.0 copy-done.3
  29.6 0.0 copy-done.4
  29.6 0.0 copy-done.5
  29.6 0.0 copy-done.6
  29.6 0.0 copy-start
  29.6 1.1 %copy-done = f32[4,32,1152]{2,1,0:T(8,128)S(1)} copy-done((f32[4,32,1152]{2,1,0:T(8,128)S(1)}, f32[4,32,1152]{2,1,0:T(8,128)}, u32[]{:S(2)}) %copy-start) | copy-done | bytes 589848
  30.7 8.4 %shard_map.101 = (bf16[4,64,1024]{2,1,0:T(8,128)(2,1)S(1)}, bf16[4,64,128]{2,1,0:T(8,128)(2,1)S(1)}, bf16[4,64,128]{2,1,0:T(8,128)(2,1)S(1)}) custom-call(f32[4,32,1152]{2,1,0:T(8,128)S(1)} %copy-done, s32[64,1]{1,0:T(8,128)S(1)} %reshape.5.shift_ref, bf16[256,512]{1,0:T(8,128)(2,1)S(1)} %copy-done.2, bf16[1536,256]{1,0:T(8,128)(2,1)S(1)} %copy-done.1, ...), custom_call_target="tpu_custom_call" | custom-call | tf_op jit(solution)/shard_map/pallas_call | solution.py:277
  39.1 24.6 %shard_map.102 = bf16[128,2,1024]{2,1,0:T(2,128)(2,1)S(1)} custom-call(bf16[4,64,1024]{2,1,0:T(8,128)(2,1)S(1)} %get-tuple-element.8.est_ref, bf16[4,64,128]{2,1,0:T(8,128)(2,1)S(1)} %get-tuple-element.14.before_ref, bf16[4,64,128]{2,1,0:T(8,128)(2,1)S(1)} %get-tuple-element.13.after_ref, f32[4,32,1152]{2,1,0:T(8,128)S(1)} %copy-done, ...), custom_call_target="tpu_custom_call" | custom-call | tf_op jit(solution)/shard_map/pallas_call | solution.py:367
  63.7 0.8 %copy.22 = bf16[128,2,1024]{2,1,0:T(2,128)(2,1)} copy(bf16[128,2,1024]{2,1,0:T(2,128)(2,1)S(1)} %shard_map.102) | data formatting | bytes 1048576
  (1 shorter events, 0.0 us)
Async XLA Ops:
  0.0 29.6 %copy-start.1 = (bf16[1536,256]{1,0:T(8,128)(2,1)S(1)}, bf16[1536,256]{1,0:T(8,128)(2,1)}, u32[]{:S(2)}) copy-start(bf16[1536,256]{1,0:T(8,128)(2,1)} %constant.32.refs_1_) | copy-start | bytes 2359300
  1.8 27.8 %copy-start.2 = (bf16[256,512]{1,0:T(8,128)(2,1)S(1)}, bf16[256,512]{1,0:T(8,128)(2,1)}, u32[]{:S(2)}) copy-start(bf16[256,512]{1,0:T(8,128)(2,1)} %constant.24.clone.refs_0_) | copy-start | bytes 786436
  1.8 27.8 %copy-start.3 = (bf16[128,128]{1,0:T(8,128)(2,1)S(1)}, bf16[128,128]{1,0:T(8,128)(2,1)}, u32[]{:S(2)}) copy-start(bf16[128,128]{1,0:T(8,128)(2,1)} %constant.30.clone.refs_5_) | copy-start | bytes 98308
  1.8 27.8 %copy-start.4 = (bf16[128,128]{1,0:T(8,128)(2,1)S(1)}, bf16[128,128]{1,0:T(8,128)(2,1)}, u32[]{:S(2)}) copy-start(bf16[128,128]{1,0:T(8,128)(2,1)} %constant.29.clone.refs_4_) | copy-start | bytes 98308
  1.8 27.8 %copy-start.5 = (bf16[128,128]{1,0:T(8,128)(2,1)S(1)}, bf16[128,128]{1,0:T(8,128)(2,1)}, u32[]{:S(2)}) copy-start(bf16[128,128]{1,0:T(8,128)(2,1)} %constant.28.clone.refs_3_) | copy-start | bytes 98308
  1.8 27.8 %copy-start.6 = (bf16[128,128]{1,0:T(8,128)(2,1)S(1)}, bf16[128,128]{1,0:T(8,128)(2,1)}, u32[]{:S(2)}) copy-start(bf16[128,128]{1,0:T(8,128)(2,1)} %constant.27.clone.refs_2_) | copy-start | bytes 98308
  29.6 1.1 %copy-start = (f32[4,32,1152]{2,1,0:T(8,128)S(1)}, f32[4,32,1152]{2,1,0:T(8,128)}, u32[]{:S(2)}) copy-start(f32[4,32,1152]{2,1,0:T(8,128)} %shard_map.100.res_ref.rec_ref) | copy-start | bytes 1769476

commit v19 on v17

--- a/solution.py
+++ b/solution.py
@@ -156,7 +156,7 @@
     return jnp.where(hit, 1.0, 0.0).astype(jnp.bfloat16)
 
 
-def blend_residual(rec_ref, est_ref, before_ref, after_ref, shift_ref, last, res_ref, rows):
+def blend_residual(rec_ref, est_ref, before_ref, after_ref, shift_ref, last, res_ref, rows, wait):
     receivers, experiments, width = rec_ref.shape
     pair = pairs(experiments, est_ref.shape[1], True)
     shift = shift_ref[...]
@@ -172,16 +172,19 @@
             pair, moved[:, full - width :].astype(jnp.bfloat16),
             preferred_element_type=jnp.float32,
         )
+        wait(r)
         residual = (rec_ref[r] - summed).astype(res_ref.dtype)
         res_ref[r] = jnp.where(drop, jnp.zeros_like(residual), residual)
 
 
-def spread_update(res_ref, shift_ref, est_ref, u_ref, rows, last=None):
+def spread_update(res_ref, shift_ref, est_ref, u_ref, rows, last=None, wait=None):
     receivers, sources, samples = u_ref.shape
     experiments, width = res_ref.shape[1:]
     shift = shift_ref[...]
     dup = pairs(sources, experiments, False)
     for r in rows:
+        if wait is not None:
+            wait(r)
         residual = res_ref[r]
         if last is not None:
             lane = lax.broadcasted_iota(jnp.int32, (experiments, width), 1)
@@ -208,8 +211,14 @@
 
 def filter_halo_kernel(stages, res_ref, shift_ref, *refs):
     tables = refs[:7]
-    out_ref, before_ref, after_ref, u_ref, send_sem, recv_sem = refs[7:]
+    out_ref, before_ref, after_ref, u_ref, res_vmem, load_sem, send_sem, recv_sem = refs[7:]
     samples = u_ref.shape[2]
+    loads = [
+        pltpu.make_async_copy(res_ref.at[r], res_vmem.at[r], load_sem.at[r])
+        for r in range(res_ref.shape[0])
+    ]
+    for load in loads:
+        load.start()
     shot = lax.axis_index("shot")
     row = lax.axis_index("tm")
     has_prev = row > 0
@@ -225,7 +234,10 @@
     def _():
         pl.semaphore_signal(barrier, 1, device_id=(shot, row + 1), device_id_type=mesh_id)
 
-    spread_update(res_ref, shift_ref, None, u_ref, range(u_ref.shape[0]), jnp.logical_not(has_next))
+    spread_update(
+        res_vmem, shift_ref, None, u_ref, range(u_ref.shape[0]), jnp.logical_not(has_next),
+        lambda r: loads[r].wait(),
+    )
     windows = samples // WIN
     filter_block(u_ref, 0, u_ref.shape[0], tables, out_ref, (0, windows - 1))
     pl.semaphore_wait(barrier, has_prev.astype(jnp.int32) + has_next.astype(jnp.int32))
@@ -276,16 +288,18 @@
     edge = jax.ShapeDtypeStruct((receivers, sources, BLK), jnp.bfloat16)
     return pl.pallas_call(
         functools.partial(filter_halo_kernel, stages),
-        in_specs=[vmem] * 9,
+        in_specs=[anywhere] + [vmem] * 8,
         out_specs=(vmem, anywhere, anywhere),
         out_shape=(jax.ShapeDtypeStruct((receivers, sources, samples), jnp.bfloat16), edge, edge),
         scratch_shapes=[
             pltpu.VMEM((receivers, sources, samples), jnp.bfloat16),
+            pltpu.VMEM(residual.shape, residual.dtype),
+            pltpu.SemaphoreType.DMA((receivers,)),
             pltpu.SemaphoreType.DMA((2,)),
             pltpu.SemaphoreType.DMA((2,)),
         ],
         compiler_params=pltpu.CompilerParams(
-            collective_id=3, has_side_effects=True, vmem_limit_bytes=48 * 1024 * 1024
+            collective_id=3, has_side_effects=True
         ),
     )(
         *spread_inputs(residual, delays),
@@ -297,7 +311,13 @@
     count, stages, halves, est_ref, before_ref, after_ref, rec_ref, shift_ref, *refs
 ):
     tables = refs[:7]
-    out_ref, done_ref, u_ref, res_ref, send_sem, recv_sem, own_sem = refs[7:]
+    out_ref, done_ref, u_ref, res_ref, rec_vmem, load_sem, send_sem, recv_sem, own_sem = refs[7:]
+    loads = [
+        pltpu.make_async_copy(rec_ref.at[r], rec_vmem.at[r], load_sem.at[r])
+        for r in range(rec_ref.shape[0])
+    ]
+    for load in loads:
+        load.start()
     receivers, sources, samples = u_ref.shape
     own = sources // count
     per = receivers // halves
@@ -326,7 +346,10 @@
     locals_ = []
     for half in range(halves):
         rows = range(half * per, (half + 1) * per)
-        blend_residual(rec_ref, est_ref, before_ref, after_ref, shift_ref, last, res_ref, rows)
+        blend_residual(
+            rec_vmem, est_ref, before_ref, after_ref, shift_ref, last, res_ref, rows,
+            lambda r: loads[r].wait(),
+        )
         spread_update(res_ref, shift_ref, est_ref, u_ref, rows)
         filter_block(u_ref, half * per, per, tables, done_ref)
         if half == 0:
@@ -365,7 +388,7 @@
     vmem = pl.BlockSpec(memory_space=pltpu.VMEM)
     return pl.pallas_call(
         functools.partial(filter_send_kernel, count, lax.axis_size("tm"), halves),
-        in_specs=[vmem] * 12,
+        in_specs=[vmem] * 3 + [pl.BlockSpec(memory_space=pl.ANY)] + [vmem] * 8,
         out_specs=pl.BlockSpec(memory_space=pl.ANY),
         out_shape=jax.ShapeDtypeStruct(
             (receivers * count, sources // count, samples), jnp.bfloat16
@@ -374,12 +397,14 @@
             pltpu.VMEM(estimate.shape, jnp.bfloat16),
             pltpu.VMEM(estimate.shape, jnp.bfloat16),
             pltpu.VMEM(records.shape, jnp.bfloat16),
+            pltpu.VMEM(records.shape, records.dtype),
+            pltpu.SemaphoreType.DMA((records.shape[0],)),
             pltpu.SemaphoreType.DMA((halves, count)),
             pltpu.SemaphoreType.DMA((halves, count)),
             pltpu.SemaphoreType.DMA((halves,)),
         ],
         compiler_params=pltpu.CompilerParams(
-            collective_id=2, has_side_effects=True, vmem_limit_bytes=48 * 1024 * 1024
+            collective_id=2, has_side_effects=True
         ),
     )(
         estimate,

time: 62.7 us -> 72.5 us (1.16)
  Pallas kernels: 58.2 us -> 64.9 us
  local copies, waits for them, and re-layouts: 3.68 us -> 5.75 us
  other arithmetic: 0.02 us -> 1.53 us
    pallas_call x1, Pallas kernels: 8.36 us -> 12.4 us  [filter_with_halos(): pl.pallas_call(functools.partial(filter_halo_kernel, stages), in_specs=[a...]
    pallas_call x1, Pallas kernels: 22.2 us -> 25.2 us  [filter_and_send(): pl.pallas_call(functools.partial(filter_send_kernel, count, lax.axis_size...]
    select_n x1, other arithmetic: 0.02 us -> 1.53 us  [local(): after = jnp.where(last, jnp.zeros_like(after), after)]
    unnamed x16 -> x6, local copies, waits for them, and re-layouts: 2.64 us -> 3.64 us
where the time goes in v19:
time: 72.5 us; the launch traced here: 72.2 us
  Pallas kernels  64.9 us (90%)
  local copies, waits for them, and re-layouts  5.75 us (8%)
  other arithmetic  1.53 us (2%)
    pallas_call x1, Pallas kernels, to_receivers(): pl.pallas_call(functools.partial(receive_kernel, count, lax.axis_size('tm...  27.3 us
    pallas_call x1, Pallas kernels, filter_and_send(): pl.pallas_call(functools.partial(filter_send_kernel, count, lax.axis_size...  25.2 us
    pallas_call x1, Pallas kernels, filter_with_halos(): pl.pallas_call(functools.partial(filter_halo_kernel, stages), in_specs=[a...  12.4 us
    unnamed x6, local copies, waits for them, and re-layouts  3.64 us
    select_n x1, other arithmetic, local(): after = jnp.where(last, jnp.zeros_like(after), after)  1.53 us

profile of v19, /device:TPU:3, one launch (start us, length us, event | category | flops | bytes accessed | tf_op | source)
XLA Modules:
  0.0 72.2 jit_solution(18406527831463077014)
XLA Ops:
  0.0 0.0 copy-start.1
  0.0 0.7 copy-done.1
  0.7 0.0 copy-start
  0.7 0.7 copy-done
  1.4 0.1 copy.16
  1.5 0.7 reshape.5.shift_ref
  2.1 0.7 copy.20.refs_6_
  2.8 0.7 copy.18.refs_6_
  3.6 27.3 %shard_map.100.res_ref.rec_ref = f32[4,32,1152]{2,1,0:T(8,128)} custom-call(f32[128,1,1024]{2,1,0:T(1,128)} %src_ref.1), custom_call_target="tpu_custom_call" | custom-call | tf_op jit(solution)/shard_map/pallas_call | solution.py:606
  30.9 12.4 %shard_map.101 = (bf16[4,64,1024]{2,1,0:T(8,128)(2,1)}, bf16[4,64,128]{2,1,0:T(8,128)(2,1)}, bf16[4,64,128]{2,1,0:T(8,128)(2,1)}) custom-call(f32[4,32,1152]{2,1,0:T(8,128)} %shard_map.100.res_ref.rec_ref, s32[64,1]{1,0:T(8,128)} %reshape.5.shift_ref, bf16[256,512]{1,0:T(8,128)(2,1)} %constant.24.clone.refs_0_, bf16[1536,256]{1,0:T(8,128)(2,1)} %constant.32.refs_1_, ...), custom_call_target="tpu_custom_call" | custom-call | tf_op jit(solution)/shard_map/pallas_call | solution.py:289
  43.3 1.5 %broadcast_select_fusion = (bf16[4,64,128]{2,1,0:T(8,128)(2,1)}, bf16[4,64,128]{2,1,0:T(8,128)(2,1)}) fusion(bf16[4,64,128]{2,1,0:T(8,128)(2,1)} %get-tuple-element.10, pred[]{:T(512)S(6)} %eq.7, bf16[4,64,128]{2,1,0:T(8,128)(2,1)} %get-tuple-element.9, pred[]{:T(512)S(6)} %eq.6), kind=kLoop, calls=%fused_computation | loop fusion | flops 65536 | bytes 262146 | tf_op jit(solution)/shard_map/jit(_where)/select_n | solution.py:627
  44.8 25.2 %shard_map.102 = bf16[128,2,1024]{2,1,0:T(2,128)(2,1)} custom-call(bf16[4,64,1024]{2,1,0:T(8,128)(2,1)} %get-tuple-element.8.est_ref, bf16[4,64,128]{2,1,0:T(8,128)(2,1)} %get-tuple-element.14.before_ref, bf16[4,64,128]{2,1,0:T(8,128)(2,1)} %get-tuple-element.13.after_ref, f32[4,32,1152]{2,1,0:T(8,128)} %shard_map.100.res_ref.rec_ref, ...), custom_call_target="tpu_custom_call" | custom-call | tf_op jit(solution)/shard_map/pallas_call | solution.py:389
  70.0 2.2 %copy.22 = bf16[128,2,1024]{2,1,0:T(2,128)(2,1)} copy(bf16[128,2,1024]{2,1,0:T(2,128)(2,1)} %shard_map.102) | data formatting | bytes 1048576
  (1 shorter events, 0.0 us)
Async XLA Ops:
  0.0 0.7 copy-start.1
  0.7 0.7 copy-start
